TPU v7x, 256 devices: a whole 4x4x8 slice. The times are simulated.
256 devices in a mesh: tile: 64 (over x, y, z_hi), view: 4 (over z_lo, core).
Axes of the slice: x: 4, y: 4, z: 8 (z_hi: 4, z_lo: 2; z = z_hi * 2 + z_lo), core: 2. Of those that a mesh axis runs over, the one named last changes fastest.
Arguments:
- initial: float32 [64, 4, 256, 256], P('tile'), may hold values from 0.5 to 2
- recorded: float32 [4, 64, 4, 256, 256], P('view', 'tile'), may hold values from 0.2 to 3
- tap_table: float32 [4, 8, 3, 31], P('view'), may hold values from 0.02 to 1
- variants: int32 [4, 64], P('view'), may hold values from 0 to 7
Outputs:
- estimate: float32 [64, 4, 256, 256], P('tile')
Inputs may be any that keep to these rules, and one draw needn't show every extreme that they name: `variants`: indices of the 8 tap tables of the view.
All inputs are finite; a program needn't handle non-finite values.
Results may differ from a plain program's by a relative error of at most 0.0001.
Values sent between devices are 32-bit elements; how exact they have to be, the bound alone decides.
No kernel may reach another device: no remote copies, remote signals or barrier semaphores. Data moves between devices by JAX's collectives and lax.ppermute only.
A program may use at most 192 MiB of HBM per device.

v0:
```python
import jax
import jax.numpy as jnp
from jax import lax
from jax.sharding import PartitionSpec as P

GX = 8
ITERS = 2
HALF = 15


def passed_along(block, axis, distance):
    devices = range(lax.axis_size(axis))
    route = [(i - distance, i) for i in devices if i - distance in devices]
    return lax.ppermute(block, axis, route)


def normalized(tap_table):
    return tap_table / jnp.sum(tap_table, axis=-1, keepdims=True)


def tile_kernels(kernels, variant_ids, grid_rows, grid_cols):
    count_variants = kernels.shape[0]
    onehot = (variant_ids[:, None] == jnp.arange(count_variants, dtype=jnp.int32)[None, :]).astype(
        jnp.float32
    )
    flat = jnp.dot(onehot, kernels.reshape(count_variants, -1), precision=lax.Precision.HIGHEST)
    return flat.reshape(grid_rows, grid_cols, 3, kernels.shape[-1])


def tile_onehot(positions, extent, count):
    owner = jnp.clip(jnp.floor_divide(positions, extent), 0, count - 1)
    return (owner[:, None] == jnp.arange(count, dtype=jnp.int32)[None, :]).astype(jnp.float32)


def weight_map(tile_taps, axis_id, offset, row_hot, col_hot):
    inner = jnp.dot(row_hot, tile_taps[:, :, axis_id, offset], precision=lax.Precision.HIGHEST)
    return jnp.dot(inner, col_hot.T, precision=lax.Precision.HIGHEST)


def blur_cols(padded, tile_taps, row_hot, col_hot):
    count = col_hot.shape[0]
    result = jnp.zeros((padded.shape[0], padded.shape[1], count), jnp.float32)
    for offset in range(tile_taps.shape[3]):
        weights = weight_map(tile_taps, 0, offset, row_hot, col_hot)
        result = result + weights[None] * padded[:, :, offset : offset + count]
    return result


def blur_rows(padded, tile_taps, row_hot, col_hot):
    count = row_hot.shape[0]
    result = jnp.zeros((padded.shape[0], count, padded.shape[2]), jnp.float32)
    for offset in range(tile_taps.shape[3]):
        weights = weight_map(tile_taps, 1, offset, row_hot, col_hot)
        result = result + weights[None] * padded[:, offset : offset + count, :]
    return result


def blur_planes(field, tile_taps, row_hot, col_hot, reverse):
    taps = tile_taps.shape[3]
    margin = taps // 2
    padded = jnp.pad(field, ((margin, margin), (0, 0), (0, 0)))
    planes = field.shape[0]
    result = jnp.zeros(field.shape, jnp.float32)
    for offset in range(taps):
        which = taps - 1 - offset if reverse else offset
        weights = weight_map(tile_taps, 2, which, row_hot, col_hot)
        result = result + weights[None] * padded[offset : offset + planes]
    return result


def adjoint_rows(padded, tile_taps, row_hot, col_hot):
    margin = tile_taps.shape[3] // 2
    count = padded.shape[1] - 2 * margin
    result = jnp.zeros((padded.shape[0], count, padded.shape[2]), jnp.float32)
    for offset in range(tile_taps.shape[3]):
        lead = 2 * margin - offset
        weights = weight_map(tile_taps, 1, offset, row_hot, col_hot)
        result = result + weights[None, lead : lead + count, :] * padded[:, lead : lead + count, :]
    return result


def adjoint_cols(padded, tile_taps, row_hot, col_hot):
    margin = tile_taps.shape[3] // 2
    count = padded.shape[2] - 2 * margin
    result = jnp.zeros((padded.shape[0], padded.shape[1], count), jnp.float32)
    for offset in range(tile_taps.shape[3]):
        lead = 2 * margin - offset
        weights = weight_map(tile_taps, 0, offset, row_hot, col_hot)
        result = result + weights[None, :, lead : lead + count] * padded[:, :, lead : lead + count]
    return result


def widen_cols(field, width, tile_col):
    west_send = field[:, :, -width:]
    east_send = field[:, :, :width]
    west_send = jnp.where(tile_col < GX - 1, west_send, jnp.zeros_like(west_send))
    east_send = jnp.where(tile_col > 0, east_send, jnp.zeros_like(east_send))
    from_west = passed_along(west_send, "tile", 1)
    from_east = passed_along(east_send, "tile", -1)
    return jnp.concatenate([from_west, field, from_east], axis=2)


def widen_rows(field, width):
    from_north = passed_along(field[:, -width:, :], "tile", GX)
    from_south = passed_along(field[:, :width, :], "tile", -GX)
    return jnp.concatenate([from_north, field, from_south], axis=1)


def per_device(initial, recorded, tap_table, variants):
    position = lax.axis_index("tile")
    count_tiles = lax.axis_size("tile")
    count_views = lax.axis_size("view")
    grid_rows = count_tiles // GX
    tile_row = position // GX
    tile_col = position % GX
    tile_taps = tile_kernels(normalized(tap_table[0]), variants[0], grid_rows, GX)
    estimate = initial[0]
    observed = recorded[0, 0]
    tall = estimate.shape[1]
    broad = estimate.shape[2]
    row_first = tile_row * tall
    col_first = tile_col * broad

    def row_places(margin):
        return row_first + jnp.arange(tall + 2 * margin, dtype=jnp.int32) - margin

    def col_places(margin):
        return col_first + jnp.arange(broad + 2 * margin, dtype=jnp.int32) - margin

    own_rows = tile_onehot(row_places(0), tall, grid_rows)
    own_cols = tile_onehot(col_places(0), broad, GX)
    wide_rows = tile_onehot(row_places(HALF), tall, grid_rows)
    wide_cols = tile_onehot(col_places(HALF), broad, GX)
    for step in range(ITERS):
        padded = widen_cols(estimate, HALF, tile_col)
        planes = blur_planes(
            blur_cols(padded, tile_taps, own_rows, own_cols), tile_taps, own_rows, own_cols, False
        )
        blurred = blur_rows(widen_rows(planes, HALF), tile_taps, own_rows, own_cols)
        ratio = observed / blurred
        back = adjoint_rows(widen_rows(ratio, HALF), tile_taps, wide_rows, own_cols)
        back = blur_planes(back, tile_taps, own_rows, own_cols, True)
        correction = adjoint_cols(widen_cols(back, HALF, tile_col), tile_taps, own_rows, wide_cols)
        logged = jnp.log(correction)
        summed = lax.psum(logged, "view")
        estimate = estimate * jnp.exp(summed / count_views)
    return estimate[None]


def solution(mesh):
    return jax.shard_map(
        per_device,
        mesh=mesh,
        in_specs=(
            P("tile", None, None, None),
            P("view", "tile", None, None, None),
            P("view", None, None, None),
            P("view", None),
        ),
        out_specs=P("tile", None, None, None),
        check_vma=False,
    )
```

profile of v0, /device:TPU:13, one launch (start us, length us, event | category | flops | bytes accessed | tf_op | source)
XLA Modules:
  0.0 537.8 jit_solution(16397771936226846814)
XLA Ops:
  6.5 2.4 slice_select_fusion.7
  8.9 4.9 collective-permute-start
  13.8 4.8 collective-permute-start.1
  48.4 1.1 fusion.999
  59.3 1.1 fusion.991
  61.7 1.1 fusion.989
  64.1 1.1 fusion.987
  66.5 1.1 fusion.985
  68.8 1.1 fusion.983
  71.2 1.1 fusion.981
  73.6 1.1 fusion.979
  76.0 1.1 fusion.977
  78.4 1.1 fusion.975
  80.8 1.1 fusion.973
  83.2 1.1 fusion.971
  85.5 1.1 fusion.969
  87.9 1.1 fusion.967
  90.3 1.1 fusion.965
  91.4 1.1 fusion.831
  92.7 1.1 fusion.963
  95.0 1.1 fusion.961
  97.4 1.1 fusion.959
  99.8 1.1 fusion.957
  133.9 1.5 fusion.783
  146.0 1.1 fusion.819
  154.6 1.1 fusion.804
  172.7 1.1 fusion.766
  176.0 1.1 fusion.794
  177.0 1.1 fusion.764
  185.5 1.2 fusion.760
  189.8 17.9 %fusion.263 = f32[4,256,256]{2,1,0:T(8,128)S(1)} fusion(f32[4,256,256]{2,1,0:T(8,128)S(1)} %bitcast.300, f32[4,256,15]{2,1,0:T(8,128)} %collective-permute-done.1, f32[4,256,15]{2,1,0:T(8,128)} %collective-permute-done, f32[256,256]{1,0:T(8,128)} %fusion.825, f32[256,256]{1,0:T(8,128)} %fusion.826, f32[256,256]{1,0:T(8,128)} %fusion.827, ...), kind=kLoop, calls=%fused_computation.647 | loop fusion | flops 23855104 | bytes 10346496 | tf_op jit(solution)/shard_map/add | solution.py:45
  208.7 4.2 collective-permute-start.2
  213.0 3.5 collective-permute-start.3
  216.6 2.9 collective-permute-done.3
  219.5 8.2 %fusion.609 = f32[4,256,256]{2,1,0:T(8,128)S(1)} fusion(f32[4,15,256]{2,1,0:T(8,128)S(1)} %collective-permute-done.3, f32[4,15,256]{2,1,0:T(8,128)S(1)} %collective-permute-done.2, f32[4,256,256]{2,1,0:T(8,128)S(1)} %add_add_fusion.3, f32[1,1,4,256,256]{4,3,2,1,0:T(8,128)S(1)} %copy-done.49, f32[256,256]{1,0:T(8,128)} %fusion.790, f32[256,256]{1,0:T(8,128)} %fusion.791, ...), kind=kLoop, calls=%fused_computation.993 | loop fusion | flops 24117248 | bytes 11395072 | tf_op jit(solution)/shard_map/div | solution.py:140
  227.7 4.4 collective-permute-start.4
  232.0 2.4 collective-permute-start.5
  234.9 4.6 collective-permute-done.5
  239.5 8.5 %fusion.522 = f32[4,256,256]{2,1,0:T(8,128)S(1)} fusion(f32[4,15,256]{2,1,0:T(8,128)S(1)} %collective-permute-done.5, f32[4,15,256]{2,1,0:T(8,128)S(1)} %collective-permute-done.4, f32[4,256,256]{2,1,0:T(8,128)S(1)} %fusion.609, f32[256,256]{1,0:T(8,128)} %fusion.760, f32[256,256]{1,0:T(8,128)} %fusion.761, f32[256,256]{1,0:T(8,128)} %fusion.762, ...), kind=kLoop, calls=%fused_computation.906 | loop fusion | flops 23855104 | bytes 10346496 | tf_op jit(solution)/shard_map/add | solution.py:78
  249.2 4.3 collective-permute-start.6
  253.5 2.1 collective-permute-start.7
  256.0 20.0 %collective-permute-done.6 = f32[4,256,15]{2,1,0:T(8,128)S(1)} collective-permute-done((f32[4,256,15]{2,1,0:T(8,128)S(1)}, f32[4,256,15]{2,1,0:T(8,128)S(1)}, u32[]{:S(2)}, u32[]{:S(2)}) %collective-permute-start.6) | collective-permute-done | bytes 61472 | tf_op jit(solution)/shard_map/ppermute | solution.py:14
  276.1 15.6 %fusion.177 = f32[4,256,256]{2,1,0:T(8,128)} fusion(f32[4,256,256]{2,1,0:T(8,128)S(1)} %add_add_fusion.2, f32[4,256,15]{2,1,0:T(8,128)S(1)} %collective-permute-done.7, f32[4,256,15]{2,1,0:T(8,128)S(1)} %collective-permute-done.6, f32[256,256]{1,0:T(8,128)S(1)} %fusion.953, f32[256,256]{1,0:T(8,128)S(1)} %fusion.955, f32[256,256]{1,0:T(8,128)} %fusion.957, ...), kind=kLoop, calls=%fused_computation.561 | loop fusion | flops 23855104 | bytes 10346496 | tf_op jit(solution)/shard_map/log | solution.py:144
  291.8 50.4 %all-reduce.7.cloned.1.call-done = f32[4,256,256]{2,1,0:T(8,128)} async-done(((f32[4,256,256]{2,1,0:T(8,128)}), f32[4,256,256]{2,1,0:T(8,128)}) %all-reduce.7.cloned.1.call-update) | async-done | bytes 1048592 | tf_op jit(solution)/shard_map/psum | solution.py:145
  342.2 1.4 exponential_multiply_fusion
  343.8 4.2 collective-permute-start.8
  348.1 4.4 collective-permute-start.9
  352.5 13.8 %collective-permute-done.8 = f32[4,256,15]{2,1,0:T(8,128)S(1)} collective-permute-done((f32[4,256,15]{2,1,0:T(8,128)S(1)}, f32[4,256,15]{2,1,0:T(8,128)S(1)}, u32[]{:S(2)}, u32[]{:S(2)}) %collective-permute-start.8) | collective-permute-done | bytes 61472 | tf_op jit(solution)/shard_map/ppermute | solution.py:14
  366.3 10.2 %collective-permute-done.9 = f32[4,256,15]{2,1,0:T(8,128)S(1)} collective-permute-done((f32[4,256,15]{2,1,0:T(8,128)S(1)}, f32[4,256,15]{2,1,0:T(8,128)S(1)}, u32[]{:S(2)}, u32[]{:S(2)}) %collective-permute-start.9) | collective-permute-done | bytes 61472 | tf_op jit(solution)/shard_map/ppermute | solution.py:14
  376.5 15.2 %fusion.90 = f32[4,256,256]{2,1,0:T(8,128)S(1)} fusion(f32[4,256,256]{2,1,0:T(8,128)S(1)} %exponential_multiply_fusion, f32[4,256,15]{2,1,0:T(8,128)S(1)} %collective-permute-done.9, f32[4,256,15]{2,1,0:T(8,128)S(1)} %collective-permute-done.8, f32[256,256]{1,0:T(8,128)} %fusion.825, f32[256,256]{1,0:T(8,128)} %fusion.826, f32[256,256]{1,0:T(8,128)} %fusion.827, ...), kind=kLoop, calls=%fused_computation.474 | loop fusion | flops 23855104 | bytes 10346496 | tf_op jit(solution)/shard_map/add | solution.py:45
  392.7 3.7 collective-permute-start.10
  396.5 4.1 collective-permute-start.11
  400.6 2.6 collective-permute-done.11
  403.1 8.2 %fusion.436 = f32[4,256,256]{2,1,0:T(8,128)S(1)} fusion(f32[4,15,256]{2,1,0:T(8,128)S(1)} %collective-permute-done.11, f32[4,15,256]{2,1,0:T(8,128)S(1)} %collective-permute-done.10, f32[4,256,256]{2,1,0:T(8,128)S(1)} %add_add_fusion.1, f32[1,1,4,256,256]{4,3,2,1,0:T(8,128)S(1)} %copy-done.50, f32[256,256]{1,0:T(8,128)} %fusion.790, ...), kind=kLoop, calls=%fused_computation.820 | loop fusion | flops 24117248 | bytes 11395072 | tf_op jit(solution)/shard_map/div | solution.py:140
  411.3 4.8 collective-permute-start.12
  416.3 2.5 collective-permute-start.13
  418.8 5.2 collective-permute-done.13
  424.0 8.6 %fusion.349 = f32[4,256,256]{2,1,0:T(8,128)S(1)} fusion(f32[4,15,256]{2,1,0:T(8,128)S(1)} %collective-permute-done.13, f32[4,15,256]{2,1,0:T(8,128)S(1)} %collective-permute-done.12, f32[4,256,256]{2,1,0:T(8,128)S(1)} %fusion.436, f32[256,256]{1,0:T(8,128)} %fusion.760, f32[256,256]{1,0:T(8,128)} %fusion.761, f32[256,256]{1,0:T(8,128)} %fusion.762, ...), kind=kLoop, calls=%fused_computation.733 | loop fusion | flops 23855104 | bytes 10346496 | tf_op jit(solution)/shard_map/add | solution.py:78
  433.9 5.2 collective-permute-start.14
  439.1 1.9 collective-permute-start.15
  441.0 11.6 %collective-permute-done.14 = f32[4,256,15]{2,1,0:T(8,128)S(1)} collective-permute-done((f32[4,256,15]{2,1,0:T(8,128)S(1)}, f32[4,256,15]{2,1,0:T(8,128)S(1)}, u32[]{:S(2)}, u32[]{:S(2)}) %collective-permute-start.14) | collective-permute-done | bytes 61472 | tf_op jit(solution)/shard_map/ppermute | solution.py:14
  453.7 15.6 %fusion.4 = f32[4,256,256]{2,1,0:T(8,128)} fusion(f32[4,256,256]{2,1,0:T(8,128)S(1)} %add_add_fusion, f32[4,256,15]{2,1,0:T(8,128)S(1)} %collective-permute-done.15, f32[4,256,15]{2,1,0:T(8,128)S(1)} %collective-permute-done.14, f32[256,256]{1,0:T(8,128)S(1)} %copy-done.80, f32[256,256]{1,0:T(8,128)S(1)} %copy-done.78, f32[256,256]{1,0:T(8,128)} %fusion.957, ...), kind=kLoop, calls=%fused_computation.388 | loop fusion | flops 23855104 | bytes 10346496 | tf_op jit(solution)/shard_map/log | solution.py:144
  469.4 58.8 %all-reduce.9.cloned.1.call-done = f32[4,256,256]{2,1,0:T(8,128)} async-done(((f32[4,256,256]{2,1,0:T(8,128)}), f32[4,256,256]{2,1,0:T(8,128)}) %all-reduce.9.cloned.1.call-update) | async-done | bytes 1048592 | tf_op jit(solution)/shard_map/psum | solution.py:145
  528.1 2.3 multiply_bitcast_fusion
  (472 shorter events, 146.4 us)
Async XLA Ops:
  6.5 335.7 %all-reduce.7.cloned.1.call-start = ((), (), s32[]{:S(2)}) async-start(), calls=%async_computation | async-start | bytes 2097152 | tf_op jit(solution)/shard_map/psum | solution.py:145
  8.9 180.9 %collective-permute-start = (f32[4,256,15]{2,1,0:T(8,128)}, f32[4,256,15]{2,1,0:T(8,128)}, u32[]{:S(2)}, u32[]{:S(2)}) collective-permute-start(f32[4,256,15]{2,1,0:T(8,128)} %get-tuple-element.112), channel_id=1, source_target_pairs={{0,4},{4,8},{8,12},{12,16},{16,20},{20,24},{24,28},{28,32},{32,36}... | collective-permute-start | bytes 184328 | tf_op jit(solution)/shard_map/ppermute | solution.py:14
  13.8 176.0 %collective-permute-start.1 = (f32[4,256,15]{2,1,0:T(8,128)}, f32[4,256,15]{2,1,0:T(8,128)}, u32[]{:S(2)}, u32[]{:S(2)}) collective-permute-start(f32[4,256,15]{2,1,0:T(8,128)} %get-tuple-element.113), channel_id=1, source_target_pairs={{4,0},{8,4},{12,8},{16,12},{20,16},{24,20},{28,24},{32,28},{36,32}... | collective-permute-start | bytes 184328 | tf_op jit(solution)/shard_map/ppermute | solution.py:14
  38.9 237.1 %copy-start.59 = (f32[256,256]{1,0:T(8,128)}, f32[256,256]{1,0:T(8,128)S(1)}, u32[]{:S(2)}) copy-start(f32[256,256]{1,0:T(8,128)S(1)} %fusion.1011) | copy-start | bytes 786436
  40.3 235.7 %copy-start.61 = (f32[256,256]{1,0:T(8,128)}, f32[256,256]{1,0:T(8,128)S(1)}, u32[]{:S(2)}) copy-start(f32[256,256]{1,0:T(8,128)S(1)} %fusion.1009) | copy-start | bytes 786436
  42.0 234.0 %copy-start.63 = (f32[256,256]{1,0:T(8,128)}, f32[256,256]{1,0:T(8,128)S(1)}, u32[]{:S(2)}) copy-start(f32[256,256]{1,0:T(8,128)S(1)} %fusion.1007) | copy-start | bytes 786436
  43.7 232.3 %copy-start.65 = (f32[256,256]{1,0:T(8,128)}, f32[256,256]{1,0:T(8,128)S(1)}, u32[]{:S(2)}) copy-start(f32[256,256]{1,0:T(8,128)S(1)} %fusion.1005) | copy-start | bytes 786436
  45.4 230.6 %copy-start.67 = (f32[256,256]{1,0:T(8,128)}, f32[256,256]{1,0:T(8,128)S(1)}, u32[]{:S(2)}) copy-start(f32[256,256]{1,0:T(8,128)S(1)} %fusion.1003) | copy-start | bytes 786436
  47.1 229.0 %copy-start.69 = (f32[256,256]{1,0:T(8,128)}, f32[256,256]{1,0:T(8,128)S(1)}, u32[]{:S(2)}) copy-start(f32[256,256]{1,0:T(8,128)S(1)} %fusion.1001) | copy-start | bytes 786436
  51.1 224.9 %copy-start.71 = (f32[256,256]{1,0:T(8,128)}, f32[256,256]{1,0:T(8,128)S(1)}, u32[]{:S(2)}) copy-start(f32[256,256]{1,0:T(8,128)S(1)} %fusion.997) | copy-start | bytes 786436
  52.8 223.3 %copy-start.73 = (f32[256,256]{1,0:T(8,128)}, f32[256,256]{1,0:T(8,128)S(1)}, u32[]{:S(2)}) copy-start(f32[256,256]{1,0:T(8,128)S(1)} %fusion.995) | copy-start | bytes 786436
  54.5 221.6 %copy-start.75 = (f32[256,256]{1,0:T(8,128)}, f32[256,256]{1,0:T(8,128)S(1)}, u32[]{:S(2)}) copy-start(f32[256,256]{1,0:T(8,128)S(1)} %fusion.993) | copy-start | bytes 786436
  56.3 219.8 %copy-start.77 = (f32[256,256]{1,0:T(8,128)}, f32[256,256]{1,0:T(8,128)S(1)}, u32[]{:S(2)}) copy-start(f32[256,256]{1,0:T(8,128)S(1)} %fusion.955) | copy-start | bytes 786436
  58.0 218.1 %copy-start.79 = (f32[256,256]{1,0:T(8,128)}, f32[256,256]{1,0:T(8,128)S(1)}, u32[]{:S(2)}) copy-start(f32[256,256]{1,0:T(8,128)S(1)} %fusion.953) | copy-start | bytes 786436
  113.4 134.6 %copy-start.1 = (f32[256,256]{1,0:T(8,128)}, f32[256,256]{1,0:T(8,128)S(1)}, u32[]{:S(2)}) copy-start(f32[256,256]{1,0:T(8,128)S(1)} %fusion.820) | copy-start | bytes 786436
  113.8 134.2 %copy-start.3 = (f32[256,256]{1,0:T(8,128)}, f32[256,256]{1,0:T(8,128)S(1)}, u32[]{:S(2)}) copy-start(f32[256,256]{1,0:T(8,128)S(1)} %fusion.859) | copy-start | bytes 786436
  114.2 133.9 %copy-start.5 = (f32[256,256]{1,0:T(8,128)}, f32[256,256]{1,0:T(8,128)S(1)}, u32[]{:S(2)}) copy-start(f32[256,256]{1,0:T(8,128)S(1)} %convolution_multiply_fusion.6) | copy-start | bytes 786436
  114.5 133.5 %copy-start.7 = (f32[256,256]{1,0:T(8,128)}, f32[256,256]{1,0:T(8,128)S(1)}, u32[]{:S(2)}) copy-start(f32[256,256]{1,0:T(8,128)S(1)} %convolution_multiply_fusion.5) | copy-start | bytes 786436
  114.9 133.1 %copy-start.9 = (f32[256,256]{1,0:T(8,128)}, f32[256,256]{1,0:T(8,128)S(1)}, u32[]{:S(2)}) copy-start(f32[256,256]{1,0:T(8,128)S(1)} %convolution_multiply_fusion.4) | copy-start | bytes 786436
  115.3 132.8 %copy-start.11 = (f32[256,256]{1,0:T(8,128)}, f32[256,256]{1,0:T(8,128)S(1)}, u32[]{:S(2)}) copy-start(f32[256,256]{1,0:T(8,128)S(1)} %convolution_multiply_fusion.3) | copy-start | bytes 786436
  115.7 132.4 %copy-start.13 = (f32[256,256]{1,0:T(8,128)}, f32[256,256]{1,0:T(8,128)S(1)}, u32[]{:S(2)}) copy-start(f32[256,256]{1,0:T(8,128)S(1)} %convolution_multiply_fusion.2) | copy-start | bytes 786436
  116.1 132.0 %copy-start.15 = (f32[256,256]{1,0:T(8,128)}, f32[256,256]{1,0:T(8,128)S(1)}, u32[]{:S(2)}) copy-start(f32[256,256]{1,0:T(8,128)S(1)} %convolution_multiply_fusion.1) | copy-start | bytes 786436
  116.4 131.7 %copy-start.17 = (f32[256,256]{1,0:T(8,128)}, f32[256,256]{1,0:T(8,128)S(1)}, u32[]{:S(2)}) copy-start(f32[256,256]{1,0:T(8,128)S(1)} %convolution_multiply_fusion.10) | copy-start | bytes 786436
  116.8 90.9 %copy-start.27 = (f32[256,256]{1,0:T(8,128)}, f32[256,256]{1,0:T(8,128)S(1)}, u32[]{:S(2)}) copy-start(f32[256,256]{1,0:T(8,128)S(1)} %convolution_multiply_fusion.23) | copy-start | bytes 786436
  117.2 90.5 %copy-start.29 = (f32[256,256]{1,0:T(8,128)}, f32[256,256]{1,0:T(8,128)S(1)}, u32[]{:S(2)}) copy-start(f32[256,256]{1,0:T(8,128)S(1)} %convolution_multiply_fusion.22) | copy-start | bytes 786436
  117.6 90.2 %copy-start.31 = (f32[256,256]{1,0:T(8,128)}, f32[256,256]{1,0:T(8,128)S(1)}, u32[]{:S(2)}) copy-start(f32[256,256]{1,0:T(8,128)S(1)} %convolution_multiply_fusion.21) | copy-start | bytes 786436
  118.0 89.8 %copy-start.33 = (f32[256,256]{1,0:T(8,128)}, f32[256,256]{1,0:T(8,128)S(1)}, u32[]{:S(2)}) copy-start(f32[256,256]{1,0:T(8,128)S(1)} %convolution_multiply_fusion.20) | copy-start | bytes 786436
  118.3 89.4 %copy-start.35 = (f32[256,256]{1,0:T(8,128)}, f32[256,256]{1,0:T(8,128)S(1)}, u32[]{:S(2)}) copy-start(f32[256,256]{1,0:T(8,128)S(1)} %convolution_multiply_fusion.19) | copy-start | bytes 786436
  118.7 89.1 %copy-start.37 = (f32[256,256]{1,0:T(8,128)}, f32[256,256]{1,0:T(8,128)S(1)}, u32[]{:S(2)}) copy-start(f32[256,256]{1,0:T(8,128)S(1)} %convolution_multiply_fusion.18) | copy-start | bytes 786436
  119.1 88.7 %copy-start.39 = (f32[256,256]{1,0:T(8,128)}, f32[256,256]{1,0:T(8,128)S(1)}, u32[]{:S(2)}) copy-start(f32[256,256]{1,0:T(8,128)S(1)} %convolution_multiply_fusion.17) | copy-start | bytes 786436
  119.5 88.3 %copy-start.41 = (f32[256,256]{1,0:T(8,128)}, f32[256,256]{1,0:T(8,128)S(1)}, u32[]{:S(2)}) copy-start(f32[256,256]{1,0:T(8,128)S(1)} %convolution_multiply_fusion.16) | copy-start | bytes 786436
  119.8 87.9 %copy-start.43 = (f32[256,256]{1,0:T(8,128)}, f32[256,256]{1,0:T(8,128)S(1)}, u32[]{:S(2)}) copy-start(f32[256,256]{1,0:T(8,128)S(1)} %convolution_multiply_fusion.15) | copy-start | bytes 786436
  120.2 87.6 %copy-start.45 = (f32[256,256]{1,0:T(8,128)}, f32[256,256]{1,0:T(8,128)S(1)}, u32[]{:S(2)}) copy-start(f32[256,256]{1,0:T(8,128)S(1)} %convolution_multiply_fusion.14) | copy-start | bytes 786436
  120.6 87.2 %copy-start.47 = (f32[256,256]{1,0:T(8,128)}, f32[256,256]{1,0:T(8,128)S(1)}, u32[]{:S(2)}) copy-start(f32[256,256]{1,0:T(8,128)S(1)} %convolution_multiply_fusion.13) | copy-start | bytes 786436
  121.0 127.1 %copy-start.19 = (f32[256,256]{1,0:T(8,128)}, f32[256,256]{1,0:T(8,128)S(1)}, u32[]{:S(2)}) copy-start(f32[256,256]{1,0:T(8,128)S(1)} %convolution_multiply_fusion.9) | copy-start | bytes 786436
  121.4 126.8 %copy-start.21 = (f32[256,256]{1,0:T(8,128)}, f32[256,256]{1,0:T(8,128)S(1)}, u32[]{:S(2)}) copy-start(f32[256,256]{1,0:T(8,128)S(1)} %convolution_multiply_fusion.8) | copy-start | bytes 786436
  121.7 126.4 %copy-start.23 = (f32[256,256]{1,0:T(8,128)}, f32[256,256]{1,0:T(8,128)S(1)}, u32[]{:S(2)}) copy-start(f32[256,256]{1,0:T(8,128)S(1)} %convolution_multiply_fusion.7) | copy-start | bytes 786436
  122.1 126.0 %copy-start.25 = (f32[256,256]{1,0:T(8,128)}, f32[256,256]{1,0:T(8,128)S(1)}, u32[]{:S(2)}) copy-start(f32[256,256]{1,0:T(8,128)S(1)} %convolution_multiply_fusion.11) | copy-start | bytes 786436
  188.2 59.9 %copy-start.51 = (f32[256,256]{1,0:T(8,128)}, f32[256,256]{1,0:T(8,128)S(1)}, u32[]{:S(2)}) copy-start(f32[256,256]{1,0:T(8,128)S(1)} %get-tuple-element.115) | copy-start | bytes 786436
  188.7 59.4 %copy-start.53 = (f32[256,256]{1,0:T(8,128)}, f32[256,256]{1,0:T(8,128)S(1)}, u32[]{:S(2)}) copy-start(f32[256,256]{1,0:T(8,128)S(1)} %get-tuple-element.116) | copy-start | bytes 786436
  208.7 7.9 %collective-permute-start.2 = (f32[4,15,256]{2,1,0:T(8,128)S(1)}, f32[4,15,256]{2,1,0:T(8,128)S(1)}, u32[]{:S(2)}, u32[]{:S(2)}) collective-permute-start(f32[4,15,256]{2,1,0:T(8,128)S(1)} %get-tuple-element.110), channel_id=1, source_target_pairs={{0,32},{4,36},{8,40},{12,44},{16,48},{20,52},{24,56},{28,60},{32,6... | collective-permute-start | bytes 184328 | tf_op jit(solution)/shard_map/ppermute | solution.py:14
  213.0 6.5 %collective-permute-start.3 = (f32[4,15,256]{2,1,0:T(8,128)S(1)}, f32[4,15,256]{2,1,0:T(8,128)S(1)}, u32[]{:S(2)}, u32[]{:S(2)}) collective-permute-start(f32[4,15,256]{2,1,0:T(8,128)S(1)} %get-tuple-element.111), channel_id=1, source_target_pairs={{32,0},{36,4},{40,8},{44,12},{48,16},{52,20},{56,24},{60,28},{64,3... | collective-permute-start | bytes 184328 | tf_op jit(solution)/shard_map/ppermute | solution.py:14
  227.7 7.2 %collective-permute-start.4 = (f32[4,15,256]{2,1,0:T(8,128)S(1)}, f32[4,15,256]{2,1,0:T(8,128)S(1)}, u32[]{:S(2)}, u32[]{:S(2)}) collective-permute-start(f32[4,15,256]{2,1,0:T(8,128)S(1)} %get-tuple-element.108), channel_id=1, source_target_pairs={{32,0},{36,4},{40,8},{44,12},{48,16},{52,20},{56,24},{60,28},{64,3... | collective-permute-start | bytes 184328 | tf_op jit(solution)/shard_map/ppermute | solution.py:14
  232.0 7.4 %collective-permute-start.5 = (f32[4,15,256]{2,1,0:T(8,128)S(1)}, f32[4,15,256]{2,1,0:T(8,128)S(1)}, u32[]{:S(2)}, u32[]{:S(2)}) collective-permute-start(f32[4,15,256]{2,1,0:T(8,128)S(1)} %get-tuple-element.109), channel_id=1, source_target_pairs={{0,32},{4,36},{8,40},{12,44},{16,48},{20,52},{24,56},{28,60},{32,6... | collective-permute-start | bytes 184328 | tf_op jit(solution)/shard_map/ppermute | solution.py:14
  249.2 26.8 %collective-permute-start.6 = (f32[4,256,15]{2,1,0:T(8,128)S(1)}, f32[4,256,15]{2,1,0:T(8,128)S(1)}, u32[]{:S(2)}, u32[]{:S(2)}) collective-permute-start(f32[4,256,15]{2,1,0:T(8,128)S(1)} %get-tuple-element.106), channel_id=1, source_target_pairs={{4,0},{8,4},{12,8},{16,12},{20,16},{24,20},{28,24},{32,28},{36,32}... | collective-permute-start | bytes 184328 | tf_op jit(solution)/shard_map/ppermute | solution.py:14
  253.5 22.5 %collective-permute-start.7 = (f32[4,256,15]{2,1,0:T(8,128)S(1)}, f32[4,256,15]{2,1,0:T(8,128)S(1)}, u32[]{:S(2)}, u32[]{:S(2)}) collective-permute-start(f32[4,256,15]{2,1,0:T(8,128)S(1)} %get-tuple-element.107), channel_id=1, source_target_pairs={{0,4},{4,8},{8,12},{12,16},{16,20},{20,24},{24,28},{28,32},{32,36}... | collective-permute-start | bytes 184328 | tf_op jit(solution)/shard_map/ppermute | solution.py:14
  291.8 236.4 %all-reduce.9.cloned.1.call-start = ((), (), s32[]{:S(2)}) async-start(), calls=%async_computation.1 | async-start | bytes 2097152 | tf_op jit(solution)/shard_map/psum | solution.py:145
  343.8 22.5 %collective-permute-start.8 = (f32[4,256,15]{2,1,0:T(8,128)S(1)}, f32[4,256,15]{2,1,0:T(8,128)S(1)}, u32[]{:S(2)}, u32[]{:S(2)}) collective-permute-start(f32[4,256,15]{2,1,0:T(8,128)S(1)} %get-tuple-element.104), channel_id=1, source_target_pairs={{0,4},{4,8},{8,12},{12,16},{16,20},{20,24},{24,28},{28,32},{32,36}... | collective-permute-start | bytes 184328 | tf_op jit(solution)/shard_map/ppermute | solution.py:14
  348.0 43.8 %copy-start.2 = (f32[256,256]{1,0:T(8,128)S(1)}, f32[256,256]{1,0:T(8,128)}, u32[]{:S(2)}) copy-start(f32[256,256]{1,0:T(8,128)} %copy-done.1) | copy-start | bytes 786436
  348.0 43.8 %copy-start.4 = (f32[256,256]{1,0:T(8,128)S(1)}, f32[256,256]{1,0:T(8,128)}, u32[]{:S(2)}) copy-start(f32[256,256]{1,0:T(8,128)} %copy-done.3) | copy-start | bytes 786436
  348.0 43.8 %copy-start.28 = (f32[256,256]{1,0:T(8,128)S(1)}, f32[256,256]{1,0:T(8,128)}, u32[]{:S(2)}) copy-start(f32[256,256]{1,0:T(8,128)} %copy-done.27) | copy-start | bytes 786436
  348.0 43.8 %copy-start.30 = (f32[256,256]{1,0:T(8,128)S(1)}, f32[256,256]{1,0:T(8,128)}, u32[]{:S(2)}) copy-start(f32[256,256]{1,0:T(8,128)} %copy-done.29) | copy-start | bytes 786436
  348.0 43.8 %copy-start.32 = (f32[256,256]{1,0:T(8,128)S(1)}, f32[256,256]{1,0:T(8,128)}, u32[]{:S(2)}) copy-start(f32[256,256]{1,0:T(8,128)} %copy-done.31) | copy-start | bytes 786436
  348.0 43.8 %copy-start.34 = (f32[256,256]{1,0:T(8,128)S(1)}, f32[256,256]{1,0:T(8,128)}, u32[]{:S(2)}) copy-start(f32[256,256]{1,0:T(8,128)} %copy-done.33) | copy-start | bytes 786436
  348.0 43.8 %copy-start.36 = (f32[256,256]{1,0:T(8,128)S(1)}, f32[256,256]{1,0:T(8,128)}, u32[]{:S(2)}) copy-start(f32[256,256]{1,0:T(8,128)} %copy-done.35) | copy-start | bytes 786436
  348.0 43.8 %copy-start.38 = (f32[256,256]{1,0:T(8,128)S(1)}, f32[256,256]{1,0:T(8,128)}, u32[]{:S(2)}) copy-start(f32[256,256]{1,0:T(8,128)} %copy-done.37) | copy-start | bytes 786436
  348.0 43.8 %copy-start.40 = (f32[256,256]{1,0:T(8,128)S(1)}, f32[256,256]{1,0:T(8,128)}, u32[]{:S(2)}) copy-start(f32[256,256]{1,0:T(8,128)} %copy-done.39) | copy-start | bytes 786436
  348.1 28.4 %collective-permute-start.9 = (f32[4,256,15]{2,1,0:T(8,128)S(1)}, f32[4,256,15]{2,1,0:T(8,128)S(1)}, u32[]{:S(2)}, u32[]{:S(2)}) collective-permute-start(f32[4,256,15]{2,1,0:T(8,128)S(1)} %get-tuple-element.105), channel_id=1, source_target_pairs={{4,0},{8,4},{12,8},{16,12},{20,16},{24,20},{28,24},{32,28},{36,32}... | collective-permute-start | bytes 184328 | tf_op jit(solution)/shard_map/ppermute | solution.py:14
  392.7 7.8 %collective-permute-start.10 = (f32[4,15,256]{2,1,0:T(8,128)S(1)}, f32[4,15,256]{2,1,0:T(8,128)S(1)}, u32[]{:S(2)}, u32[]{:S(2)}) collective-permute-start(f32[4,15,256]{2,1,0:T(8,128)S(1)} %get-tuple-element.102), channel_id=1, source_target_pairs={{0,32},{4,36},{8,40},{12,44},{16,48},{20,52},{24,56},{28,60},{32,6... | collective-permute-start | bytes 184328 | tf_op jit(solution)/shard_map/ppermute | solution.py:14
  396.5 6.6 %collective-permute-start.11 = (f32[4,15,256]{2,1,0:T(8,128)S(1)}, f32[4,15,256]{2,1,0:T(8,128)S(1)}, u32[]{:S(2)}, u32[]{:S(2)}) collective-permute-start(f32[4,15,256]{2,1,0:T(8,128)S(1)} %get-tuple-element.103), channel_id=1, source_target_pairs={{32,0},{36,4},{40,8},{44,12},{48,16},{52,20},{56,24},{60,28},{64,3... | collective-permute-start | bytes 184328 | tf_op jit(solution)/shard_map/ppermute | solution.py:14
  411.3 7.5 %collective-permute-start.12 = (f32[4,15,256]{2,1,0:T(8,128)S(1)}, f32[4,15,256]{2,1,0:T(8,128)S(1)}, u32[]{:S(2)}, u32[]{:S(2)}) collective-permute-start(f32[4,15,256]{2,1,0:T(8,128)S(1)} %get-tuple-element.100), channel_id=1, source_target_pairs={{32,0},{36,4},{40,8},{44,12},{48,16},{52,20},{56,24},{60,28},{64,3... | collective-permute-start | bytes 184328 | tf_op jit(solution)/shard_map/ppermute | solution.py:14
  416.3 7.7 %collective-permute-start.13 = (f32[4,15,256]{2,1,0:T(8,128)S(1)}, f32[4,15,256]{2,1,0:T(8,128)S(1)}, u32[]{:S(2)}, u32[]{:S(2)}) collective-permute-start(f32[4,15,256]{2,1,0:T(8,128)S(1)} %get-tuple-element.101), channel_id=1, source_target_pairs={{0,32},{4,36},{8,40},{12,44},{16,48},{20,52},{24,56},{28,60},{32,6... | collective-permute-start | bytes 184328 | tf_op jit(solution)/shard_map/ppermute | solution.py:14
  433.9 18.8 %collective-permute-start.14 = (f32[4,256,15]{2,1,0:T(8,128)S(1)}, f32[4,256,15]{2,1,0:T(8,128)S(1)}, u32[]{:S(2)}, u32[]{:S(2)}) collective-permute-start(f32[4,256,15]{2,1,0:T(8,128)S(1)} %get-tuple-element.98), channel_id=1, source_target_pairs={{4,0},{8,4},{12,8},{16,12},{20,16},{24,20},{28,24},{32,28},{36,32}... | collective-permute-start | bytes 184328 | tf_op jit(solution)/shard_map/ppermute | solution.py:14
  439.1 14.5 %collective-permute-start.15 = (f32[4,256,15]{2,1,0:T(8,128)S(1)}, f32[4,256,15]{2,1,0:T(8,128)S(1)}, u32[]{:S(2)}, u32[]{:S(2)}) collective-permute-start(f32[4,256,15]{2,1,0:T(8,128)S(1)} %get-tuple-element.99), channel_id=1, source_target_pairs={{0,4},{4,8},{8,12},{12,16},{16,20},{20,24},{24,28},{28,32},{32,36}... | collective-permute-start | bytes 184328 | tf_op jit(solution)/shard_map/ppermute | solution.py:14
  (41 other events, 868.7 us)
Sparse Core Ops, SparseCore 0:
  291.9 50.2 all-reduce.6
  469.5 58.6 all-reduce.8
where the time goes:
time: 548 us; the launch traced here: 538 us
  waiting for transfers between devices  181 us (33%)
  matrix products  167 us (30%)
  other arithmetic  109 us (20%)
  starting transfers between devices  61.5 us (11%)
  between operations  15.9 us (3%)
    dot_general x155, matrix products, weight_map(): return jnp.dot(inner, col_hot.T, precision=lax.Precision.HIGHEST)  136 us
    psum x2, waiting for transfers between devices, per_device(): summed = lax.psum(logged, 'view')  109 us
    ppermute x16, waiting for transfers between devices, passed_along(): return lax.ppermute(block, axis, route)  71.9 us
    ppermute x16, starting transfers between devices, passed_along(): return lax.ppermute(block, axis, route)  61.4 us
    add x2, other arithmetic, blur_cols(): result = result + weights[None] * padded[:, :, offset:offset + count]  33.1 us
    log x2, other arithmetic, per_device(): logged = jnp.log(correction)  31.2 us
    dot_general x124, matrix products, weight_map(): jnp.dot(row_hot, tile_taps[:, :, axis_id, offset], precision=lax.Precisio...  30.2 us
    add x2, other arithmetic, adjoint_rows(): result + weights[None, lead:lead + count, :] * padded[:, lead:lead + coun...  17.1 us
  transfers between devices with their start and end apart: 18, of which 11 were waited for; matrix products, arithmetic and copies ran while one was open for 32% of the time, Pallas kernels for 0%

commit v1 on v0

v1 whole, which is shorter than its diff:
```python
import functools

import jax
import jax.numpy as jnp
from jax import lax
from jax.experimental import pallas as pl
from jax.experimental.pallas import tpu as pltpu
from jax.sharding import PartitionSpec as P

GX = 8
ITERS = 2
HALF = 15
F32 = jnp.float32
BF16 = jnp.bfloat16
VMEM = pltpu.VMEM
SMEM = pltpu.SMEM


def call(body, outs, scratch, *args, cost=None):
    specs = [pl.BlockSpec(memory_space=SMEM)] + [pl.BlockSpec(memory_space=VMEM)] * (len(args) - 1)
    return pl.pallas_call(
        body,
        out_shape=outs,
        in_specs=specs,
        out_specs=jax.tree.map(lambda _: pl.BlockSpec(memory_space=VMEM), outs),
        scratch_shapes=scratch,
        compiler_params=pltpu.CompilerParams(vmem_limit_bytes=52 * 1024 * 1024),
        cost_estimate=cost,
    )(*args)


def shape(*dims, dtype=F32):
    return jax.ShapeDtypeStruct(dims, dtype)


def lanes(rows, width=128):
    return lax.broadcasted_iota(jnp.int32, (rows, width), 1)


def turn(x, amount):
    amount = amount % x.shape[-1]
    return x if amount == 0 else pltpu.roll(x, amount, axis=x.ndim - 1)


def packed(pieces, first, width):
    rows = pieces[0].shape[0]
    lane = lanes(rows)
    out = jnp.zeros((rows, 128), F32)
    for n, piece in enumerate(pieces):
        inside = (lane >= n * width) & (lane < (n + 1) * width)
        out = jnp.where(inside, turn(piece, n * width - first), out)
    return out


def split(x):
    high = x.astype(BF16)
    return high, (x - high.astype(F32)).astype(BF16)


def dot3(a, b):
    (ah, al), (bh, bl) = a, b
    dot = functools.partial(jnp.dot, preferred_element_type=F32)
    return dot(ah, bh) + (dot(al, bh) + dot(ah, bl))


def pack_kernel(info, rec, first, taps, sent, main, inside, edge):
    view = info[0]
    for q in range(4):
        qx, qy = q // 2, q % 2
        rows = slice(112 * qy, 112 * qy + 144)
        slot = jnp.bitwise_xor(view, q)
        for z in range(4):
            sent[slot, z] = rec[z, rows, 128 * qx : 128 * qx + 128]
        near = [rec[z, rows, 128 - 128 * qx : 256 - 128 * qx] for z in range(4)]
        side = packed(near, 112 * qx, 16)
        sent[slot, 4, 16:] = side[16:]
        sent[slot, 4, :16] = side[:16] + taps[q]

        @pl.when(view == q)
        def _():
            span = slice(96 * qy, 96 * qy + 160)
            for z in range(4):
                main[z] = first[z, span, 128 * qx : 128 * qx + 128]
            beside = [first[z, span, 128 - 128 * qx : 256 - 128 * qx] for z in range(4)]
            inside[...] = packed(beside, 96 * qx, 32)
            own = [first[z, span, 128 * qx : 128 * qx + 128] for z in range(4)]
            edge[...] = packed(own, 96 * qx, 32)


def pack_cols_kernel(info, got, edge, out):
    qx = info[1]
    for side in range(2):

        @pl.when(qx == side)
        def _():
            for h in range(2):
                pieces = [got[(2 * h + s) ^ 2, z] for s in range(2) for z in range(4)]
                out[h * 144 : h * 144 + 144] = packed(pieces, 112 * side, 16)

    out[288:] = edge[...]


def pack_rows_kernel(info, got, cols, main, inside, out):
    qy = info[2]
    low = lanes(16) < 64
    for side in range(2):

        @pl.when(qy == side)
        def _():
            rows = slice(128 * side, 128 * side + 16)
            for s in range(4):
                for z in range(4):
                    n = 4 * s + z
                    out[n * 16 : n * 16 + 16] = got[s ^ 1, z, rows]
            for h in range(2):
                one, two = got[2 * h + 1, 4, rows], got[2 * h, 4, rows]
                out[256 + 16 * h : 272 + 16 * h] = jnp.where(low, one, turn(two, 64))
                wide = cols[h * 144 + rows.start : h * 144 + rows.stop]
                out[288 + 16 * h : 304 + 16 * h] = turn(wide, 64)
            rows = slice(128 * side, 128 * side + 32)
            for z in range(4):
                out[320 + 32 * z : 352 + 32 * z] = main[z, rows]
            out[448:480] = inside[rows]
            out[480:512] = cols[288 + rows.start : 288 + rows.stop]


def toeplitz(base, shift):
    return pltpu.roll(base, shift % 256, axis=1, stride=1, stride_axis=0)


def matrices_kernel(info, got, xh, xl, ah, al, yh, yl, th, tl, zw):
    qx, qy = info[1], info[2]

    def far_lane(rows):
        lane = lanes(rows, 256)
        return (lane >= 128) & ((lane < 192) == (qx == 1))

    def body(s, carry):
        table = got[s, 4, 0:16]
        lane = lanes(16)
        fwd = jnp.where(lane < 31, turn(table, 64), 0.0)
        rev = jnp.where(lane < 31, turn(table, 32), 0.0)
        zero = jnp.zeros((16, 128), F32)
        fwd = jnp.concatenate([fwd, zero], 1)
        rev = jnp.concatenate([rev, zero], 1)

        def wide(which, tile, axis, rows):
            return jnp.broadcast_to(which[3 * tile + axis : 3 * tile + axis + 1], (rows, 256))

        def keep(high, low, index, value):
            high[index], low[index] = split(value)

        far = far_lane(256)
        for g in range(2):
            near_t = toeplitz(wide(rev, 2 * g, 0, 256), -HALF)
            far_t = toeplitz(wide(rev, 2 * g + 1, 0, 256), -HALF)
            keep(xh, xl, (s, g), jnp.where(far, far_t, near_t))
        row = lax.broadcasted_iota(jnp.int32, (256, 256), 0)
        far_row = (row >= 128) & ((row < 192) == (qx == 1))
        base = jnp.where(far_row, wide(fwd, 1, 0, 256), wide(fwd, 0, 0, 256))
        keep(ah, al, s, toeplitz(base, -HALF)[:, :128])
        for g in range(2):
            row = lax.broadcasted_iota(jnp.int32, (160, 256), 0)
            other = jnp.where(qy == 0, row, 159 - row) < 16
            base = jnp.where(other, wide(fwd, 2 + g, 1, 160), wide(fwd, g, 1, 160))
            keep(yh, yl, (s, g), toeplitz(base, 1))
            lane = lanes(128, 256)
            other = jnp.where(qy == 0, lane, 159 - lane) < 16
            near_t = toeplitz(wide(rev, g, 1, 128), 1)
            far_t = toeplitz(wide(rev, 2 + g, 1, 128), 1)
            keep(th, tl, (s, g), jnp.where(other, far_t, near_t))
        far = far_lane(1)
        for g in range(2):
            for d in range(7):
                near_w = fwd[6 * g + 2 : 6 * g + 3, 12 + d : 13 + d]
                far_w = fwd[6 * g + 5 : 6 * g + 6, 12 + d : 13 + d]
                weight = jnp.where(
                    far, jnp.broadcast_to(far_w, (1, 256)), jnp.broadcast_to(near_w, (1, 256))
                )
                zw[s, g, d : d + 1] = weight
        return carry

    lax.fori_loop(0, 4, body, 0)


def sided(left, right, width, n, rows):
    lane = lanes(rows)
    out = jnp.where(lane < width, turn(right, -n * width), 0.0)
    return jnp.where(lane >= 128 - width, turn(left, 128 - width - n * width), out)


def step_kernel(first, info, *refs):
    if first:
        (main, inside, cols, rows_in, got), refs = refs[:5], refs[5:]
    else:
        (main, inside, beyond, rows_in, rows_out, rec), refs = refs[:6], refs[6:]
    (xh, xl, ah, al, yh, yl, th, tl, zw), refs = refs[:9], refs[9:]
    if first:
        (out, near_edge, far_edge, rec), refs = refs[:4], refs[4:]
    else:
        (out,), refs = refs[:1], refs[1:]
    region, eh, el, mid, ph, plo, rh, rl, total = refs
    qx, qy = info[1], info[2]
    own = pl.multiple_of(32 * (1 - qy), 32)
    other = pl.multiple_of(160 * qy, 32)

    if first:
        for z in range(4):
            region[z, pl.ds(own, 160)] = main[z]
            region[z, pl.ds(other, 32)] = rows_in[320 + 32 * z : 352 + 32 * z]
        region[4, pl.ds(own, 160)] = inside[...]
        region[5, pl.ds(own, 160)] = cols[288:448]
        region[4, pl.ds(other, 32)] = rows_in[448:480]
        region[5, pl.ds(other, 32)] = rows_in[480:512]
    else:
        for z in range(4):
            region[z, 32:160] = main[z]
        region[4, 32:160] = inside[...]
        region[5, 32:160] = beyond[...]
        for p in range(6):
            region[p, pl.ds(pl.multiple_of(160 * (1 - qy), 32), 32)] = rows_in[p]
            region[p, pl.ds(other, 32)] = rows_out[p]
    left = jnp.where(qx == 0, region[5], region[4])
    right = jnp.where(qx == 0, region[4], region[5])
    for z in range(4):
        eh[z, :, :128], el[z, :, :128] = split(region[z])
        eh[z, :, 128:], el[z, :, 128:] = split(sided(left, right, 32, z, 192))

    if first:
        in_tile = pl.multiple_of(16 * (1 - qy), 16)
        out_tile = pl.multiple_of(144 * qy, 16)
        for s in range(4):
            h, m = s // 2, 4 * (s % 2)
            for z in range(4):
                rec[s, z, pl.ds(in_tile, 144), :128] = got[s, z]
                n = 4 * s + z
                rec[s, z, pl.ds(out_tile, 16), :128] = rows_in[n * 16 : n * 16 + 16]
            for at, count, inner, outer, shift in (
                (in_tile, 144, got[s, 4], cols[h * 144 : h * 144 + 144], 0),
                (
                    out_tile,
                    16,
                    rows_in[256 + 16 * h : 272 + 16 * h],
                    rows_in[288 + 16 * h : 304 + 16 * h],
                    64 * (s % 2),
                ),
            ):
                inner = turn(inner, -shift)
                outer = turn(outer, -16 * m)
                lhs = jnp.where(qx == 0, outer, inner)
                rhs = jnp.where(qx == 0, inner, outer)
                for z in range(4):
                    rec[s, z, pl.ds(at, count), 128:] = sided(lhs, rhs, 16, z, count)

    ph[:, 192:] = jnp.zeros((4, 64, 256), BF16)
    plo[:, 192:] = jnp.zeros((4, 64, 256), BF16)
    rh[:, 160:] = jnp.zeros((4, 96, 256), BF16)
    rl[:, 160:] = jnp.zeros((4, 96, 256), BF16)
    total[...] = jnp.zeros_like(total)

    lane = lanes(160, 256)
    row = lax.broadcasted_iota(jnp.int32, (160, 256), 0)
    used = (lane < 144) | (lane >= 240)
    far = (lane >= 128) & ((lane < 192) == (qx == 1))
    past = jnp.where(qy == 0, row, 159 - row) < 16
    valid = used & ((info[3] > 0) | ~far) & ((info[4] > 0) | ~past)
    far160 = far[:, 128:]
    far128 = far[:128, 128:]

    def body(s, carry):
        for g, at, count in ((0, own, 160), (1, other, 32)):
            for z in range(4):
                here = (eh[z, pl.ds(at, count)], el[z, pl.ds(at, count)])
                mid[z, pl.ds(at, count)] = dot3(here, (xh[s, g], xl[s, g]))
            weights = [zw[s, g, d : d + 1] for d in range(7)]
            planes = [mid[z, pl.ds(at, count)] for z in range(4)]
            for z in range(4):
                value = sum(weights[3 + k - z] * planes[k] for k in range(4))
                ph[z, pl.ds(at, count)], plo[z, pl.ds(at, count)] = split(value)
        y_own, y_far = (yh[s, 0], yl[s, 0]), (yh[s, 1], yl[s, 1])
        for z in range(4):
            blurred = dot3(y_own, (ph[z], plo[z]))
            edge = dot3(y_far, (ph[z, :, 128:], plo[z, :, 128:]))
            blurred = jnp.concatenate(
                [blurred[:, :128], jnp.where(far160, edge, blurred[:, 128:])], 1
            )
            ratio = jnp.where(valid, rec[s, z] / blurred, 0.0)
            rh[z, :160], rl[z, :160] = split(ratio)
        t_own, t_far = (th[s, 0], tl[s, 0]), (th[s, 1], tl[s, 1])
        planes = []
        for z in range(4):
            back = dot3(t_own, (rh[z], rl[z]))
            edge = dot3(t_far, (rh[z, :, 128:], rl[z, :, 128:]))
            mid[z, :128] = jnp.concatenate(
                [back[:, :128], jnp.where(far128, edge, back[:, 128:])], 1
            )
        weights = [zw[s, 0, d : d + 1] for d in range(7)]
        planes = [mid[z, :128] for z in range(4)]
        for z in range(4):
            value = sum(weights[3 + z - k] * planes[k] for k in range(4))
            correction = dot3(split(value), (ah[s], al[s]))
            total[z] += jnp.log(correction)
        return carry

    lax.fori_loop(0, 4, body, 0)
    new = []
    for z in range(4):
        value = region[z, 32:160] * jnp.exp(total[z] / 4)
        out[z] = value
        new.append(value)
    if first:
        low, high = packed(new, 0, 32), packed(new, 96, 32)
        near_edge[...] = jnp.where(qx == 0, high, low)
        far_edge[...] = jnp.where(qx == 0, low, high)


def per_device(initial, recorded, tap_table, variants):
    tile = lax.axis_index("tile")
    view = lax.axis_index("view")
    count_tiles = lax.axis_size("tile")
    grid_rows = count_tiles // GX
    tile_row, tile_col = tile // GX, tile % GX
    qx, qy = view // 2, view % 2
    has_x = jnp.where(qx == 0, tile_col > 0, tile_col < GX - 1)
    has_y = jnp.where(qy == 0, tile_row > 0, tile_row < grid_rows - 1)
    info = jnp.stack([view, qx, qy, has_x.astype(jnp.int32), has_y.astype(jnp.int32)])

    def route(x, pairs):
        return lax.ppermute(x, ("tile", "view"), pairs)

    def over_view(x, flip):
        return lax.ppermute(x, "view", [(i, i ^ flip) for i in range(4)])

    x_pairs, y_pairs = [], []
    for t in range(count_tiles):
        for v in range(4):
            if v // 2 and t % GX < GX - 1:
                x_pairs += [(4 * t + v, 4 * (t + 1) + v - 2), (4 * (t + 1) + v - 2, 4 * t + v)]
            if v % 2 and t + GX < count_tiles:
                y_pairs += [(4 * t + v, 4 * (t + GX) + v - 1), (4 * (t + GX) + v - 1, 4 * t + v)]

    kernels = tap_table[0] / jnp.sum(tap_table[0], axis=-1, keepdims=True)
    steps_x = jnp.array([[0, d, 0, d] for d in (-1, -1, 1, 1)], jnp.int32)
    steps_y = jnp.array([[0, 0, d, d] for d in (-1, 1, -1, 1)], jnp.int32)
    near_x = jnp.clip(tile_col + steps_x, 0, GX - 1)
    near_y = jnp.clip(tile_row + steps_y, 0, grid_rows - 1)
    near = (near_y * GX + near_x).reshape(16)
    ids = jnp.sum(
        jnp.where(near[:, None] == jnp.arange(count_tiles)[None], variants[0][None], 0), axis=1
    )
    picked = ids[:, None] == jnp.arange(kernels.shape[0])[None]
    taps = jnp.sum(jnp.where(picked[:, :, None, None], kernels[None], 0.0), axis=1)
    taps = taps.reshape(4, 12, 31)
    taps = jnp.concatenate([jnp.pad(taps, ((0, 0), (0, 0), (64, 1))), taps[..., ::-1]], axis=-1)
    taps = jnp.pad(taps, ((0, 0), (0, 4), (0, 1)))

    sent, main, inside, edge = call(
        pack_kernel,
        (shape(4, 5, 144, 128), shape(4, 160, 128), shape(160, 128), shape(160, 128)),
        [],
        info,
        recorded[0, 0],
        initial[0],
        taps,
    )
    got = jnp.stack([sent[0]] + [over_view(sent[s], s) for s in (1, 2, 3)])
    cols = route(call(pack_cols_kernel, shape(448, 128), [], info, got, edge), x_pairs)
    mats = call(
        matrices_kernel,
        tuple(
            shape(4, *dims, dtype=BF16)
            for dims in ((2, 256, 256), (256, 128), (2, 160, 256), (2, 128, 256))
            for _ in range(2)
        )
        + (shape(4, 2, 8, 256),),
        [],
        info,
        got,
    )
    rows = route(
        call(pack_rows_kernel, shape(512, 128), [], info, got, cols, main, inside), y_pairs
    )
    scratch = [
        VMEM((6, 192, 128), F32),
        VMEM((4, 192, 256), BF16),
        VMEM((4, 192, 256), BF16),
        VMEM((4, 192, 256), F32),
        VMEM((4, 256, 256), BF16),
        VMEM((4, 256, 256), BF16),
        VMEM((4, 256, 256), BF16),
        VMEM((4, 256, 256), BF16),
        VMEM((4, 128, 128), F32),
    ]
    quad = shape(4, 128, 128)
    cost = pl.CostEstimate(flops=8_000_000_000, bytes_accessed=12_000_000, transcendentals=600_000)
    estimate, near_edge, far_edge, rec = call(
        functools.partial(step_kernel, True),
        (quad, shape(128, 128), shape(128, 128), shape(4, 4, 160, 256)),
        scratch,
        info,
        main,
        inside,
        cols,
        rows,
        got,
        *mats,
        cost=cost,
    )
    for step in range(1, ITERS):
        inside = over_view(near_edge, 2)
        beyond = route(far_edge, x_pairs)
        whole = jnp.concatenate([estimate, inside[None], beyond[None]])
        low, high = whole[:, :32], whole[:, 96:]
        rows_in = over_view(jnp.where(qy == 0, high, low), 1)
        rows_out = route(jnp.where(qy == 0, low, high), y_pairs)
        estimate = call(
            functools.partial(step_kernel, False),
            quad,
            scratch,
            info,
            estimate,
            inside,
            beyond,
            rows_in,
            rows_out,
            rec,
            *mats,
            cost=cost,
        )
    across = over_view(estimate, 2)
    wide = jnp.where(
        qx == 0,
        jnp.concatenate([estimate, across], 2),
        jnp.concatenate([across, estimate], 2),
    )
    down = over_view(wide, 1)
    return jnp.where(
        qy == 0, jnp.concatenate([wide, down], 1), jnp.concatenate([down, wide], 1)
    )[None]


def solution(mesh):
    return jax.shard_map(
        per_device,
        mesh=mesh,
        in_specs=(
            P("tile", None, None, None),
            P("view", "tile", None, None, None),
            P("view", None, None, None),
            P("view", None),
        ),
        out_specs=P("tile", None, None, None),
        check_vma=False,
    )
```

time: 548 us -> 114 us (0.21); the launches traced: 538 us -> 114 us
  matrix products: 167 us -> 0 us
  waiting for transfers between devices: 181 us -> 41.6 us
  other arithmetic: 109 us -> 4.69 us
  Pallas kernels: 0 us -> 37.3 us
  starting transfers between devices: 61.5 us -> 25.7 us
  between operations: 15.9 us -> 0.15 us
    dot_general x280 -> x0, matrix products: 167 us -> none  [the longest x155 136 us: weight_map(): return jnp.dot(inner, col_hot.T, precision=lax.Precision.HIGHEST)]
    psum x2 -> x0, waiting for transfers between devices: 109 us -> none  [per_device(): summed = lax.psum(logged, 'view')]
    add x8 -> x1, other arithmetic: 53.6 us -> 0.7 us  [per_device(): near = (near_y * GX + near_x).reshape(16)]
    pallas_call x0 -> x6, Pallas kernels: none -> 37.3 us  [call(): pl.pallas_call(body, out_shape=outs, in_specs=specs, out_specs=jax.tree.m...]
    ppermute x16 -> x11, starting transfers between devices: 61.4 us -> 25.7 us  [the longest x4 21.4 us: route(): return lax.ppermute(x, ('tile', 'view'), pairs)]
    log x2 -> x0, other arithmetic: 31.2 us -> none  [per_device(): logged = jnp.log(correction)]
    ppermute x16 -> x11, waiting for transfers between devices: 71.9 us -> 41.6 us  [the longest x7 25.1 us: over_view(): return lax.ppermute(x, 'view', [(i, i ^ flip) for i in range(4)])]
    div x2 -> x0, other arithmetic: 16.4 us -> none  [per_device(): ratio = observed / blurred]
  transfers between devices with their start and end apart: 18 -> 11, of which waited for: 11 -> 8; matrix products, arithmetic and copies ran while one was open for 32% -> 0% of each run, Pallas kernels for 0% -> 5%
where the time goes in v1:
time: 114 us
  waiting for transfers between devices  41.6 us (36%)
  Pallas kernels  37.3 us (33%)
  starting transfers between devices  25.7 us (23%)
  other arithmetic  4.69 us (4%)
  local copies, waits for them, and re-layouts  4.52 us (4%)
    pallas_call x6, Pallas kernels, call(): pl.pallas_call(body, out_shape=outs, in_specs=specs, out_specs=jax.tree.m...  37.3 us
    ppermute x7, waiting for transfers between devices, over_view(): return lax.ppermute(x, 'view', [(i, i ^ flip) for i in range(4)])  25.1 us
    ppermute x4, starting transfers between devices, route(): return lax.ppermute(x, ('tile', 'view'), pairs)  21.4 us
    ppermute x4, waiting for transfers between devices, route(): return lax.ppermute(x, ('tile', 'view'), pairs)  16.5 us
    ppermute x7, starting transfers between devices, over_view(): return lax.ppermute(x, 'view', [(i, i ^ flip) for i in range(4)])  4.34 us
    unnamed x10, local copies, waits for them, and re-layouts  2.82 us
  transfers between devices with their start and end apart: 11, of which 8 were waited for; matrix products, arithmetic and copies ran while one was open for 0% of the time, Pallas kernels for 5%

profile of v1, /device:TPU:13, one launch (start us, length us, event | category | flops | bytes accessed | tf_op | source)
XLA Modules:
  0.0 113.9 jit_solution(8377213691524457671)
XLA Ops:
  0.0 0.7 clamp_add_fusion
  0.7 0.1 eq.47
  0.8 0.8 select_reduce_fusion.1
  1.6 0.1 iota_compare_fusion.1
  1.7 0.8 reduce_sum.28
  2.5 0.8 divide_bitcast_fusion
  3.3 0.2 select_reduce_fusion
  3.5 0.1 rev.3
  3.5 0.1 select_maximum_fusion
  3.6 0.1 stack.43.info
  3.7 0.0 copy-start.1
  3.7 1.2 %copy-done.1 = f32[1,1,4,256,256]{4,3,2,1,0:T(8,128)S(1)} copy-done((f32[1,1,4,256,256]{4,3,2,1,0:T(8,128)S(1)}, f32[1,1,4,256,256]{4,3,2,1,0:T(8,128)}, u32[]{:S(2)}) %copy-start.1) | copy-done | bytes 1048600
  5.0 3.1 %shard_map.64 = (f32[4,5,144,128]{3,2,1,0:T(8,128)}, f32[4,160,128]{2,1,0:T(8,128)S(1)}, f32[160,128]{1,0:T(8,128)S(1)}, f32[160,128]{1,0:T(8,128)S(1)}) custom-call(s32[5]{0:T(128)S(1)} %stack.43.info, f32[4,256,256]{2,1,0:T(8,128)S(1)} %bitcast.23, f32[4,256,256]{2,1,0:T(8,128)} %bitcast.27, f32[4,16,128]{2,1,0:T(8,128)S(1)} %pad.9.taps), custom_call_target="tpu_custom_call" | custom-call | tf_op jit(solution)/shard_map/pallas_call | solution.py:21
  8.0 1.4 %fusion = (f32[1,5,144,128]{3,2,1,0:T(8,128)S(1)}, f32[5,144,128]{2,1,0:T(8,128)S(1)}, f32[5,144,128]{2,1,0:T(8,128)S(1)}, f32[5,144,128]{2,1,0:T(8,128)S(1)}) fusion(f32[4,5,144,128]{3,2,1,0:T(8,128)} %get-tuple-element.24), kind=kLoop, calls=%fused_computation.19 | loop fusion | bytes 2949120 | tf_op jit(solution)/shard_map/slice | solution.py:366
  9.5 2.3 %collective-permute-start.2 = (f32[5,144,128]{2,1,0:T(8,128)S(1)}, f32[5,144,128]{2,1,0:T(8,128)S(1)}, u32[]{:S(2)}, u32[]{:S(2)}) collective-permute-start(f32[5,144,128]{2,1,0:T(8,128)S(1)} %get-tuple-element.43), channel_id=1, source_target_pairs={{0,3},{1,2},{2,1},{3,0},{4,7},{5,6},{6,5},{7,4},{8,11},{9,10},{10,... | collective-permute-start | bytes 1105928 | tf_op jit(solution)/shard_map/ppermute | solution.py:332
  11.8 0.0 collective-permute-start.1
  11.8 0.5 collective-permute-start
  12.3 8.6 %collective-permute-done.2 = f32[5,144,128]{2,1,0:T(8,128)S(1)} collective-permute-done((f32[5,144,128]{2,1,0:T(8,128)S(1)}, f32[5,144,128]{2,1,0:T(8,128)S(1)}, u32[]{:S(2)}, u32[]{:S(2)}) %collective-permute-start.2) | collective-permute-done | bytes 368672 | tf_op jit(solution)/shard_map/ppermute | solution.py:332
  20.8 7.4 %collective-permute-done.1 = f32[5,144,128]{2,1,0:T(8,128)S(1)} collective-permute-done((f32[5,144,128]{2,1,0:T(8,128)S(1)}, f32[5,144,128]{2,1,0:T(8,128)S(1)}, u32[]{:S(2)}, u32[]{:S(2)}) %collective-permute-start.1) | collective-permute-done | bytes 368672 | tf_op jit(solution)/shard_map/ppermute | solution.py:332
  28.2 0.0 collective-permute-done
  28.2 0.1 pad_maximum_fusion.got.refs_4_
  28.4 0.0 copy-start
  28.4 0.9 shard_map.65
  29.3 7.8 %collective-permute-start.3 = (f32[448,128]{1,0:T(8,128)S(1)}, f32[448,128]{1,0:T(8,128)S(1)}, u32[]{:S(2)}, u32[]{:S(2)}) collective-permute-start(f32[448,128]{1,0:T(8,128)S(1)} %shard_map.65), channel_id=1, source_target_pairs={{2,4},{4,2},{3,5},{5,3},{6,8},{8,6},{7,9},{9,7},{10,12},{12,10},{1... | collective-permute-start | bytes 688136 | tf_op jit(solution)/shard_map/ppermute | solution.py:329
  37.0 7.9 %collective-permute-done.3.cols.refs_2_ = f32[448,128]{1,0:T(8,128)S(1)} collective-permute-done((f32[448,128]{1,0:T(8,128)S(1)}, f32[448,128]{1,0:T(8,128)S(1)}, u32[]{:S(2)}, u32[]{:S(2)}) %collective-permute-start.3) | collective-permute-done | bytes 229408 | tf_op jit(solution)/shard_map/ppermute | solution.py:329
  45.0 0.0 copy-done
  45.0 1.5 %shard_map.66 = f32[512,128]{1,0:T(8,128)S(1)} custom-call(s32[5]{0:T(128)S(1)} %stack.43.info, f32[4,5,144,128]{3,2,1,0:T(8,128)} %copy-done, f32[448,128]{1,0:T(8,128)S(1)} %collective-permute-done.3.cols.refs_2_, f32[4,160,128]{2,1,0:T(8,128)S(1)} %get-tuple-element.22.main.refs_0_, f32[160,128]{1,0:T(8,128)S(1)} %get-tuple-element.23.inside.refs_1_), custom_call_target="tpu_custom_call" | custom-call | tf_op jit(solution)/shard_map/pallas_call | solution.py:21
  46.4 3.7 %collective-permute-start.4 = (f32[512,128]{1,0:T(8,128)S(1)}, f32[512,128]{1,0:T(8,128)S(1)}, u32[]{:S(2)}, u32[]{:S(2)}) collective-permute-start(f32[512,128]{1,0:T(8,128)S(1)} %shard_map.66), channel_id=1, source_target_pairs={{1,32},{32,1},{3,34},{34,3},{5,36},{36,5},{7,38},{38,7},{9,40},{40... | collective-permute-start | bytes 786440 | tf_op jit(solution)/shard_map/ppermute | solution.py:329
  50.2 5.4 %shard_map.67 = (bf16[4,2,256,256]{3,2,1,0:T(8,128)(2,1)}, bf16[4,2,256,256]{3,2,1,0:T(8,128)(2,1)}, bf16[4,256,128]{2,1,0:T(8,128)(2,1)S(1)}, bf16[4,256,128]{2...) custom-call(s32[5]{0:T(128)S(1)} %stack.43.info, ...), custom_call_target="tpu_custom_call" | custom-call | tf_op jit(solution)/shard_map/pallas_call | solution.py:21
  55.6 0.0 copy-start.2
  55.6 0.8 copy-done.2
  56.4 0.0 copy-start.4
  56.4 0.8 copy-done.4
  57.2 1.3 %collective-permute-done.4.refs_3_ = f32[512,128]{1,0:T(8,128)S(1)} collective-permute-done((f32[512,128]{1,0:T(8,128)S(1)}, f32[512,128]{1,0:T(8,128)S(1)}, u32[]{:S(2)}, u32[]{:S(2)}) %collective-permute-start.4) | collective-permute-done | bytes 262176 | tf_op jit(solution)/shard_map/ppermute | solution.py:329
  58.4 0.0 copy-start.3
  58.4 14.3 %shard_map.68 = (f32[4,128,128]{2,1,0:T(8,128)S(1)}, f32[128,128]{1,0:T(8,128)S(1)}, f32[128,128]{1,0:T(8,128)S(1)}, f32[4,4,160,256]{3,2,1,0:T(8,128)}) custom-call(s32[5]{0:T(128)S(1)} %stack.43.info, f32[4,160,128]{2,1,0:T(8,128)S(1)} %get-tuple-element.22.main.refs_0_, f32[160,128]{1,0:T(8,128)S(1)} %get-tuple-element.23.inside.refs_1_, ...), custom_call_target="tpu_custom_call" | custom-call | flops 8000000000 | bytes 12000000 | tf_op jit(solution)/shard_map/pallas_call | solution.py:21
  72.8 0.0 collective-permute-start.5
  72.8 6.2 %collective-permute-start.6 = (f32[128,128]{1,0:T(8,128)S(1)}, f32[128,128]{1,0:T(8,128)S(1)}, u32[]{:S(2)}, u32[]{:S(2)}) collective-permute-start(f32[128,128]{1,0:T(8,128)S(1)} %get-tuple-element.37), channel_id=1, source_target_pairs={{2,4},{4,2},{3,5},{5,3},{6,8},{8,6},{7,9},{9,7},{10,12},{12,10},{1... | collective-permute-start | bytes 196616 | tf_op jit(solution)/shard_map/ppermute | solution.py:329
  79.0 0.0 collective-permute-done.5.refs_1_
  79.0 2.5 %collective-permute-done.6.refs_2_ = f32[128,128]{1,0:T(8,128)S(1)} collective-permute-done((f32[128,128]{1,0:T(8,128)S(1)}, f32[128,128]{1,0:T(8,128)S(1)}, u32[]{:S(2)}, u32[]{:S(2)}) %collective-permute-start.6) | collective-permute-done | bytes 65568 | tf_op jit(solution)/shard_map/ppermute | solution.py:329
  81.6 0.2 collective-permute-start.7
  81.8 3.7 %collective-permute-start.8 = (f32[6,32,128]{2,1,0:T(8,128)S(1)}, f32[6,32,128]{2,1,0:T(8,128)S(1)}, u32[]{:S(2)}, u32[]{:S(2)}) collective-permute-start(f32[6,32,128]{2,1,0:T(8,128)S(1)} %get-tuple-element.39), channel_id=1, source_target_pairs={{1,32},{32,1},{3,34},{34,3},{5,36},{36,5},{7,38},{38,7},{9,40},{40... | collective-permute-start | bytes 294920 | tf_op jit(solution)/shard_map/ppermute | solution.py:329
  85.5 0.0 collective-permute-done.7.refs_3_
  85.5 4.8 %collective-permute-done.8.refs_4_ = f32[6,32,128]{2,1,0:T(8,128)S(1)} collective-permute-done((f32[6,32,128]{2,1,0:T(8,128)S(1)}, f32[6,32,128]{2,1,0:T(8,128)S(1)}, u32[]{:S(2)}, u32[]{:S(2)}) %collective-permute-start.8) | collective-permute-done | bytes 98336 | tf_op jit(solution)/shard_map/ppermute | solution.py:329
  90.3 0.0 copy-done.3
  90.3 12.1 %shard_map.69 = f32[4,128,128]{2,1,0:T(8,128)S(1)} custom-call(s32[5]{0:T(128)S(1)} %stack.43.info, f32[4,128,128]{2,1,0:T(8,128)S(1)} %get-tuple-element.35.refs_0_, f32[128,128]{1,0:T(8,128)S(1)} %collective-permute-done.5.refs_1_, f32[128,128]{1,0:T(8,128)S(1)} %collective-permute-done.6.refs_2_, f32[6,32,128]{2,1,0:T(8,128)S(1)} %collective-permute-done.7.refs_3_, ...), custom_call_target="tpu_custom_call" | custom-call | flops 8000000000 | bytes 12000000 | tf_op jit(solution)/shard_map/pallas_call | solution.py:21
  102.4 0.1 collective-permute-start.9
  102.5 7.6 %collective-permute-done.9 = f32[4,128,128]{2,1,0:T(8,128)S(1)} collective-permute-done((f32[4,128,128]{2,1,0:T(8,128)S(1)}, f32[4,128,128]{2,1,0:T(8,128)S(1)}, u32[]{:S(2)}, u32[]{:S(2)}) %collective-permute-start.9) | collective-permute-done | bytes 262176 | tf_op jit(solution)/shard_map/ppermute | solution.py:332
  110.1 1.2 %collective-permute-start.10 = (f32[4,128,256]{2,1,0:T(8,128)S(1)}, f32[4,128,256]{2,1,0:T(8,128)S(1)}, u32[]{:S(2)}, u32[]{:S(2)}) collective-permute-start(f32[4,128,256]{2,1,0:T(8,128)S(1)} %maximum_select_fusion.1), channel_id=1, source_target_pairs={{0,1},{1,0},{2,3},{3,2},{4,5},{5,4},{6,7},{7,6},{8,9},{9,8},{10,11... | collective-permute-start | bytes 1572872 | tf_op jit(solution)/shard_map/ppermute | solution.py:332
  111.3 1.5 %collective-permute-done.10 = f32[4,128,256]{2,1,0:T(8,128)S(1)} collective-permute-done((f32[4,128,256]{2,1,0:T(8,128)S(1)}, f32[4,128,256]{2,1,0:T(8,128)S(1)}, u32[]{:S(2)}, u32[]{:S(2)}) %collective-permute-start.10) | collective-permute-done | bytes 524320 | tf_op jit(solution)/shard_map/ppermute | solution.py:332
  112.9 1.0 maximum_select_fusion
  (5 shorter events, 0.1 us)
Async XLA Ops:
  3.7 1.2 %copy-start.1 = (f32[1,1,4,256,256]{4,3,2,1,0:T(8,128)S(1)}, f32[1,1,4,256,256]{4,3,2,1,0:T(8,128)}, u32[]{:S(2)}) copy-start(f32[1,1,4,256,256]{4,3,2,1,0:T(8,128)} %param.7) | copy-start | bytes 3145732
  9.5 11.4 %collective-permute-start.2 = (f32[5,144,128]{2,1,0:T(8,128)S(1)}, f32[5,144,128]{2,1,0:T(8,128)S(1)}, u32[]{:S(2)}, u32[]{:S(2)}) collective-permute-start(f32[5,144,128]{2,1,0:T(8,128)S(1)} %get-tuple-element.43), channel_id=1, source_target_pairs={{0,3},{1,2},{2,1},{3,0},{4,7},{5,6},{6,5},{7,4},{8,11},{9,10},{10,... | collective-permute-start | bytes 1105928 | tf_op jit(solution)/shard_map/ppermute | solution.py:332
  11.8 16.5 %collective-permute-start.1 = (f32[5,144,128]{2,1,0:T(8,128)S(1)}, f32[5,144,128]{2,1,0:T(8,128)S(1)}, u32[]{:S(2)}, u32[]{:S(2)}) collective-permute-start(f32[5,144,128]{2,1,0:T(8,128)S(1)} %get-tuple-element.44), channel_id=1, source_target_pairs={{0,2},{1,3},{2,0},{3,1},{4,6},{5,7},{6,4},{7,5},{8,10},{9,11},{10,... | collective-permute-start | bytes 1105928 | tf_op jit(solution)/shard_map/ppermute | solution.py:332
  11.8 16.5 %collective-permute-start = (f32[5,144,128]{2,1,0:T(8,128)S(1)}, f32[5,144,128]{2,1,0:T(8,128)S(1)}, u32[]{:S(2)}, u32[]{:S(2)}) collective-permute-start(f32[5,144,128]{2,1,0:T(8,128)S(1)} %get-tuple-element.45), channel_id=1, source_target_pairs={{0,1},{1,0},{2,3},{3,2},{4,5},{5,4},{6,7},{7,6},{8,9},{9,8},{10,11... | collective-permute-start | bytes 1105928 | tf_op jit(solution)/shard_map/ppermute | solution.py:332
  28.4 16.6 %copy-start = (f32[4,5,144,128]{3,2,1,0:T(8,128)}, f32[4,5,144,128]{3,2,1,0:T(8,128)S(1)}, u32[]{:S(2)}) copy-start(f32[4,5,144,128]{3,2,1,0:T(8,128)S(1)} %pad_maximum_fusion.got.refs_4_) | copy-start | bytes 4423684
  29.3 15.7 %collective-permute-start.3 = (f32[448,128]{1,0:T(8,128)S(1)}, f32[448,128]{1,0:T(8,128)S(1)}, u32[]{:S(2)}, u32[]{:S(2)}) collective-permute-start(f32[448,128]{1,0:T(8,128)S(1)} %shard_map.65), channel_id=1, source_target_pairs={{2,4},{4,2},{3,5},{5,3},{6,8},{8,6},{7,9},{9,7},{10,12},{12,10},{1... | collective-permute-start | bytes 688136 | tf_op jit(solution)/shard_map/ppermute | solution.py:329
  46.4 12.0 %collective-permute-start.4 = (f32[512,128]{1,0:T(8,128)S(1)}, f32[512,128]{1,0:T(8,128)S(1)}, u32[]{:S(2)}, u32[]{:S(2)}) collective-permute-start(f32[512,128]{1,0:T(8,128)S(1)} %shard_map.66), channel_id=1, source_target_pairs={{1,32},{32,1},{3,34},{34,3},{5,36},{36,5},{7,38},{38,7},{9,40},{40... | collective-permute-start | bytes 786440 | tf_op jit(solution)/shard_map/ppermute | solution.py:329
  55.6 0.8 copy-start.2
  56.4 0.8 copy-start.4
  58.4 31.9 %copy-start.3 = (bf16[4,2,128,256]{3,2,1,0:T(8,128)(2,1)S(1)}, bf16[4,2,128,256]{3,2,1,0:T(8,128)(2,1)}, u32[]{:S(2)}) copy-start(bf16[4,2,128,256]{3,2,1,0:T(8,128)(2,1)} %copy-done.2) | copy-start | bytes 1572868
  72.8 6.2 %collective-permute-start.5 = (f32[128,128]{1,0:T(8,128)S(1)}, f32[128,128]{1,0:T(8,128)S(1)}, u32[]{:S(2)}, u32[]{:S(2)}) collective-permute-start(f32[128,128]{1,0:T(8,128)S(1)} %get-tuple-element.36), channel_id=1, source_target_pairs={{0,2},{1,3},{2,0},{3,1},{4,6},{5,7},{6,4},{7,5},{8,10},{9,11},{10,... | collective-permute-start | bytes 196616 | tf_op jit(solution)/shard_map/ppermute | solution.py:332
  72.8 8.8 %collective-permute-start.6 = (f32[128,128]{1,0:T(8,128)S(1)}, f32[128,128]{1,0:T(8,128)S(1)}, u32[]{:S(2)}, u32[]{:S(2)}) collective-permute-start(f32[128,128]{1,0:T(8,128)S(1)} %get-tuple-element.37), channel_id=1, source_target_pairs={{2,4},{4,2},{3,5},{5,3},{6,8},{8,6},{7,9},{9,7},{10,12},{12,10},{1... | collective-permute-start | bytes 196616 | tf_op jit(solution)/shard_map/ppermute | solution.py:329
  81.6 3.9 %collective-permute-start.7 = (f32[6,32,128]{2,1,0:T(8,128)S(1)}, f32[6,32,128]{2,1,0:T(8,128)S(1)}, u32[]{:S(2)}, u32[]{:S(2)}) collective-permute-start(f32[6,32,128]{2,1,0:T(8,128)S(1)} %broadcast_select_fusion.1), channel_id=1, source_target_pairs={{0,1},{1,0},{2,3},{3,2},{4,5},{5,4},{6,7},{7,6},{8,9},{9,8},{10,11... | collective-permute-start | bytes 294920 | tf_op jit(solution)/shard_map/ppermute | solution.py:332
  81.8 8.5 %collective-permute-start.8 = (f32[6,32,128]{2,1,0:T(8,128)S(1)}, f32[6,32,128]{2,1,0:T(8,128)S(1)}, u32[]{:S(2)}, u32[]{:S(2)}) collective-permute-start(f32[6,32,128]{2,1,0:T(8,128)S(1)} %get-tuple-element.39), channel_id=1, source_target_pairs={{1,32},{32,1},{3,34},{34,3},{5,36},{36,5},{7,38},{38,7},{9,40},{40... | collective-permute-start | bytes 294920 | tf_op jit(solution)/shard_map/ppermute | solution.py:329
  102.4 7.7 %collective-permute-start.9 = (f32[4,128,128]{2,1,0:T(8,128)S(1)}, f32[4,128,128]{2,1,0:T(8,128)S(1)}, u32[]{:S(2)}, u32[]{:S(2)}) collective-permute-start(f32[4,128,128]{2,1,0:T(8,128)S(1)} %shard_map.69), channel_id=1, source_target_pairs={{0,2},{1,3},{2,0},{3,1},{4,6},{5,7},{6,4},{7,5},{8,10},{9,11},{10,... | collective-permute-start | bytes 786440 | tf_op jit(solution)/shard_map/ppermute | solution.py:332
  110.1 2.8 %collective-permute-start.10 = (f32[4,128,256]{2,1,0:T(8,128)S(1)}, f32[4,128,256]{2,1,0:T(8,128)S(1)}, u32[]{:S(2)}, u32[]{:S(2)}) collective-permute-start(f32[4,128,256]{2,1,0:T(8,128)S(1)} %maximum_select_fusion.1), channel_id=1, source_target_pairs={{0,1},{1,0},{2,3},{3,2},{4,5},{5,4},{6,7},{7,6},{8,9},{9,8},{10,11... | collective-permute-start | bytes 1572872 | tf_op jit(solution)/shard_map/ppermute | solution.py:332

commit v2 on v0

v2 whole, which is shorter than its diff:
```python
import functools

import jax
import jax.numpy as jnp
from jax import lax
from jax.experimental import pallas as pl
from jax.experimental.pallas import tpu as pltpu
from jax.sharding import PartitionSpec as P

GX = 8
ITERS = 2
HALF = 15
F32 = jnp.float32
BF16 = jnp.bfloat16
VMEM = pltpu.VMEM
SMEM = pltpu.SMEM


def call(body, outs, scratch, scalars, *args, flops=0):
    specs = [pl.BlockSpec(memory_space=SMEM)] * len(scalars)
    specs += [pl.BlockSpec(memory_space=VMEM)] * len(args)
    moved = sum(a.size * a.dtype.itemsize for a in args)
    return pl.pallas_call(
        body,
        out_shape=outs,
        in_specs=specs,
        out_specs=jax.tree.map(lambda _: pl.BlockSpec(memory_space=VMEM), outs),
        scratch_shapes=scratch,
        compiler_params=pltpu.CompilerParams(vmem_limit_bytes=48 * 1024 * 1024),
        cost_estimate=pl.CostEstimate(flops=flops, bytes_accessed=moved, transcendentals=0),
    )(*scalars, *args)


def shape(*dims, dtype=F32):
    return jax.ShapeDtypeStruct(dims, dtype)


def lanes(rows, width=128):
    return lax.broadcasted_iota(jnp.int32, (rows, width), 1)


def turn(x, amount):
    if isinstance(amount, int):
        amount = amount % x.shape[-1]
        if amount == 0:
            return x
    return pltpu.roll(x, amount, axis=x.ndim - 1)


def packed(pieces, first, width):
    rows = pieces[0].shape[0]
    lane = lanes(rows)
    out = jnp.zeros((rows, 128), F32)
    for n, piece in enumerate(pieces):
        inside = (lane >= n * width) & (lane < (n + 1) * width)
        out = jnp.where(inside, turn(piece, n * width - first), out)
    return out


def right_half(rows):
    return lax.rem(lanes(rows), 32) < 16


def shared(pieces, qx):
    rows = pieces[0].shape[0]
    lane = lanes(rows)
    out = jnp.zeros((rows, 128), F32)
    for z, piece in enumerate(pieces):
        mine = jnp.where(qx == 0, turn(piece, 32 * z), turn(piece, 32 * z + 32))
        out = jnp.where((lane >= 32 * z) & (lane < 32 * z + 32), mine, out)
    return jnp.where(right_half(rows) == (qx == 0), out, 0.0)


def split(x):
    high = x.astype(BF16)
    return high, (x - high.astype(F32)).astype(BF16)


def dot3(stacked, high, low):
    rows = stacked.shape[0] // 2
    both = jnp.dot(stacked, high, preferred_element_type=F32)
    rest = jnp.dot(stacked[:rows], low, preferred_element_type=F32)
    return both[:rows] + (both[rows:] + rest)


def send_kernel(info, variants, rec, table, *refs):
    sent, taps = refs[:4], refs[4]
    view, row, col, last = info[0], info[5], info[6], info[7]
    sums = jnp.sum(table[...], axis=-1, keepdims=True)
    taps[...] = table[...] / sums
    for s in range(4):
        q = jnp.bitwise_xor(view, s)
        qx, qy = lax.shift_right_logical(q, 1), jnp.bitwise_and(q, 1)
        rows = pl.ds(pl.multiple_of(112 * qy, 16), 144)
        here = pl.ds(pl.multiple_of(128 * qx, 128), 128)
        there = pl.ds(pl.multiple_of(128 - 128 * qx, 128), 128)
        for z in range(4):
            sent[s][144 * z : 144 * z + 144] = rec[z, rows, here]
        sent[s][576:720] = shared([rec[z, rows, there] for z in range(4)], qx)
        sent[s][720:736] = jnp.zeros((16, 128), F32)
        for n in range(4):
            x = jnp.clip(col + (2 * qx - 1) * (n % 2), 0, GX - 1)
            y = jnp.clip(row + (2 * qy - 1) * (n // 2), 0, last)
            sent[s][720 + 3 * n : 723 + 3 * n, 0:31] = taps[variants[y * GX + x]]


def start_kernel(info, first, main, inside, edge):
    for q in range(4):
        qx, qy = q // 2, q % 2

        @pl.when(info[0] == q)
        def _():
            span = slice(96 * qy, 96 * qy + 160)
            own = [first[z, span, 128 * qx : 128 * qx + 128] for z in range(4)]
            for z in range(4):
                main[z] = own[z]
            beside = [first[z, span, 128 - 128 * qx : 256 - 128 * qx] for z in range(4)]
            inside[...] = packed(beside, 96 * qx, 32)
            edge[...] = packed(own, 96 * qx, 32)


def pack_cols_kernel(info, *refs):
    got, out = refs[:4], refs[4]
    qx = info[1]
    for h in range(2):
        cols = []
        for s in (2 * h, 2 * h + 1):
            block = got[s ^ 2]
            cols.append(shared([block[144 * z : 144 * z + 144] for z in range(4)], qx))
        other = jnp.where(qx == 0, turn(cols[1], 16), turn(cols[1], -16))
        out[h * 144 : h * 144 + 144] = cols[0] + other


def both_sides(inner, cols, odd, qx):
    rows = inner.shape[0]
    if odd:
        cols = jnp.where(qx == 0, turn(cols, 16), turn(cols, -16))
    return jnp.where(right_half(rows) == (qx == 0), inner, cols)


def pack_rows_kernel(info, *refs):
    got, cols, out = refs[:4], refs[4], refs[5]
    at = pl.multiple_of(128 * info[2], 16)
    for s in range(4):
        o = s ^ 1
        for z in range(4):
            n = 4 * s + z
            out[n * 16 : n * 16 + 16] = got[o][pl.ds(144 * z + at, 16)]
        inner = got[o][pl.ds(576 + at, 16)]
        outer = cols[pl.ds((o // 2) * 144 + at, 16)]
        out[256 + 16 * s : 272 + 16 * s] = both_sides(inner, outer, o % 2, info[1])


def start_rows_kernel(info, main, inside, cols, out):
    at = pl.multiple_of(128 * info[2], 32)
    for z in range(4):
        out[32 * z : 32 * z + 32] = main[z, pl.ds(at, 32)]
    out[128:160] = inside[pl.ds(at, 32)]
    out[160:192] = cols[pl.ds(at, 32)]


def toeplitz(base, shift):
    return pltpu.roll(base, shift % 256, axis=1, stride=1, stride_axis=0)


def matrices_kernel(info, one, two, xh, xl, ah, al, y, t, zm, zs):
    qx, qy = info[1], info[2]
    for s, table in enumerate((one, two)):
        fwd = table[720:736]
        flip = lax.broadcasted_iota(jnp.int32, (128, 128), 0) + lanes(128) == 30
        rev = jnp.dot(fwd, flip.astype(F32), precision=lax.Precision.HIGHEST)
        zero = jnp.zeros((16, 128), F32)
        fwd = jnp.concatenate([fwd, zero], 1)
        rev = jnp.concatenate([rev, zero], 1)

        def wide(which, tile, axis, rows):
            return jnp.broadcast_to(which[3 * tile + axis : 3 * tile + axis + 1], (rows, 256))

        lane = lanes(256)
        right, left = lane < 16, (lane >= 16) & (lane < 32)
        for g in range(2):
            near_t = toeplitz(wide(rev, 2 * g, 0, 256), -HALF)
            far_t = toeplitz(wide(rev, 2 * g + 1, 0, 256), -HALF)
            rhs = jnp.where(qx == 1, far_t[:, 128:], near_t[:, 128:])
            lhs = jnp.where(qx == 0, far_t[:, 128:], near_t[:, 128:])
            side = jnp.where(right, rhs, jnp.where(left, turn(lhs, 32), 0.0))
            xh[s, g], xl[s, g] = split(jnp.concatenate([near_t[:, :128], side], 1))
        row = lax.broadcasted_iota(jnp.int32, (256, 256), 0)
        far_row = (row >= 128) & ((row < 192) == (qx == 1))
        base = jnp.where(far_row, wide(fwd, 1, 0, 256), wide(fwd, 0, 0, 256))
        adj = toeplitz(base, -HALF)[:, :128]
        adj = jnp.concatenate(
            [adj[:144], adj[240:], jnp.zeros((96, 128), F32)], 0
        )
        ah[s], al[s] = split(adj)
        for g in range(2):
            row = lax.broadcasted_iota(jnp.int32, (160, 256), 0)
            other = jnp.where(qy == 0, row, 159 - row) < 16
            base = jnp.where(other, wide(fwd, 2 + g, 1, 160), wide(fwd, g, 1, 160))
            y[s, g, :160], y[s, g, 160:] = split(toeplitz(base, 1))
            wider = lanes(128, 256)
            other = jnp.where(qy == 0, wider, 159 - wider) < 16
            near_t = toeplitz(wide(rev, g, 1, 128), 1)
            far_t = toeplitz(wide(rev, 2 + g, 1, 128), 1)
            t[s, g, :128], t[s, g, 128:] = split(jnp.where(other, far_t, near_t))
        lane = lanes(1)
        plane = lax.div(lane, 32)
        far = right_half(1) == (qx == 1)
        for g in range(2):
            near_w = [
                jnp.broadcast_to(fwd[6 * g + 2 : 6 * g + 3, c : c + 1], (1, 128))
                for c in range(12, 19)
            ]
            far_w = [
                jnp.broadcast_to(fwd[6 * g + 5 : 6 * g + 6, c : c + 1], (1, 128))
                for c in range(12, 19)
            ]
            for d in range(7):
                zm[s, g, d : d + 1] = near_w[d]
                inside = (plane + (d - 3) >= 0) & (plane + (d - 3) < 4)
                for adjoint in range(2):
                    c = 6 - d if adjoint else d
                    value = jnp.where(far, far_w[c], near_w[c])
                    at = 8 * adjoint + d
                    zs[s, g, at : at + 1] = jnp.where(inside, value, 0.0)


def sided(left, right, width, n, rows):
    lane = lanes(rows)
    out = jnp.where(lane < width, turn(right, -n * width), 0.0)
    return jnp.where(lane >= 128 - width, turn(left, 128 - width - n * width), out)


def spread(region, e, qx):
    left = jnp.where(qx == 0, region[5], region[4])
    right = jnp.where(qx == 0, region[4], region[5])
    for z in range(4):
        e[0, z, :, :128], e[1, z, :, :128] = split(region[z])
        e[0, z, :, 128:], e[1, z, :, 128:] = split(sided(left, right, 32, z, 192))


def region_kernel(info, main, inside, cols, rows_in, e, region):
    own = pl.multiple_of(32 * (1 - info[2]), 32)
    other = pl.multiple_of(160 * info[2], 32)
    for z in range(4):
        region[z, pl.ds(own, 160)] = main[z]
        region[z, pl.ds(other, 32)] = rows_in[32 * z : 32 * z + 32]
    region[4, pl.ds(own, 160)] = inside[...]
    region[5, pl.ds(own, 160)] = cols[...]
    region[4, pl.ds(other, 32)] = rows_in[128:160]
    region[5, pl.ds(other, 32)] = rows_in[160:192]
    spread(region, e, info[1])


def mix_planes(planes, side, main_w, side_w, adjoint):
    out = []
    for z in range(4):
        order = [3 + z - k if adjoint else 3 + k - z for k in range(4)]
        out.append(sum(main_w[order[k]] * planes[k] for k in range(4)))
    out.append(sum(side_w[d] * turn(side, -32 * (d - 3)) for d in range(7)))
    return out


def forward(s, qy, e, mats, p, put):
    xh, xl, _, _, y, _, zm, zs = mats
    own = pl.multiple_of(32 * (1 - qy), 32)
    other = pl.multiple_of(160 * qy, 32)
    for g, at, count in ((0, own, 160), (1, other, 32)):
        planes, side = [], None
        for z in range(4):
            here = jnp.concatenate([e[0, z, pl.ds(at, count)], e[1, z, pl.ds(at, count)]], 0)
            value = dot3(here, xh[s, g], xl[s, g])
            planes.append(value[:, :128])
            moved = turn(value[:, 128:], 32 * z)
            side = moved if side is None else side + moved
        main_w = [zm[s, g, d : d + 1] for d in range(7)]
        side_w = [zs[s, g, d : d + 1] for d in range(7)]
        for z, value in enumerate(mix_planes(planes, side, main_w, side_w, False)):
            here = slice(128 * z, 128 * z + 128)
            p[0, pl.ds(at, count), here], p[1, pl.ds(at, count), here] = split(value)
    for a in (0, 256):
        put(slice(a, a + 256), dot3(y[s, 0], p[0, :, a : a + 256], p[1, :, a : a + 256]))
    high, low = p[0, :, 512:], p[1, :, 512:]
    near, edge = dot3(y[s, 0], high, low), dot3(y[s, 1], high, low)
    return near, edge


def adjoint(s, mats, r, total):
    _, _, ah, al, _, t, zm, zs = mats
    planes = []
    for a in (0, 256):
        pair = dot3(t[s, 0], r[0, :, a : a + 256], r[1, :, a : a + 256])
        planes += [pair[:, :128], pair[:, 128:]]
    high, low = r[0, :, 512:], r[1, :, 512:]
    return planes, dot3(t[s, 0], high, low), dot3(t[s, 1], high, low)


def finish(s, mats, planes, side, total):
    _, _, ah, al, _, _, zm, zs = mats
    main_w = [zm[s, 0, d : d + 1] for d in range(7)]
    side_w = [zs[s, 0, 8 + d : 9 + d] for d in range(7)]
    *planes, side = mix_planes(planes, side, main_w, side_w, True)
    for z in range(4):
        both = jnp.concatenate([planes[z], turn(side, -32 * z)], 1)
        correction = dot3(jnp.concatenate(split(both), 0), ah[s], al[s])
        total[z] += jnp.log(correction)


def far_mask(rows, qx):
    return right_half(rows) == (qx == 1)


def clear(ref, first):
    ref[:, first:] = jnp.zeros((2, 256 - first, 640), BF16)


def forward_kernel(info, e, *refs):
    mats, refs = refs[:8], refs[8:]
    out, p = refs
    clear(p, 192)
    far = far_mask(160, info[1])

    def body(s, carry):
        def put(where, value):
            out[s, :, where] = value

        near, edge = forward(s, info[2], e, mats, p, put)
        out[s, :, 512:] = jnp.where(far, edge, near)
        return carry

    lax.fori_loop(0, 2, body, 0)


def row_masks(info):
    row = lax.broadcasted_iota(jnp.int32, (160, 128), 0)
    past = jnp.where(info[2] == 0, row, 159 - row) < 16
    inside = (info[4] > 0) | ~past
    side = inside & ((info[3] > 0) | ~far_mask(160, info[1]))
    return inside, side


def take_ratio(s, rec, r, masks, where, blurred):
    wide = jnp.concatenate([masks[0], masks[0]], 1) if blurred.shape[1] == 256 else masks[1]
    ratio = jnp.where(wide, rec[s, :, where] / blurred, 0.0)
    r[0, :160, where], r[1, :160, where] = split(ratio)


def update(first, main, at, total, out, edges, qx):
    new = []
    for z in range(4):
        new.append(main[z, at] * jnp.exp(total[z] / 4))
        out[z] = new[z]
    if first:
        low, high = packed(new, 0, 32), packed(new, 96, 32)
        edges[0][...] = jnp.where(qx == 0, high, low)
        edges[1][...] = jnp.where(qx == 0, low, high)


def adjoint_kernel(info, main, cols, rows_in, *refs):
    got, blurs, refs = refs[:4], refs[4:6], refs[6:]
    groups, refs = (refs[:8], refs[8:16]), refs[16:]
    out, near_edge, far_edge, rec, r, total = refs
    qx, qy = info[1], info[2]
    in_tile = pl.multiple_of(16 * (1 - qy), 16)
    out_tile = pl.multiple_of(144 * qy, 16)
    for s in range(4):
        for z in range(4):
            here = slice(128 * z, 128 * z + 128)
            rec[s, pl.ds(in_tile, 144), here] = got[s][144 * z : 144 * z + 144]
            n = 4 * s + z
            rec[s, pl.ds(out_tile, 16), here] = rows_in[n * 16 : n * 16 + 16]
        outer = cols[(s // 2) * 144 : (s // 2) * 144 + 144]
        rec[s, pl.ds(in_tile, 144), 512:] = both_sides(got[s][576:720], outer, s % 2, qx)
        rec[s, pl.ds(out_tile, 16), 512:] = rows_in[256 + 16 * s : 272 + 16 * s]
    clear(r, 160)
    total[...] = jnp.zeros_like(total)
    masks = row_masks(info)
    far = far_mask(128, qx)
    for pair in range(2):
        mats, blur = groups[pair], blurs[pair]

        def body(s, carry):
            for a, b in ((0, 256), (256, 512), (512, 640)):
                take_ratio(2 * pair + s, rec, r, masks, slice(a, b), blur[s, :, a:b])
            planes, near, edge = adjoint(s, mats, r, total)
            finish(s, mats, planes, jnp.where(far, edge, near), total)
            return carry

        lax.fori_loop(0, 2, body, 0)
    at = pl.ds(pl.multiple_of(32 * qy, 32), 128)
    update(True, main, at, total, out, (near_edge, far_edge), qx)


def step_kernel(info, main, inside, beyond, rows_in, rows_out, rec, *refs):
    groups, refs = (refs[:8], refs[8:16]), refs[16:]
    out, region, e, p, r, total = refs
    qx, qy = info[1], info[2]
    for z in range(4):
        region[z, 32:160] = main[z]
    region[4, 32:160] = inside[...]
    region[5, 32:160] = beyond[...]
    for n in range(6):
        region[n, pl.ds(pl.multiple_of(160 * (1 - qy), 32), 32)] = rows_in[n]
        region[n, pl.ds(pl.multiple_of(160 * qy, 32), 32)] = rows_out[n]
    spread(region, e, qx)
    clear(p, 192)
    clear(r, 160)
    total[...] = jnp.zeros_like(total)
    masks = row_masks(info)
    far160, far128 = far_mask(160, qx), far_mask(128, qx)
    for pair in range(2):
        mats = groups[pair]

        def body(s, carry):
            slot = 2 * pair + s

            def put(where, value):
                take_ratio(slot, rec, r, masks, where, value)

            near, edge = forward(s, qy, e, mats, p, put)
            put(slice(512, 640), jnp.where(far160, edge, near))
            planes, near, edge = adjoint(s, mats, r, total)
            finish(s, mats, planes, jnp.where(far128, edge, near), total)
            return carry

        lax.fori_loop(0, 2, body, 0)
    update(False, main, slice(0, 128), total, out, None, qx)


def per_device(initial, recorded, tap_table, variants):
    tile = lax.axis_index("tile")
    view = lax.axis_index("view")
    count_tiles = lax.axis_size("tile")
    grid_rows = count_tiles // GX
    tile_row, tile_col = tile // GX, tile % GX
    qx, qy = view // 2, view % 2
    has_x = jnp.where(qx == 0, tile_col > 0, tile_col < GX - 1).astype(jnp.int32)
    has_y = jnp.where(qy == 0, tile_row > 0, tile_row < grid_rows - 1).astype(jnp.int32)
    info = jnp.stack([view, qx, qy, has_x, has_y, tile_row, tile_col, grid_rows - 1])

    def route(x, pairs):
        return lax.ppermute(x, ("tile", "view"), pairs)

    def over_view(x, flip):
        return lax.ppermute(x, "view", [(i, i ^ flip) for i in range(4)])

    x_pairs, y_pairs = [], []
    for t in range(count_tiles):
        for v in range(4):
            if v // 2 and t % GX < GX - 1:
                x_pairs += [(4 * t + v, 4 * (t + 1) + v - 2), (4 * (t + 1) + v - 2, 4 * t + v)]
            if v % 2 and t + GX < count_tiles:
                y_pairs += [(4 * t + v, 4 * (t + GX) + v - 1), (4 * (t + GX) + v - 1, 4 * t + v)]

    sent = call(
        send_kernel,
        (shape(736, 128),) * 4,
        [VMEM((8, 3, 31), F32)],
        (info, variants[0]),
        recorded[0, 0],
        tap_table[0],
    )
    got = [sent[0]] + [over_view(sent[s], s) for s in (1, 2, 3)]
    main, inside, edge = call(
        start_kernel,
        (shape(4, 160, 128), shape(160, 128), shape(160, 128)),
        [],
        (info,),
        initial[0],
    )
    start_cols = route(edge, x_pairs)
    start_rows = route(
        call(start_rows_kernel, shape(192, 128), [], (info,), main, inside, start_cols), y_pairs
    )
    e = call(
        region_kernel,
        shape(2, 4, 192, 256, dtype=BF16),
        [VMEM((6, 192, 128), F32)],
        (info,),
        main,
        inside,
        start_cols,
        start_rows,
    )
    mats, blurs = [], []
    for pair in (got[:2], got[2:]):
        mats.append(
            call(
                matrices_kernel,
                (
                    shape(2, 2, 256, 256, dtype=BF16),
                    shape(2, 2, 256, 256, dtype=BF16),
                    shape(2, 256, 128, dtype=BF16),
                    shape(2, 256, 128, dtype=BF16),
                    shape(2, 2, 320, 256, dtype=BF16),
                    shape(2, 2, 256, 256, dtype=BF16),
                    shape(2, 2, 8, 128),
                    shape(2, 2, 16, 128),
                ),
                [],
                (info,),
                *pair,
                flops=1_000_000_000,
            )
        )
        blurs.append(
            call(
                forward_kernel,
                shape(2, 160, 640),
                [VMEM((2, 256, 640), BF16)],
                (info,),
                e,
                *mats[-1],
                flops=2_000_000_000,
            )
        )
    cols = route(call(pack_cols_kernel, shape(288, 128), [], (info,), *got), x_pairs)
    rows = route(call(pack_rows_kernel, shape(320, 128), [], (info,), *got, cols), y_pairs)
    quad = shape(4, 128, 128)
    flat = [*mats[0], *mats[1]]
    estimate, near_edge, far_edge, rec = call(
        adjoint_kernel,
        (quad, shape(128, 128), shape(128, 128), shape(4, 160, 640)),
        [VMEM((2, 256, 640), BF16), VMEM((4, 128, 128), F32)],
        (info,),
        main,
        cols,
        rows,
        *got,
        *blurs,
        *flat,
        flops=4_000_000_000,
    )
    for step in range(1, ITERS):
        inside = over_view(near_edge, 2)
        beyond = route(far_edge, x_pairs)
        whole = jnp.concatenate([estimate, inside[None], beyond[None]])
        low, high = whole[:, :32], whole[:, 96:]
        rows_in = over_view(jnp.where(qy == 0, high, low), 1)
        rows_out = route(jnp.where(qy == 0, low, high), y_pairs)
        estimate = call(
            step_kernel,
            quad,
            [
                VMEM((6, 192, 128), F32),
                VMEM((2, 4, 192, 256), BF16),
                VMEM((2, 256, 640), BF16),
                VMEM((2, 256, 640), BF16),
                VMEM((4, 128, 128), F32),
            ],
            (info,),
            estimate,
            inside,
            beyond,
            rows_in,
            rows_out,
            rec,
            *flat,
            flops=8_000_000_000,
        )
    across = over_view(estimate, 2)
    wide = jnp.where(
        qx == 0,
        jnp.concatenate([estimate, across], 2),
        jnp.concatenate([across, estimate], 2),
    )
    down = over_view(wide, 1)
    return jnp.where(
        qy == 0, jnp.concatenate([wide, down], 1), jnp.concatenate([down, wide], 1)
    )[None]


def solution(mesh):
    return jax.shard_map(
        per_device,
        mesh=mesh,
        in_specs=(
            P("tile", None, None, None),
            P("view", "tile", None, None, None),
            P("view", None, None, None),
            P("view", None),
        ),
        out_specs=P("tile", None, None, None),
        check_vma=False,
    )
```

time: 548 us -> 97 us (0.18); the launches traced: 538 us -> 96.7 us
  matrix products: 167 us -> 0 us
  waiting for transfers between devices: 181 us -> 25.9 us
  other arithmetic: 109 us -> 1.12 us
  Pallas kernels: 0 us -> 30.5 us
  starting transfers between devices: 61.5 us -> 35.3 us
  between operations: 15.9 us -> 0.28 us
    dot_general x280 -> x0, matrix products: 167 us -> none  [the longest x155 136 us: weight_map(): return jnp.dot(inner, col_hot.T, precision=lax.Precision.HIGHEST)]
    psum x2 -> x0, waiting for transfers between devices: 109 us -> none  [per_device(): summed = lax.psum(logged, 'view')]
    add x8 -> x0, other arithmetic: 53.6 us -> none  [the longest x2 33.1 us: blur_cols(): result = result + weights[None] * padded[:, :, offset:offset + count]]
    ppermute x16 -> x13, waiting for transfers between devices: 71.9 us -> 25.9 us  [the longest x6 16.4 us: route(): return lax.ppermute(x, ('tile', 'view'), pairs)]
    log x2 -> x0, other arithmetic: 31.2 us -> none  [per_device(): logged = jnp.log(correction)]
    pallas_call x0 -> x12, Pallas kernels: none -> 30.5 us  [call(): pl.pallas_call(body, out_shape=outs, in_specs=specs, out_specs=jax.tree.m...]
    ppermute x16 -> x13, starting transfers between devices: 61.4 us -> 35.3 us  [the longest x6 31.3 us: route(): return lax.ppermute(x, ('tile', 'view'), pairs)]
    div x2 -> x0, other arithmetic: 16.4 us -> none  [per_device(): ratio = observed / blurred]
  transfers between devices with their start and end apart: 18 -> 13, of which waited for: 11 -> 8; matrix products, arithmetic and copies ran while one was open for 32% -> 0% of each run, Pallas kernels for 0% -> 12%
where the time goes in v2:
time: 97 us; the launch traced here: 96.7 us
  starting transfers between devices  35.3 us (36%)
  Pallas kernels  30.5 us (31%)
  waiting for transfers between devices  25.9 us (27%)
  local copies, waits for them, and re-layouts  3.59 us (4%)
  other arithmetic  1.12 us (1%)
    ppermute x6, starting transfers between devices, route(): return lax.ppermute(x, ('tile', 'view'), pairs)  31.3 us
    pallas_call x12, Pallas kernels, call(): pl.pallas_call(body, out_shape=outs, in_specs=specs, out_specs=jax.tree.m...  30.5 us
    ppermute x6, waiting for transfers between devices, route(): return lax.ppermute(x, ('tile', 'view'), pairs)  16.4 us
    ppermute x7, waiting for transfers between devices, over_view(): return lax.ppermute(x, 'view', [(i, i ^ flip) for i in range(4)])  9.51 us
    ppermute x7, starting transfers between devices, over_view(): return lax.ppermute(x, 'view', [(i, i ^ flip) for i in range(4)])  3.99 us
    unnamed x23, local copies, waits for them, and re-layouts  3.51 us
  transfers between devices with their start and end apart: 13, of which 8 were waited for; matrix products, arithmetic and copies ran while one was open for 0% of the time, Pallas kernels for 12%

profile of v2, /device:TPU:13, one launch (start us, length us, event | category | flops | bytes accessed | tf_op | source)
XLA Modules:
  0.0 96.7 jit_solution(7746053403114028993)
XLA Ops:
  0.0 0.7 copy.7
  0.7 0.1 stack.39.info
  0.8 0.0 copy-start
  0.8 1.2 %copy-done = f32[1,1,4,256,256]{4,3,2,1,0:T(8,128)S(1)} copy-done((f32[1,1,4,256,256]{4,3,2,1,0:T(8,128)S(1)}, f32[1,1,4,256,256]{4,3,2,1,0:T(8,128)}, u32[]{:S(2)}) %copy-start) | copy-done | bytes 1048600
  2.0 0.0 copy-start.2
  2.0 0.7 copy-done.2
  2.7 0.0 copy-start.1
  2.7 1.1 %shard_map.47 = (f32[736,128]{1,0:T(8,128)S(1)}, f32[736,128]{1,0:T(8,128)S(1)}, f32[736,128]{1,0:T(8,128)S(1)}, f32[736,128]{1,0:T(8,128)S(1)}) custom-call(s32[8]{0:T(128)S(1)} %stack.39.info, s32[64]{0:T(128)S(1)} %bitcast.22, f32[4,256,256]{2,1,0:T(8,128)S(1)} %bitcast.17, f32[8,3,31]{2,1,0:T(4,128)S(1)} %bitcast.19), custom_call_target="tpu_custom_call" | custom-call | bytes 1051552 | tf_op jit(solution)/shard_map/pallas_call | solution.py:23
  3.8 0.8 collective-permute-start
  4.6 1.7 %collective-permute-start.1 = (f32[736,128]{1,0:T(8,128)S(1)}, f32[736,128]{1,0:T(8,128)S(1)}, u32[]{:S(2)}, u32[]{:S(2)}) collective-permute-start(f32[736,128]{1,0:T(8,128)S(1)} %get-tuple-element.35), channel_id=1, source_target_pairs={{0,2},{1,3},{2,0},{3,1},{4,6},{5,7},{6,4},{7,5},{8,10},{9,11},{10,... | collective-permute-start | bytes 1130504 | tf_op jit(solution)/shard_map/ppermute | solution.py:445
  6.2 0.1 collective-permute-start.2
  6.3 0.0 copy-done.1
  6.3 0.8 shard_map.46
  7.1 7.4 %collective-permute-start.5 = (f32[160,128]{1,0:T(8,128)S(1)}, f32[160,128]{1,0:T(8,128)S(1)}, u32[]{:S(2)}, u32[]{:S(2)}) collective-permute-start(f32[160,128]{1,0:T(8,128)S(1)} %get-tuple-element.38), channel_id=1, source_target_pairs={{2,4},{4,2},{3,5},{5,3},{6,8},{8,6},{7,9},{9,7},{10,12},{12,10},{1... | collective-permute-start | bytes 245768 | tf_op jit(solution)/shard_map/ppermute | solution.py:442
  14.5 3.5 %collective-permute-done.5.cols = f32[160,128]{1,0:T(8,128)S(1)} collective-permute-done((f32[160,128]{1,0:T(8,128)S(1)}, f32[160,128]{1,0:T(8,128)S(1)}, u32[]{:S(2)}, u32[]{:S(2)}) %collective-permute-start.5) | collective-permute-done | bytes 81952 | tf_op jit(solution)/shard_map/ppermute | solution.py:442
  17.9 0.6 shard_map.50
  18.5 4.0 %collective-permute-start.6 = (f32[192,128]{1,0:T(8,128)S(1)}, f32[192,128]{1,0:T(8,128)S(1)}, u32[]{:S(2)}, u32[]{:S(2)}) collective-permute-start(f32[192,128]{1,0:T(8,128)S(1)} %shard_map.50), channel_id=1, source_target_pairs={{1,32},{32,1},{3,34},{34,3},{5,36},{36,5},{7,38},{38,7},{9,40},{40... | collective-permute-start | bytes 294920 | tf_op jit(solution)/shard_map/ppermute | solution.py:442
  22.5 3.4 %collective-permute-done.6.rows_in = f32[192,128]{1,0:T(8,128)S(1)} collective-permute-done((f32[192,128]{1,0:T(8,128)S(1)}, f32[192,128]{1,0:T(8,128)S(1)}, u32[]{:S(2)}, u32[]{:S(2)}) %collective-permute-start.6) | collective-permute-done | bytes 98336 | tf_op jit(solution)/shard_map/ppermute | solution.py:442
  25.9 0.8 shard_map.51.e
  26.8 0.0 collective-permute-done.refs_1_.two
  26.8 0.0 collective-permute-done.1.refs_2_.one
  26.8 0.0 collective-permute-done.2.refs_3_.two
  26.8 1.3 %shard_map.48 = f32[288,128]{1,0:T(8,128)S(1)} custom-call(s32[8]{0:T(128)S(1)} %stack.39.info, f32[736,128]{1,0:T(8,128)S(1)} %get-tuple-element.33.refs_0_.one, f32[736,128]{1,0:T(8,128)S(1)} %collective-permute-done.refs_1_.two, f32[736,128]{1,0:T(8,128)S(1)} %collective-permute-done.1.refs_2_.one, f32[736,128]{1,0:T(8,128)S(1)} %collective-permute-done.2.refs_3_.two), custom_call_target="tpu_custom_call" | custom-call | bytes 1507328 | tf_op jit(solution)/shard_map/pallas_call | solution.py:23
  28.1 6.7 %collective-permute-start.3 = (f32[288,128]{1,0:T(8,128)S(1)}, f32[288,128]{1,0:T(8,128)S(1)}, u32[]{:S(2)}, u32[]{:S(2)}) collective-permute-start(f32[288,128]{1,0:T(8,128)S(1)} %shard_map.48), channel_id=1, source_target_pairs={{2,4},{4,2},{3,5},{5,3},{6,8},{8,6},{7,9},{9,7},{10,12},{12,10},{1... | collective-permute-start | bytes 442376 | tf_op jit(solution)/shard_map/ppermute | solution.py:442
  34.8 1.7 %shard_map.54 = (bf16[2,2,256,256]{3,2,1,0:T(8,128)(2,1)S(1)}, bf16[2,2,256,256]{3,2,1,0:T(8,128)(2,1)S(1)}, bf16[2,256,128]{2,1,0:T(8,128)(2,1)S(1)}, bf16[2,25...) custom-call(s32[8]{0:T(128)S(1)} %stack.39.info, ...), custom_call_target="tpu_custom_call" | custom-call | flops 1000000000 | bytes 753664 | tf_op jit(solution)/shard_map/pallas_call | solution.py:23
  36.5 0.0 copy-start.5
  36.5 0.0 copy-start.9
  36.5 1.7 %shard_map.52 = (bf16[2,2,256,256]{3,2,1,0:T(8,128)(2,1)S(1)}, bf16[2,2,256,256]{3,2,1,0:T(8,128)(2,1)S(1)}, bf16[2,256,128]{2,1,0:T(8,128)(2,1)S(1)}, bf16[2,25...) custom-call(s32[8]{0:T(128)S(1)} %stack.39.info, ...), custom_call_target="tpu_custom_call" | custom-call | flops 1000000000 | bytes 753664 | tf_op jit(solution)/shard_map/pallas_call | solution.py:23
  38.2 0.0 copy-start.7
  38.2 0.0 copy-done.5
  38.2 0.0 copy-done.9
  38.2 2.8 %shard_map.55.refs_5_ = f32[2,160,640]{2,1,0:T(8,128)S(1)} custom-call(s32[8]{0:T(128)S(1)} %stack.39.info, bf16[2,4,192,256]{3,2,1,0:T(8,128)(2,1)S(1)} %shard_map.51.e, bf16[2,2,256,256]{3,2,1,0:T(8,128)(2,1)S(1)} %get-tuple-element.47.refs_0_.refs_14_.refs_8_, bf16[2,2,256,256]{3,2,1,0:T(8,128)(2,1)S(1)} %get-tuple-element.48.refs_1_.refs_15_.refs_9_, ...), custom_call_target="tpu_custom_call" | custom-call | flops 2000000000 | bytes 3325952 | tf_op jit(solution)/shard_map/pallas_call | solution.py:23
  41.1 0.0 copy-start.3
  41.1 0.0 collective-permute-done.3.refs_4_.cols
  41.1 0.6 shard_map.49
  41.7 5.1 %collective-permute-start.4 = (f32[320,128]{1,0:T(8,128)S(1)}, f32[320,128]{1,0:T(8,128)S(1)}, u32[]{:S(2)}, u32[]{:S(2)}) collective-permute-start(f32[320,128]{1,0:T(8,128)S(1)} %shard_map.49), channel_id=1, source_target_pairs={{1,32},{32,1},{3,34},{34,3},{5,36},{36,5},{7,38},{38,7},{9,40},{40... | collective-permute-start | bytes 491528 | tf_op jit(solution)/shard_map/ppermute | solution.py:442
  46.9 0.0 copy-done.3
  46.9 0.0 copy-done.7
  46.9 2.8 %shard_map.53.refs_4_ = f32[2,160,640]{2,1,0:T(8,128)S(1)} custom-call(s32[8]{0:T(128)S(1)} %stack.39.info, bf16[2,4,192,256]{3,2,1,0:T(8,128)(2,1)S(1)} %shard_map.51.e, bf16[2,2,256,256]{3,2,1,0:T(8,128)(2,1)S(1)} %get-tuple-element.39.refs_0_.refs_6_, bf16[2,2,256,256]{3,2,1,0:T(8,128)(2,1)S(1)} %get-tuple-element.40.refs_1_.refs_7_, ...), custom_call_target="tpu_custom_call" | custom-call | flops 2000000000 | bytes 3325952 | tf_op jit(solution)/shard_map/pallas_call | solution.py:23
  49.7 0.0 copy-start.4
  49.7 0.9 copy-done.4
  50.6 0.0 copy-start.6
  50.6 0.0 copy-start.8
  50.6 0.0 copy-start.10
  50.6 1.0 %collective-permute-done.4.rows_in = f32[320,128]{1,0:T(8,128)S(1)} collective-permute-done((f32[320,128]{1,0:T(8,128)S(1)}, f32[320,128]{1,0:T(8,128)S(1)}, u32[]{:S(2)}, u32[]{:S(2)}) %collective-permute-start.4) | collective-permute-done | bytes 163872 | tf_op jit(solution)/shard_map/ppermute | solution.py:442
  51.6 6.9 %shard_map.56 = (f32[4,128,128]{2,1,0:T(8,128)S(1)}, f32[128,128]{1,0:T(8,128)S(1)}, f32[128,128]{1,0:T(8,128)S(1)}, f32[4,160,640]{2,1,0:T(8,128)}) custom-call(s32[8]{0:T(128)S(1)} %stack.39.info, f32[4,160,128]{2,1,0:T(8,128)S(1)} %get-tuple-element.32.main, f32[288,128]{1,0:T(8,128)S(1)} %collective-permute-done.3.refs_4_.cols, ...), custom_call_target="tpu_custom_call" | custom-call | flops 4000000000 | bytes 8863744 | tf_op jit(solution)/shard_map/pallas_call | solution.py:23
  58.5 0.0 collective-permute-start.7
  58.5 3.4 %collective-permute-start.8 = (f32[128,128]{1,0:T(8,128)S(1)}, f32[128,128]{1,0:T(8,128)S(1)}, u32[]{:S(2)}, u32[]{:S(2)}) collective-permute-start(f32[128,128]{1,0:T(8,128)S(1)} %get-tuple-element.57), channel_id=1, source_target_pairs={{2,4},{4,2},{3,5},{5,3},{6,8},{8,6},{7,9},{9,7},{10,12},{12,10},{1... | collective-permute-start | bytes 196616 | tf_op jit(solution)/shard_map/ppermute | solution.py:442
  61.9 0.1 collective-permute-done.7.inside
  62.0 4.7 %collective-permute-done.8.beyond = f32[128,128]{1,0:T(8,128)S(1)} collective-permute-done((f32[128,128]{1,0:T(8,128)S(1)}, f32[128,128]{1,0:T(8,128)S(1)}, u32[]{:S(2)}, u32[]{:S(2)}) %collective-permute-start.8) | collective-permute-done | bytes 65568 | tf_op jit(solution)/shard_map/ppermute | solution.py:442
  66.8 0.5 collective-permute-start.9
  67.2 4.7 %collective-permute-start.10 = (f32[6,32,128]{2,1,0:T(8,128)S(1)}, f32[6,32,128]{2,1,0:T(8,128)S(1)}, u32[]{:S(2)}, u32[]{:S(2)}) collective-permute-start(f32[6,32,128]{2,1,0:T(8,128)S(1)} %get-tuple-element.59), channel_id=1, source_target_pairs={{1,32},{32,1},{3,34},{34,3},{5,36},{36,5},{7,38},{38,7},{9,40},{40... | collective-permute-start | bytes 294920 | tf_op jit(solution)/shard_map/ppermute | solution.py:442
  71.9 0.0 collective-permute-done.9.rows_in
  71.9 3.8 %collective-permute-done.10.rows_out = f32[6,32,128]{2,1,0:T(8,128)S(1)} collective-permute-done((f32[6,32,128]{2,1,0:T(8,128)S(1)}, f32[6,32,128]{2,1,0:T(8,128)S(1)}, u32[]{:S(2)}, u32[]{:S(2)}) %collective-permute-start.10) | collective-permute-done | bytes 98336 | tf_op jit(solution)/shard_map/ppermute | solution.py:442
  75.7 0.0 copy-done.6
  75.7 0.0 copy-done.8
  75.7 0.0 copy-done.10
  75.7 9.4 %shard_map.57 = f32[4,128,128]{2,1,0:T(8,128)S(1)} custom-call(s32[8]{0:T(128)S(1)} %stack.39.info, f32[4,128,128]{2,1,0:T(8,128)S(1)} %get-tuple-element.55.main, f32[128,128]{1,0:T(8,128)S(1)} %collective-permute-done.7.inside, f32[128,128]{1,0:T(8,128)S(1)} %collective-permute-done.8.beyond, f32[6,32,128]{2,1,0:T(8,128)S(1)} %collective-permute-done.9.rows_in, ...), custom_call_target="tpu_custom_call" | custom-call | flops 8000000000 | bytes 7307264 | tf_op jit(solution)/shard_map/pallas_call | solution.py:23
  85.1 0.1 collective-permute-start.11
  85.2 7.9 %collective-permute-done.11 = f32[4,128,128]{2,1,0:T(8,128)S(1)} collective-permute-done((f32[4,128,128]{2,1,0:T(8,128)S(1)}, f32[4,128,128]{2,1,0:T(8,128)S(1)}, u32[]{:S(2)}, u32[]{:S(2)}) %collective-permute-start.11) | collective-permute-done | bytes 262176 | tf_op jit(solution)/shard_map/ppermute | solution.py:445
  93.2 0.9 collective-permute-start.12
  94.1 1.5 %collective-permute-done.12 = f32[4,128,256]{2,1,0:T(8,128)S(1)} collective-permute-done((f32[4,128,256]{2,1,0:T(8,128)S(1)}, f32[4,128,256]{2,1,0:T(8,128)S(1)}, u32[]{:S(2)}, u32[]{:S(2)}) %collective-permute-start.12) | collective-permute-done | bytes 524320 | tf_op jit(solution)/shard_map/ppermute | solution.py:445
  95.6 1.0 %maximum_select_fusion = f32[1,4,256,256]{3,2,1,0:T(8,128)} fusion(f32[1,4,128,256]{3,2,1,0:T(8,128)S(1)} %bitcast.24, f32[1,4,128,256]{3,2,1,0:T(8,128)S(1)} %bitcast.23, pred[]{:T(512)S(6)} %eq.7), kind=kLoop, calls=%fused_computation | loop fusion | flops 786432 | bytes 2097153 | tf_op jit(solution)/shard_map/jit(_where)/select_n | solution.py:568
  (3 shorter events, 0.1 us)
Async XLA Ops:
  0.8 1.2 %copy-start = (f32[1,1,4,256,256]{4,3,2,1,0:T(8,128)S(1)}, f32[1,1,4,256,256]{4,3,2,1,0:T(8,128)}, u32[]{:S(2)}) copy-start(f32[1,1,4,256,256]{4,3,2,1,0:T(8,128)} %param.5) | copy-start | bytes 3145732
  2.0 0.7 copy-start.2
  2.7 3.6 %copy-start.1 = (f32[1,4,256,256]{3,2,1,0:T(8,128)S(1)}, f32[1,4,256,256]{3,2,1,0:T(8,128)}, u32[]{:S(2)}) copy-start(f32[1,4,256,256]{3,2,1,0:T(8,128)} %param.4) | copy-start | bytes 3145732
  3.8 23.0 %collective-permute-start = (f32[736,128]{1,0:T(8,128)S(1)}, f32[736,128]{1,0:T(8,128)S(1)}, u32[]{:S(2)}, u32[]{:S(2)}) collective-permute-start(f32[736,128]{1,0:T(8,128)S(1)} %get-tuple-element.34), channel_id=1, source_target_pairs={{0,1},{1,0},{2,3},{3,2},{4,5},{5,4},{6,7},{7,6},{8,9},{9,8},{10,11... | collective-permute-start | bytes 1130504 | tf_op jit(solution)/shard_map/ppermute | solution.py:445
  4.6 22.2 %collective-permute-start.1 = (f32[736,128]{1,0:T(8,128)S(1)}, f32[736,128]{1,0:T(8,128)S(1)}, u32[]{:S(2)}, u32[]{:S(2)}) collective-permute-start(f32[736,128]{1,0:T(8,128)S(1)} %get-tuple-element.35), channel_id=1, source_target_pairs={{0,2},{1,3},{2,0},{3,1},{4,6},{5,7},{6,4},{7,5},{8,10},{9,11},{10,... | collective-permute-start | bytes 1130504 | tf_op jit(solution)/shard_map/ppermute | solution.py:445
  6.2 20.6 %collective-permute-start.2 = (f32[736,128]{1,0:T(8,128)S(1)}, f32[736,128]{1,0:T(8,128)S(1)}, u32[]{:S(2)}, u32[]{:S(2)}) collective-permute-start(f32[736,128]{1,0:T(8,128)S(1)} %get-tuple-element.36), channel_id=1, source_target_pairs={{0,3},{1,2},{2,1},{3,0},{4,7},{5,6},{6,5},{7,4},{8,11},{9,10},{10,... | collective-permute-start | bytes 1130504 | tf_op jit(solution)/shard_map/ppermute | solution.py:445
  7.1 10.8 %collective-permute-start.5 = (f32[160,128]{1,0:T(8,128)S(1)}, f32[160,128]{1,0:T(8,128)S(1)}, u32[]{:S(2)}, u32[]{:S(2)}) collective-permute-start(f32[160,128]{1,0:T(8,128)S(1)} %get-tuple-element.38), channel_id=1, source_target_pairs={{2,4},{4,2},{3,5},{5,3},{6,8},{8,6},{7,9},{9,7},{10,12},{12,10},{1... | collective-permute-start | bytes 245768 | tf_op jit(solution)/shard_map/ppermute | solution.py:442
  18.5 7.4 %collective-permute-start.6 = (f32[192,128]{1,0:T(8,128)S(1)}, f32[192,128]{1,0:T(8,128)S(1)}, u32[]{:S(2)}, u32[]{:S(2)}) collective-permute-start(f32[192,128]{1,0:T(8,128)S(1)} %shard_map.50), channel_id=1, source_target_pairs={{1,32},{32,1},{3,34},{34,3},{5,36},{36,5},{7,38},{38,7},{9,40},{40... | collective-permute-start | bytes 294920 | tf_op jit(solution)/shard_map/ppermute | solution.py:442
  28.1 13.0 %collective-permute-start.3 = (f32[288,128]{1,0:T(8,128)S(1)}, f32[288,128]{1,0:T(8,128)S(1)}, u32[]{:S(2)}, u32[]{:S(2)}) collective-permute-start(f32[288,128]{1,0:T(8,128)S(1)} %shard_map.48), channel_id=1, source_target_pairs={{2,4},{4,2},{3,5},{5,3},{6,8},{8,6},{7,9},{9,7},{10,12},{12,10},{1... | collective-permute-start | bytes 442376 | tf_op jit(solution)/shard_map/ppermute | solution.py:442
  36.5 1.7 %copy-start.5 = (bf16[2,2,320,256]{3,2,1,0:T(8,128)(2,1)}, bf16[2,2,320,256]{3,2,1,0:T(8,128)(2,1)S(1)}, u32[]{:S(2)}) copy-start(bf16[2,2,320,256]{3,2,1,0:T(8,128)(2,1)S(1)} %get-tuple-element.51.refs_4_.refs_18_.refs_12_) | copy-start | bytes 1966084
  36.5 1.7 %copy-start.9 = (bf16[2,2,256,256]{3,2,1,0:T(8,128)(2,1)}, bf16[2,2,256,256]{3,2,1,0:T(8,128)(2,1)S(1)}, u32[]{:S(2)}) copy-start(bf16[2,2,256,256]{3,2,1,0:T(8,128)(2,1)S(1)} %get-tuple-element.52.refs_5_.refs_19_.refs_13_) | copy-start | bytes 1572868
  38.2 8.7 %copy-start.7 = (bf16[2,2,320,256]{3,2,1,0:T(8,128)(2,1)}, bf16[2,2,320,256]{3,2,1,0:T(8,128)(2,1)S(1)}, u32[]{:S(2)}) copy-start(bf16[2,2,320,256]{3,2,1,0:T(8,128)(2,1)S(1)} %get-tuple-element.43.refs_4_.refs_10_) | copy-start | bytes 1966084
  41.1 5.8 %copy-start.3 = (f32[2,160,640]{2,1,0:T(8,128)}, f32[2,160,640]{2,1,0:T(8,128)S(1)}, u32[]{:S(2)}) copy-start(f32[2,160,640]{2,1,0:T(8,128)S(1)} %shard_map.55.refs_5_) | copy-start | bytes 2457604
  41.7 9.9 %collective-permute-start.4 = (f32[320,128]{1,0:T(8,128)S(1)}, f32[320,128]{1,0:T(8,128)S(1)}, u32[]{:S(2)}, u32[]{:S(2)}) collective-permute-start(f32[320,128]{1,0:T(8,128)S(1)} %shard_map.49), channel_id=1, source_target_pairs={{1,32},{32,1},{3,34},{34,3},{5,36},{36,5},{7,38},{38,7},{9,40},{40... | collective-permute-start | bytes 491528 | tf_op jit(solution)/shard_map/ppermute | solution.py:442
  49.7 0.9 copy-start.4
  50.6 25.1 %copy-start.6 = (bf16[2,2,320,256]{3,2,1,0:T(8,128)(2,1)S(1)}, bf16[2,2,320,256]{3,2,1,0:T(8,128)(2,1)}, u32[]{:S(2)}) copy-start(bf16[2,2,320,256]{3,2,1,0:T(8,128)(2,1)} %copy-done.5) | copy-start | bytes 1966084
  50.6 25.1 %copy-start.8 = (bf16[2,2,320,256]{3,2,1,0:T(8,128)(2,1)S(1)}, bf16[2,2,320,256]{3,2,1,0:T(8,128)(2,1)}, u32[]{:S(2)}) copy-start(bf16[2,2,320,256]{3,2,1,0:T(8,128)(2,1)} %copy-done.7) | copy-start | bytes 1966084
  50.6 25.1 %copy-start.10 = (bf16[2,2,256,256]{3,2,1,0:T(8,128)(2,1)S(1)}, bf16[2,2,256,256]{3,2,1,0:T(8,128)(2,1)}, u32[]{:S(2)}) copy-start(bf16[2,2,256,256]{3,2,1,0:T(8,128)(2,1)} %copy-done.9) | copy-start | bytes 1572868
  58.5 3.5 %collective-permute-start.7 = (f32[128,128]{1,0:T(8,128)S(1)}, f32[128,128]{1,0:T(8,128)S(1)}, u32[]{:S(2)}, u32[]{:S(2)}) collective-permute-start(f32[128,128]{1,0:T(8,128)S(1)} %get-tuple-element.56), channel_id=1, source_target_pairs={{0,2},{1,3},{2,0},{3,1},{4,6},{5,7},{6,4},{7,5},{8,10},{9,11},{10,... | collective-permute-start | bytes 196616 | tf_op jit(solution)/shard_map/ppermute | solution.py:445
  58.5 8.2 %collective-permute-start.8 = (f32[128,128]{1,0:T(8,128)S(1)}, f32[128,128]{1,0:T(8,128)S(1)}, u32[]{:S(2)}, u32[]{:S(2)}) collective-permute-start(f32[128,128]{1,0:T(8,128)S(1)} %get-tuple-element.57), channel_id=1, source_target_pairs={{2,4},{4,2},{3,5},{5,3},{6,8},{8,6},{7,9},{9,7},{10,12},{12,10},{1... | collective-permute-start | bytes 196616 | tf_op jit(solution)/shard_map/ppermute | solution.py:442
  66.8 5.1 %collective-permute-start.9 = (f32[6,32,128]{2,1,0:T(8,128)S(1)}, f32[6,32,128]{2,1,0:T(8,128)S(1)}, u32[]{:S(2)}, u32[]{:S(2)}) collective-permute-start(f32[6,32,128]{2,1,0:T(8,128)S(1)} %broadcast_select_fusion.1), channel_id=1, source_target_pairs={{0,1},{1,0},{2,3},{3,2},{4,5},{5,4},{6,7},{7,6},{8,9},{9,8},{10,11... | collective-permute-start | bytes 294920 | tf_op jit(solution)/shard_map/ppermute | solution.py:445
  67.2 8.5 %collective-permute-start.10 = (f32[6,32,128]{2,1,0:T(8,128)S(1)}, f32[6,32,128]{2,1,0:T(8,128)S(1)}, u32[]{:S(2)}, u32[]{:S(2)}) collective-permute-start(f32[6,32,128]{2,1,0:T(8,128)S(1)} %get-tuple-element.59), channel_id=1, source_target_pairs={{1,32},{32,1},{3,34},{34,3},{5,36},{36,5},{7,38},{38,7},{9,40},{40... | collective-permute-start | bytes 294920 | tf_op jit(solution)/shard_map/ppermute | solution.py:442
  85.1 8.0 %collective-permute-start.11 = (f32[4,128,128]{2,1,0:T(8,128)S(1)}, f32[4,128,128]{2,1,0:T(8,128)S(1)}, u32[]{:S(2)}, u32[]{:S(2)}) collective-permute-start(f32[4,128,128]{2,1,0:T(8,128)S(1)} %shard_map.57), channel_id=1, source_target_pairs={{0,2},{1,3},{2,0},{3,1},{4,6},{5,7},{6,4},{7,5},{8,10},{9,11},{10,... | collective-permute-start | bytes 786440 | tf_op jit(solution)/shard_map/ppermute | solution.py:445
  93.2 2.5 %collective-permute-start.12 = (f32[4,128,256]{2,1,0:T(8,128)S(1)}, f32[4,128,256]{2,1,0:T(8,128)S(1)}, u32[]{:S(2)}, u32[]{:S(2)}) collective-permute-start(f32[4,128,256]{2,1,0:T(8,128)S(1)} %maximum_select_fusion.1), channel_id=1, source_target_pairs={{0,1},{1,0},{2,3},{3,2},{4,5},{5,4},{6,7},{7,6},{8,9},{9,8},{10,11... | collective-permute-start | bytes 1572872 | tf_op jit(solution)/shard_map/ppermute | solution.py:445

commit v3 on v2

--- a/solution.py
+++ b/solution.py
@@ -13,20 +13,36 @@
 F32 = jnp.float32
 BF16 = jnp.bfloat16
 VMEM = pltpu.VMEM
+HBM = pltpu.MemorySpace.HBM
 SMEM = pltpu.SMEM
 
 
-def call(body, outs, scratch, scalars, *args, flops=0):
+def call(body, outs, scratch, scalars, *args, flops=0, in_place=(), in_hbm=(), limit=24):
     specs = [pl.BlockSpec(memory_space=SMEM)] * len(scalars)
-    specs += [pl.BlockSpec(memory_space=VMEM)] * len(args)
+    specs += [
+        pl.BlockSpec(memory_space=HBM if n in in_place else VMEM) for n in range(len(args))
+    ]
+    args = [
+        pltpu.with_memory_space_constraint(a, HBM) if n in in_place else a
+        for n, a in enumerate(args)
+    ]
     moved = sum(a.size * a.dtype.itemsize for a in args)
+    leaves = [
+        HBM(a.shape, a.dtype) if n in in_hbm else a for n, a in enumerate(jax.tree.leaves(outs))
+    ]
     return pl.pallas_call(
         body,
-        out_shape=outs,
+        out_shape=jax.tree.unflatten(jax.tree.structure(outs), leaves),
         in_specs=specs,
-        out_specs=jax.tree.map(lambda _: pl.BlockSpec(memory_space=VMEM), outs),
+        out_specs=jax.tree.unflatten(
+            jax.tree.structure(outs),
+            [
+                pl.BlockSpec(memory_space=HBM if n in in_hbm else VMEM)
+                for n in range(len(jax.tree.leaves(outs)))
+            ],
+        ),
         scratch_shapes=scratch,
-        compiler_params=pltpu.CompilerParams(vmem_limit_bytes=48 * 1024 * 1024),
+        compiler_params=pltpu.CompilerParams(vmem_limit_bytes=limit * 1024 * 1024),
         cost_estimate=pl.CostEstimate(flops=flops, bytes_accessed=moved, transcendentals=0),
     )(*scalars, *args)
 
@@ -66,7 +82,7 @@
     lane = lanes(rows)
     out = jnp.zeros((rows, 128), F32)
     for z, piece in enumerate(pieces):
-        mine = jnp.where(qx == 0, turn(piece, 32 * z), turn(piece, 32 * z + 32))
+        mine = turn(piece, lax.rem(32 * z + 32 * qx, 128))
         out = jnp.where((lane >= 32 * z) & (lane < 32 * z + 32), mine, out)
     return jnp.where(right_half(rows) == (qx == 0), out, 0.0)
 
@@ -83,32 +99,59 @@
     return both[:rows] + (both[rows:] + rest)
 
 
-def send_kernel(info, variants, rec, table, *refs):
-    sent, taps = refs[:4], refs[4]
-    view, row, col, last = info[0], info[5], info[6], info[7]
-    sums = jnp.sum(table[...], axis=-1, keepdims=True)
-    taps[...] = table[...] / sums
+def send_kernel(grid_rows, rec, table, variants, *refs):
+    sent, (raw, ids, whole, sems) = refs[:4], refs[4:]
+    loads = [pltpu.make_async_copy(rec.at[z], whole.at[z], sems.at[z]) for z in range(4)]
+    small = [
+        pltpu.make_async_copy(table, raw, sems.at[4]),
+        pltpu.make_async_copy(variants, ids, sems.at[5]),
+    ]
+    for load in (*small, *loads):
+        load.start()
+    tile, view = lax.axis_index("tile"), lax.axis_index("view")
+    row, col = lax.div(tile, GX), lax.rem(tile, GX)
+    places = []
     for s in range(4):
         q = jnp.bitwise_xor(view, s)
         qx, qy = lax.shift_right_logical(q, 1), jnp.bitwise_and(q, 1)
         rows = pl.ds(pl.multiple_of(112 * qy, 16), 144)
         here = pl.ds(pl.multiple_of(128 * qx, 128), 128)
         there = pl.ds(pl.multiple_of(128 - 128 * qx, 128), 128)
-        for z in range(4):
-            sent[s][144 * z : 144 * z + 144] = rec[z, rows, here]
-        sent[s][576:720] = shared([rec[z, rows, there] for z in range(4)], qx)
-        sent[s][720:736] = jnp.zeros((16, 128), F32)
+        places.append((qx, qy, rows, here, there))
+    for load in small:
+        load.wait()
+    raw[...] = raw[...] / jnp.sum(raw[...], axis=-1, keepdims=True)
+    for s, (qx, qy, _, _, _) in enumerate(places):
+        sent[s][648:664] = jnp.zeros((16, 128), F32)
         for n in range(4):
             x = jnp.clip(col + (2 * qx - 1) * (n % 2), 0, GX - 1)
-            y = jnp.clip(row + (2 * qy - 1) * (n // 2), 0, last)
-            sent[s][720 + 3 * n : 723 + 3 * n, 0:31] = taps[variants[y * GX + x]]
-
-
-def start_kernel(info, first, main, inside, edge):
+            y = jnp.clip(row + (2 * qy - 1) * (n // 2), 0, grid_rows - 1)
+            which = ids[0, y * GX + x]
+            for axis in range(3):
+                at = 648 + 3 * n + axis
+                sent[s][at : at + 1, 0:31] = raw[axis, pl.ds(which, 1)]
+    for z in range(4):
+        loads[z].wait()
+        for s, (_, _, rows, here, _) in enumerate(places):
+            sent[s][144 * z : 144 * z + 144] = whole[z, rows, here]
+    for s, (qx, _, rows, _, there) in enumerate(places):
+        side = shared([whole[z, rows, there] for z in range(4)], qx)
+        sent[s][576:648] = side[:72] + turn(side[72:], 16 + 96 * qx)
+
+
+def own_side(block, qx):
+    side = block[576:648]
+    mine = right_half(72) == (qx == 0)
+    low = jnp.where(mine, turn(side, 112 - 96 * qx), 0.0)
+    return jnp.concatenate([jnp.where(mine, side, 0.0), low], 0)
+
+
+def start_kernel(first, main, inside, edge):
+    view = lax.axis_index("view")
     for q in range(4):
         qx, qy = q // 2, q % 2
 
-        @pl.when(info[0] == q)
+        @pl.when(view == q)
         def _():
             span = slice(96 * qy, 96 * qy + 160)
             own = [first[z, span, 128 * qx : 128 * qx + 128] for z in range(4)]
@@ -127,26 +170,27 @@
         for s in (2 * h, 2 * h + 1):
             block = got[s ^ 2]
             cols.append(shared([block[144 * z : 144 * z + 144] for z in range(4)], qx))
-        other = jnp.where(qx == 0, turn(cols[1], 16), turn(cols[1], -16))
+        other = turn(cols[1], 16 + 96 * qx)
         out[h * 144 : h * 144 + 144] = cols[0] + other
 
 
 def both_sides(inner, cols, odd, qx):
     rows = inner.shape[0]
     if odd:
-        cols = jnp.where(qx == 0, turn(cols, 16), turn(cols, -16))
+        cols = turn(cols, 16 + 96 * qx)
     return jnp.where(right_half(rows) == (qx == 0), inner, cols)
 
 
 def pack_rows_kernel(info, *refs):
     got, cols, out = refs[:4], refs[4], refs[5]
     at = pl.multiple_of(128 * info[2], 16)
+    sides = [own_side(got[s], info[1]) for s in range(4)]
     for s in range(4):
         o = s ^ 1
         for z in range(4):
             n = 4 * s + z
             out[n * 16 : n * 16 + 16] = got[o][pl.ds(144 * z + at, 16)]
-        inner = got[o][pl.ds(576 + at, 16)]
+        inner = jnp.where(info[2] == 0, sides[o][:16], sides[o][128:])
         outer = cols[pl.ds((o // 2) * 144 + at, 16)]
         out[256 + 16 * s : 272 + 16 * s] = both_sides(inner, outer, o % 2, info[1])
 
@@ -156,7 +200,7 @@
     for z in range(4):
         out[32 * z : 32 * z + 32] = main[z, pl.ds(at, 32)]
     out[128:160] = inside[pl.ds(at, 32)]
-    out[160:192] = cols[pl.ds(at, 32)]
+    out[160:192] = jnp.where(info[3] > 0, cols[pl.ds(at, 32)], 0.0)
 
 
 def toeplitz(base, shift):
@@ -166,7 +210,7 @@
 def matrices_kernel(info, one, two, xh, xl, ah, al, y, t, zm, zs):
     qx, qy = info[1], info[2]
     for s, table in enumerate((one, two)):
-        fwd = table[720:736]
+        fwd = table[648:664]
         flip = lax.broadcasted_iota(jnp.int32, (128, 128), 0) + lanes(128) == 30
         rev = jnp.dot(fwd, flip.astype(F32), precision=lax.Precision.HIGHEST)
         zero = jnp.zeros((16, 128), F32)
@@ -244,11 +288,12 @@
     other = pl.multiple_of(160 * info[2], 32)
     for z in range(4):
         region[z, pl.ds(own, 160)] = main[z]
-        region[z, pl.ds(other, 32)] = rows_in[32 * z : 32 * z + 32]
+    for n in range(6):
+        region[n, pl.ds(other, 32)] = jnp.where(
+            info[4] > 0, rows_in[32 * n : 32 * n + 32], 0.0
+        )
     region[4, pl.ds(own, 160)] = inside[...]
-    region[5, pl.ds(own, 160)] = cols[...]
-    region[4, pl.ds(other, 32)] = rows_in[128:160]
-    region[5, pl.ds(other, 32)] = rows_in[160:192]
+    region[5, pl.ds(own, 160)] = jnp.where(info[3] > 0, cols[...], 0.0)
     spread(region, e, info[1])
 
 
@@ -359,7 +404,7 @@
 def adjoint_kernel(info, main, cols, rows_in, *refs):
     got, blurs, refs = refs[:4], refs[4:6], refs[6:]
     groups, refs = (refs[:8], refs[8:16]), refs[16:]
-    out, near_edge, far_edge, rec, r, total = refs
+    out, near_edge, far_edge, kept, rec, r, total, sem = refs
     qx, qy = info[1], info[2]
     in_tile = pl.multiple_of(16 * (1 - qy), 16)
     out_tile = pl.multiple_of(144 * qy, 16)
@@ -370,8 +415,10 @@
             n = 4 * s + z
             rec[s, pl.ds(out_tile, 16), here] = rows_in[n * 16 : n * 16 + 16]
         outer = cols[(s // 2) * 144 : (s // 2) * 144 + 144]
-        rec[s, pl.ds(in_tile, 144), 512:] = both_sides(got[s][576:720], outer, s % 2, qx)
+        rec[s, pl.ds(in_tile, 144), 512:] = both_sides(own_side(got[s], qx), outer, s % 2, qx)
         rec[s, pl.ds(out_tile, 16), 512:] = rows_in[256 + 16 * s : 272 + 16 * s]
+    keep = pltpu.make_async_copy(rec, kept, sem)
+    keep.start()
     clear(r, 160)
     total[...] = jnp.zeros_like(total)
     masks = row_masks(info)
@@ -389,19 +436,28 @@
         lax.fori_loop(0, 2, body, 0)
     at = pl.ds(pl.multiple_of(32 * qy, 32), 128)
     update(True, main, at, total, out, (near_edge, far_edge), qx)
-
-
-def step_kernel(info, main, inside, beyond, rows_in, rows_out, rec, *refs):
-    groups, refs = (refs[:8], refs[8:16]), refs[16:]
-    out, region, e, p, r, total = refs
+    keep.wait()
+
+
+def step_kernel(info, main, inside, beyond, rows_in, rows_out, *refs):
+    far_refs, (out, region, e, p, r, total), refs = refs[:17], refs[17:23], refs[23:]
+    near_refs, sems = refs[:17], refs[17]
+    loads = []
+    for n, (there, here) in enumerate(zip(far_refs, near_refs, strict=True)):
+        loads.append(pltpu.make_async_copy(there, here, sems.at[n]))
+    for n in (0, 1, 4, 6, 7, 8, 5, 2, 3, 9, 10, 13, 15, 16, 14, 11, 12):
+        loads[n].start()
+    groups, rec = (near_refs[:8], near_refs[9:]), near_refs[8]
     qx, qy = info[1], info[2]
     for z in range(4):
         region[z, 32:160] = main[z]
     region[4, 32:160] = inside[...]
-    region[5, 32:160] = beyond[...]
+    region[5, 32:160] = jnp.where(info[3] > 0, beyond[...], 0.0)
     for n in range(6):
         region[n, pl.ds(pl.multiple_of(160 * (1 - qy), 32), 32)] = rows_in[n]
-        region[n, pl.ds(pl.multiple_of(160 * qy, 32), 32)] = rows_out[n]
+        region[n, pl.ds(pl.multiple_of(160 * qy, 32), 32)] = jnp.where(
+            info[4] > 0, rows_out[n], 0.0
+        )
     spread(region, e, qx)
     clear(p, 192)
     clear(r, 160)
@@ -410,11 +466,21 @@
     far160, far128 = far_mask(160, qx), far_mask(128, qx)
     for pair in range(2):
         mats = groups[pair]
+        early, late = ((0, 1, 4, 6, 7), (8, 5, 2, 3)) if pair == 0 else ((9, 10, 13, 15, 16), (14, 11, 12))
+        for n in early:
+            loads[n].wait()
 
         def body(s, carry):
             slot = 2 * pair + s
 
             def put(where, value):
+                if where.start == 0:
+
+                    @pl.when(s == 0)
+                    def _():
+                        for n in late:
+                            loads[n].wait()
+
                 take_ratio(slot, rec, r, masks, where, value)
 
             near, edge = forward(s, qy, e, mats, p, put)
@@ -425,6 +491,27 @@
 
         lax.fori_loop(0, 2, body, 0)
     update(False, main, slice(0, 128), total, out, None, qx)
+
+
+def make_matrices(info, one, two):
+    return call(
+        matrices_kernel,
+        (
+            shape(2, 2, 256, 256, dtype=BF16),
+            shape(2, 2, 256, 256, dtype=BF16),
+            shape(2, 256, 128, dtype=BF16),
+            shape(2, 256, 128, dtype=BF16),
+            shape(2, 2, 320, 256, dtype=BF16),
+            shape(2, 2, 256, 256, dtype=BF16),
+            shape(2, 2, 8, 128),
+            shape(2, 2, 16, 128),
+        ),
+        [],
+        (info,),
+        one,
+        two,
+        flops=1_000_000_000,
+    )
 
 
 def per_device(initial, recorded, tap_table, variants):
@@ -436,7 +523,7 @@
     qx, qy = view // 2, view % 2
     has_x = jnp.where(qx == 0, tile_col > 0, tile_col < GX - 1).astype(jnp.int32)
     has_y = jnp.where(qy == 0, tile_row > 0, tile_row < grid_rows - 1).astype(jnp.int32)
-    info = jnp.stack([view, qx, qy, has_x, has_y, tile_row, tile_col, grid_rows - 1])
+    info = jnp.stack([view, qx, qy, has_x, has_y])
 
     def route(x, pairs):
         return lax.ppermute(x, ("tile", "view"), pairs)
@@ -447,28 +534,42 @@
     x_pairs, y_pairs = [], []
     for t in range(count_tiles):
         for v in range(4):
+            me, right, below = 4 * t + v, 4 * (t + 1) + v - 2, 4 * (t + GX) + v - 1
             if v // 2 and t % GX < GX - 1:
-                x_pairs += [(4 * t + v, 4 * (t + 1) + v - 2), (4 * (t + 1) + v - 2, 4 * t + v)]
+                x_pairs += [(me, right), (right, me)]
             if v % 2 and t + GX < count_tiles:
-                y_pairs += [(4 * t + v, 4 * (t + GX) + v - 1), (4 * (t + GX) + v - 1, 4 * t + v)]
+                y_pairs += [(me, below), (below, me)]
+            if t % GX == (GX - 1 if v // 2 else 0):
+                x_pairs.append((me, 4 * t + (v ^ 1)))
+            if t // GX == (grid_rows - 1 if v % 2 else 0):
+                y_pairs.append((me, 4 * t + (v ^ 2)))
 
     sent = call(
-        send_kernel,
-        (shape(736, 128),) * 4,
-        [VMEM((8, 3, 31), F32)],
-        (info, variants[0]),
+        functools.partial(send_kernel, grid_rows),
+        (shape(664, 128),) * 4,
+        [
+            VMEM((3, 8, 31), F32),
+            SMEM((1, count_tiles), jnp.int32),
+            VMEM((4, 256, 256), F32),
+            pltpu.SemaphoreType.DMA((6,)),
+        ],
+        (),
         recorded[0, 0],
-        tap_table[0],
+        tap_table[0].transpose(1, 0, 2),
+        variants,
+        in_place=(0, 1, 2),
     )
     got = [sent[0]] + [over_view(sent[s], s) for s in (1, 2, 3)]
     main, inside, edge = call(
         start_kernel,
         (shape(4, 160, 128), shape(160, 128), shape(160, 128)),
         [],
-        (info,),
+        (),
         initial[0],
     )
     start_cols = route(edge, x_pairs)
+    mats = [make_matrices(info, *got[:2])]
+    start_cols, mats[0] = lax.optimization_barrier((start_cols, mats[0]))
     start_rows = route(
         call(start_rows_kernel, shape(192, 128), [], (info,), main, inside, start_cols), y_pairs
     )
@@ -482,38 +583,20 @@
         start_cols,
         start_rows,
     )
-    mats, blurs = [], []
-    for pair in (got[:2], got[2:]):
-        mats.append(
-            call(
-                matrices_kernel,
-                (
-                    shape(2, 2, 256, 256, dtype=BF16),
-                    shape(2, 2, 256, 256, dtype=BF16),
-                    shape(2, 256, 128, dtype=BF16),
-                    shape(2, 256, 128, dtype=BF16),
-                    shape(2, 2, 320, 256, dtype=BF16),
-                    shape(2, 2, 256, 256, dtype=BF16),
-                    shape(2, 2, 8, 128),
-                    shape(2, 2, 16, 128),
-                ),
-                [],
-                (info,),
-                *pair,
-                flops=1_000_000_000,
-            )
+    e, got = lax.optimization_barrier((e, got))
+    mats.append(make_matrices(info, *got[2:]))
+    blurs = [
+        call(
+            forward_kernel,
+            shape(2, 160, 640),
+            [VMEM((2, 256, 640), BF16)],
+            (info,),
+            e,
+            *group,
+            flops=2_000_000_000,
         )
-        blurs.append(
-            call(
-                forward_kernel,
-                shape(2, 160, 640),
-                [VMEM((2, 256, 640), BF16)],
-                (info,),
-                e,
-                *mats[-1],
-                flops=2_000_000_000,
-            )
-        )
+        for group in mats
+    ]
     cols = route(call(pack_cols_kernel, shape(288, 128), [], (info,), *got), x_pairs)
     rows = route(call(pack_rows_kernel, shape(320, 128), [], (info,), *got, cols), y_pairs)
     quad = shape(4, 128, 128)
@@ -521,7 +604,12 @@
     estimate, near_edge, far_edge, rec = call(
         adjoint_kernel,
         (quad, shape(128, 128), shape(128, 128), shape(4, 160, 640)),
-        [VMEM((2, 256, 640), BF16), VMEM((4, 128, 128), F32)],
+        [
+            VMEM((4, 160, 640), F32),
+            VMEM((2, 256, 640), BF16),
+            VMEM((4, 128, 128), F32),
+            pltpu.SemaphoreType.DMA,
+        ],
         (info,),
         main,
         cols,
@@ -530,14 +618,17 @@
         *blurs,
         *flat,
         flops=4_000_000_000,
+        in_hbm=(3,),
     )
     for step in range(1, ITERS):
         inside = over_view(near_edge, 2)
         beyond = route(far_edge, x_pairs)
-        whole = jnp.concatenate([estimate, inside[None], beyond[None]])
+        shown = jnp.where(has_x > 0, beyond, 0.0)
+        whole = jnp.concatenate([estimate, inside[None], shown[None]])
         low, high = whole[:, :32], whole[:, 96:]
         rows_in = over_view(jnp.where(qy == 0, high, low), 1)
         rows_out = route(jnp.where(qy == 0, low, high), y_pairs)
+        far_args = [*mats[0], rec, *mats[1]]
         estimate = call(
             step_kernel,
             quad,
@@ -547,6 +638,8 @@
                 VMEM((2, 256, 640), BF16),
                 VMEM((2, 256, 640), BF16),
                 VMEM((4, 128, 128), F32),
+                *(VMEM(a.shape, a.dtype) for a in far_args),
+                pltpu.SemaphoreType.DMA((17,)),
             ],
             (info,),
             estimate,
@@ -554,20 +647,18 @@
             beyond,
             rows_in,
             rows_out,
-            rec,
-            *flat,
+            *far_args,
             flops=8_000_000_000,
+            in_place=range(5, 22),
         )
-    across = over_view(estimate, 2)
-    wide = jnp.where(
-        qx == 0,
-        jnp.concatenate([estimate, across], 2),
-        jnp.concatenate([across, estimate], 2),
-    )
-    down = over_view(wide, 1)
-    return jnp.where(
-        qy == 0, jnp.concatenate([wide, down], 1), jnp.concatenate([down, wide], 1)
-    )[None]
+    across, down = over_view(estimate, 2), over_view(estimate, 1)
+    corner = over_view(across, 1)
+    halves = []
+    for y in range(2):
+        near, far = jnp.where(qy == y, estimate, down), jnp.where(qy == y, across, corner)
+        left, right = jnp.where(qx == 0, near, far), jnp.where(qx == 0, far, near)
+        halves.append(jnp.concatenate([left, right], 2))
+    return jnp.concatenate(halves, 1)[None]
 
 
 def solution(mesh):

time: 97 us -> 82.9 us (0.85)
  starting transfers between devices: 35.3 us -> 28.8 us
  local copies, waits for them, and re-layouts: 3.59 us -> 0.16 us
  waiting for transfers between devices: 25.9 us -> 22.8 us
  Pallas kernels: 30.5 us -> 29.5 us
    ppermute x6, starting transfers between devices: 31.3 us -> 24.3 us  [route(): return lax.ppermute(x, ('tile', 'view'), pairs)]
    ppermute x6, waiting for transfers between devices: 16.4 us -> 12.8 us  [route(): return lax.ppermute(x, ('tile', 'view'), pairs)]
    unnamed x23 -> x34, local copies, waits for them, and re-layouts: 3.51 us -> 0.07 us
    broadcast_in_dim x0 -> x2, other arithmetic: none -> 1.05 us  [the longest x1 1.04 us: per_device(): return jnp.concatenate(halves, 1)[None]]
    pallas_call x12, Pallas kernels: 30.5 us -> 29.5 us  [call(): pl.pallas_call(body, out_shape=jax.tree.unflatten(jax.tree.structure(outs...]
    select_n x2 -> x1, other arithmetic: 1.09 us -> 0.1 us  [per_device(): left, right = (jnp.where(qx == 0, near, far), jnp.where(qx == 0, far, near))]
    ppermute x7 -> x8, starting transfers between devices: 3.99 us -> 4.53 us  [over_view(): return lax.ppermute(x, 'view', [(i, i ^ flip) for i in range(4)])]
    ppermute x7 -> x8, waiting for transfers between devices: 9.51 us -> 9.97 us  [over_view(): return lax.ppermute(x, 'view', [(i, i ^ flip) for i in range(4)])]
  transfers between devices with their start and end apart: 13 -> 14, of which waited for: 8 -> 9; matrix products, arithmetic and copies ran while one was open for 0% -> 0% of each run, Pallas kernels for 12% -> 11%
where the time goes in v3:
time: 82.9 us; the launch traced here: 82.8 us
  Pallas kernels  29.5 us (36%)
  starting transfers between devices  28.8 us (35%)
  waiting for transfers between devices  22.8 us (28%)
  other arithmetic  1.19 us (1%)
    pallas_call x12, Pallas kernels, call(): pl.pallas_call(body, out_shape=jax.tree.unflatten(jax.tree.structure(outs...  29.5 us
    ppermute x6, starting transfers between devices, route(): return lax.ppermute(x, ('tile', 'view'), pairs)  24.3 us
    ppermute x6, waiting for transfers between devices, route(): return lax.ppermute(x, ('tile', 'view'), pairs)  12.8 us
    ppermute x8, waiting for transfers between devices, over_view(): return lax.ppermute(x, 'view', [(i, i ^ flip) for i in range(4)])  9.97 us
    ppermute x8, starting transfers between devices, over_view(): return lax.ppermute(x, 'view', [(i, i ^ flip) for i in range(4)])  4.53 us
  transfers between devices with their start and end apart: 14, of which 9 were waited for; matrix products, arithmetic and copies ran while one was open for 0% of the time, Pallas kernels for 11%

profile of v3, /device:TPU:13, one launch (start us, length us, event | category | flops | bytes accessed | tf_op | source)
XLA Modules:
  0.0 82.8 jit_solution(6920198235864675388)
XLA Ops:
  0.0 2.0 %shard_map.47 = (f32[664,128]{1,0:T(8,128)S(1)}, f32[664,128]{1,0:T(8,128)S(1)}, f32[664,128]{1,0:T(8,128)S(1)}, f32[664,128]{1,0:T(8,128)S(1)}) custom-call(f32[4,256,256]{2,1,0:T(8,128)} %bitcast.17, f32[3,8,31]{2,1,0:T(8,128)} %bitcast.18, s32[1,64]{1,0:T(1,128)} %variants.1), custom_call_target="tpu_custom_call" | custom-call | bytes 1051808 | tf_op jit(solution)/shard_map/pallas_call | solution.py:33
  2.0 0.8 collective-permute-start.1
  2.8 1.7 %collective-permute-start.3 = (f32[664,128]{1,0:T(8,128)S(1)}, f32[664,128]{1,0:T(8,128)S(1)}, u32[]{:S(2)}, u32[]{:S(2)}) collective-permute-start(f32[664,128]{1,0:T(8,128)S(1)} %get-tuple-element.60), channel_id=1, source_target_pairs={{0,2},{1,3},{2,0},{3,1},{4,6},{5,7},{6,4},{7,5},{8,10},{9,11},{10,... | collective-permute-start | bytes 1019912 | tf_op jit(solution)/shard_map/ppermute | solution.py:532
  4.4 0.1 collective-permute-start.4
  4.5 0.0 copy-done
  4.5 0.2 shard_map.46
  4.7 5.5 %collective-permute-start = (f32[160,128]{1,0:T(8,128)S(1)}, f32[160,128]{1,0:T(8,128)S(1)}, u32[]{:S(2)}, u32[]{:S(2)}) collective-permute-start(f32[160,128]{1,0:T(8,128)S(1)} %get-tuple-element.48), channel_id=1, source_target_pairs={{0,1},{1,0},{2,4},{4,2},{3,5},{5,3},{6,8},{8,6},{7,9},{9,7},{10,12... | collective-permute-start | bytes 245768 | tf_op jit(solution)/shard_map/ppermute | solution.py:529
  10.2 0.1 stack.27.info
  10.3 0.0 collective-permute-done.1.two.refs_1_
  10.3 1.7 %shard_map.48 = (bf16[2,2,256,256]{3,2,1,0:T(8,128)(2,1)S(1)}, bf16[2,2,256,256]{3,2,1,0:T(8,128)(2,1)S(1)}, bf16[2,256,128]{2,1,0:T(8,128)(2,1)S(1)}, bf16[2,25...) custom-call(s32[5]{0:T(128)S(1)} %stack.27.info, ...), custom_call_target="tpu_custom_call" | custom-call | flops 1000000000 | bytes 679936 | tf_op jit(solution)/shard_map/pallas_call | solution.py:33
  12.0 0.0 copy-start.1
  12.0 0.0 copy-start.3
  12.0 0.0 copy-start.4
  12.0 0.0 copy-start.5
  12.0 0.0 copy-start.9
  12.0 0.0 copy-start.10
  12.1 0.0 copy-start.13
  12.1 0.0 copy-start.15
  12.1 0.8 %collective-permute-done.cols = f32[160,128]{1,0:T(8,128)S(1)} collective-permute-done((f32[160,128]{1,0:T(8,128)S(1)}, f32[160,128]{1,0:T(8,128)S(1)}, u32[]{:S(2)}, u32[]{:S(2)}) %collective-permute-start) | collective-permute-done | bytes 81952 | tf_op jit(solution)/shard_map/ppermute | solution.py:529
  12.9 0.6 shard_map.49
  13.5 3.0 %collective-permute-start.2 = (f32[192,128]{1,0:T(8,128)S(1)}, f32[192,128]{1,0:T(8,128)S(1)}, u32[]{:S(2)}, u32[]{:S(2)}) collective-permute-start(f32[192,128]{1,0:T(8,128)S(1)} %shard_map.49), channel_id=1, source_target_pairs={{0,2},{1,32},{32,1},{2,0},{3,34},{34,3},{4,6},{5,36},{36,5},{6,4},... | collective-permute-start | bytes 294920 | tf_op jit(solution)/shard_map/ppermute | solution.py:529
  16.5 2.9 %collective-permute-done.2.rows_in = f32[192,128]{1,0:T(8,128)S(1)} collective-permute-done((f32[192,128]{1,0:T(8,128)S(1)}, f32[192,128]{1,0:T(8,128)S(1)}, u32[]{:S(2)}, u32[]{:S(2)}) %collective-permute-start.2) | collective-permute-done | bytes 98336 | tf_op jit(solution)/shard_map/ppermute | solution.py:529
  19.4 0.9 %shard_map.50.e = bf16[2,4,192,256]{3,2,1,0:T(8,128)(2,1)S(1)} custom-call(s32[5]{0:T(128)S(1)} %stack.27.info, f32[4,160,128]{2,1,0:T(8,128)S(1)} %get-tuple-element.46.main, f32[160,128]{1,0:T(8,128)S(1)} %get-tuple-element.47.inside, f32[160,128]{1,0:T(8,128)S(1)} %collective-permute-done.cols, f32[192,128]{1,0:T(8,128)S(1)} %collective-permute-done.2.rows_in), custom_call_target="tpu_custom_call" | custom-call | bytes 589824 | tf_op jit(solution)/shard_map/pallas_call | solution.py:33
  20.3 0.0 collective-permute-done.3.refs_2_.one
  20.3 0.0 collective-permute-done.4.refs_3_.two
  20.3 1.7 %shard_map.54 = (bf16[2,2,256,256]{3,2,1,0:T(8,128)(2,1)S(1)}, bf16[2,2,256,256]{3,2,1,0:T(8,128)(2,1)S(1)}, bf16[2,256,128]{2,1,0:T(8,128)(2,1)S(1)}, bf16[2,25...) custom-call(s32[5]{0:T(128)S(1)} %stack.27.info, ...), custom_call_target="tpu_custom_call" | custom-call | flops 1000000000 | bytes 679936 | tf_op jit(solution)/shard_map/pallas_call | solution.py:33
  22.0 0.0 copy-start.2
  22.0 0.0 copy-start.6
  22.0 0.0 copy-start.7
  22.0 0.0 copy-start.8
  22.0 0.0 copy-start.11
  22.0 0.0 copy-start.12
  22.0 0.0 copy-start.14
  22.0 0.0 copy-start.16
  22.0 1.1 %shard_map.51 = f32[288,128]{1,0:T(8,128)S(1)} custom-call(s32[5]{0:T(128)S(1)} %stack.27.info, f32[664,128]{1,0:T(8,128)S(1)} %get-tuple-element.62.one.refs_0_, f32[664,128]{1,0:T(8,128)S(1)} %collective-permute-done.1.two.refs_1_, f32[664,128]{1,0:T(8,128)S(1)} %collective-permute-done.3.refs_2_.one, f32[664,128]{1,0:T(8,128)S(1)} %collective-permute-done.4.refs_3_.two), custom_call_target="tpu_custom_call" | custom-call | bytes 1359872 | tf_op jit(solution)/shard_map/pallas_call | solution.py:33
  23.1 5.0 %collective-permute-start.5 = (f32[288,128]{1,0:T(8,128)S(1)}, f32[288,128]{1,0:T(8,128)S(1)}, u32[]{:S(2)}, u32[]{:S(2)}) collective-permute-start(f32[288,128]{1,0:T(8,128)S(1)} %shard_map.51), channel_id=1, source_target_pairs={{0,1},{1,0},{2,4},{4,2},{3,5},{5,3},{6,8},{8,6},{7,9},{9,7},{10,12... | collective-permute-start | bytes 442376 | tf_op jit(solution)/shard_map/ppermute | solution.py:529
  28.1 2.8 %shard_map.53.refs_4_ = f32[2,160,640]{2,1,0:T(8,128)S(1)} custom-call(s32[5]{0:T(128)S(1)} %stack.27.info, bf16[2,4,192,256]{3,2,1,0:T(8,128)(2,1)S(1)} %shard_map.50.e, bf16[2,2,256,256]{3,2,1,0:T(8,128)(2,1)S(1)} %get-tuple-element.67.refs_0_.refs_6_, bf16[2,2,256,256]{3,2,1,0:T(8,128)(2,1)S(1)} %get-tuple-element.68.refs_1_.refs_7_, ...), custom_call_target="tpu_custom_call" | custom-call | flops 2000000000 | bytes 3325952 | tf_op jit(solution)/shard_map/pallas_call | solution.py:33
  31.0 1.1 %collective-permute-done.5.refs_4_.cols = f32[288,128]{1,0:T(8,128)S(1)} collective-permute-done((f32[288,128]{1,0:T(8,128)S(1)}, f32[288,128]{1,0:T(8,128)S(1)}, u32[]{:S(2)}, u32[]{:S(2)}) %collective-permute-start.5) | collective-permute-done | bytes 147488 | tf_op jit(solution)/shard_map/ppermute | solution.py:529
  32.0 0.6 shard_map.52
  32.7 4.8 %collective-permute-start.6 = (f32[320,128]{1,0:T(8,128)S(1)}, f32[320,128]{1,0:T(8,128)S(1)}, u32[]{:S(2)}, u32[]{:S(2)}) collective-permute-start(f32[320,128]{1,0:T(8,128)S(1)} %shard_map.52), channel_id=1, source_target_pairs={{0,2},{1,32},{32,1},{2,0},{3,34},{34,3},{4,6},{5,36},{36,5},{6,4},... | collective-permute-start | bytes 491528 | tf_op jit(solution)/shard_map/ppermute | solution.py:529
  37.5 2.8 %shard_map.55.refs_5_ = f32[2,160,640]{2,1,0:T(8,128)S(1)} custom-call(s32[5]{0:T(128)S(1)} %stack.27.info, bf16[2,4,192,256]{3,2,1,0:T(8,128)(2,1)S(1)} %shard_map.50.e, bf16[2,2,256,256]{3,2,1,0:T(8,128)(2,1)S(1)} %get-tuple-element.75.refs_0_.refs_14_.refs_9_, bf16[2,2,256,256]{3,2,1,0:T(8,128)(2,1)S(1)} %get-tuple-element.76.refs_1_.refs_15_.refs_10_, ...), custom_call_target="tpu_custom_call" | custom-call | flops 2000000000 | bytes 3325952 | tf_op jit(solution)/shard_map/pallas_call | solution.py:33
  40.3 1.6 %collective-permute-done.6.rows_in = f32[320,128]{1,0:T(8,128)S(1)} collective-permute-done((f32[320,128]{1,0:T(8,128)S(1)}, f32[320,128]{1,0:T(8,128)S(1)}, u32[]{:S(2)}, u32[]{:S(2)}) %collective-permute-start.6) | collective-permute-done | bytes 163872 | tf_op jit(solution)/shard_map/ppermute | solution.py:529
  41.9 0.0 copy-done.1
  41.9 0.0 copy-done.3
  41.9 0.0 copy-done.4
  42.0 0.0 copy-done.5
  42.1 4.5 %shard_map.56 = (f32[4,128,128]{2,1,0:T(8,128)S(1)}, f32[128,128]{1,0:T(8,128)S(1)}, f32[128,128]{1,0:T(8,128)S(1)}, f32[4,160,640]{2,1,0:T(8,128)}) custom-call(s32[5]{0:T(128)S(1)} %stack.27.info, f32[4,160,128]{2,1,0:T(8,128)S(1)} %get-tuple-element.46.main, f32[288,128]{1,0:T(8,128)S(1)} %collective-permute-done.5.refs_4_.cols, ...), custom_call_target="tpu_custom_call" | custom-call | flops 4000000000 | bytes 8716288 | tf_op jit(solution)/shard_map/pallas_call | solution.py:33
  46.6 3.1 %collective-permute-start.8 = (f32[128,128]{1,0:T(8,128)S(1)}, f32[128,128]{1,0:T(8,128)S(1)}, u32[]{:S(2)}, u32[]{:S(2)}) collective-permute-start(f32[128,128]{1,0:T(8,128)S(1)} %get-tuple-element.85), channel_id=1, source_target_pairs={{0,1},{1,0},{2,4},{4,2},{3,5},{5,3},{6,8},{8,6},{7,9},{9,7},{10,12... | collective-permute-start | bytes 196616 | tf_op jit(solution)/shard_map/ppermute | solution.py:529
  49.7 0.0 collective-permute-start.7
  49.7 2.6 %collective-permute-done.8.beyond = f32[128,128]{1,0:T(8,128)S(1)} collective-permute-done((f32[128,128]{1,0:T(8,128)S(1)}, f32[128,128]{1,0:T(8,128)S(1)}, u32[]{:S(2)}, u32[]{:S(2)}) %collective-permute-start.8) | collective-permute-done | bytes 65568 | tf_op jit(solution)/shard_map/ppermute | solution.py:529
  52.3 1.2 %collective-permute-done.7.inside = f32[128,128]{1,0:T(8,128)S(1)} collective-permute-done((f32[128,128]{1,0:T(8,128)S(1)}, f32[128,128]{1,0:T(8,128)S(1)}, u32[]{:S(2)}, u32[]{:S(2)}) %collective-permute-start.7) | collective-permute-done | bytes 65568 | tf_op jit(solution)/shard_map/ppermute | solution.py:532
  53.6 0.8 collective-permute-start.9
  54.4 2.8 %collective-permute-start.10 = (f32[6,32,128]{2,1,0:T(8,128)S(1)}, f32[6,32,128]{2,1,0:T(8,128)S(1)}, u32[]{:S(2)}, u32[]{:S(2)}) collective-permute-start(f32[6,32,128]{2,1,0:T(8,128)S(1)} %get-tuple-element.87), channel_id=1, source_target_pairs={{0,2},{1,32},{32,1},{2,0},{3,34},{34,3},{4,6},{5,36},{36,5},{6,4},... | collective-permute-start | bytes 294920 | tf_op jit(solution)/shard_map/ppermute | solution.py:529
  57.1 0.0 collective-permute-done.9.rows_in
  57.2 3.8 %collective-permute-done.10.rows_out = f32[6,32,128]{2,1,0:T(8,128)S(1)} collective-permute-done((f32[6,32,128]{2,1,0:T(8,128)S(1)}, f32[6,32,128]{2,1,0:T(8,128)S(1)}, u32[]{:S(2)}, u32[]{:S(2)}) %collective-permute-start.10) | collective-permute-done | bytes 98336 | tf_op jit(solution)/shard_map/ppermute | solution.py:529
  61.0 10.7 %shard_map.57 = f32[4,128,128]{2,1,0:T(8,128)S(1)} custom-call(s32[5]{0:T(128)S(1)} %stack.27.info, f32[4,128,128]{2,1,0:T(8,128)S(1)} %get-tuple-element.83.main, f32[128,128]{1,0:T(8,128)S(1)} %collective-permute-done.7.inside, f32[128,128]{1,0:T(8,128)S(1)} %collective-permute-done.8.beyond, f32[6,32,128]{2,1,0:T(8,128)S(1)} %collective-permute-done.9.rows_in, ...), custom_call_target="tpu_custom_call" | custom-call | flops 8000000000 | bytes 7307264 | tf_op jit(solution)/shard_map/pallas_call | solution.py:33
  71.7 0.1 collective-permute-start.12
  71.8 0.3 collective-permute-start.11
  72.1 7.6 %collective-permute-done.12 = f32[4,128,128]{2,1,0:T(8,128)S(1)} collective-permute-done((f32[4,128,128]{2,1,0:T(8,128)S(1)}, f32[4,128,128]{2,1,0:T(8,128)S(1)}, u32[]{:S(2)}, u32[]{:S(2)}) %collective-permute-start.12) | collective-permute-done | bytes 262176 | tf_op jit(solution)/shard_map/ppermute | solution.py:532
  79.6 0.8 %collective-permute-start.13 = (f32[4,128,128]{2,1,0:T(8,128)S(1)}, f32[4,128,128]{2,1,0:T(8,128)S(1)}, u32[]{:S(2)}, u32[]{:S(2)}) collective-permute-start(f32[4,128,128]{2,1,0:T(8,128)S(1)} %collective-permute-done.12), channel_id=1, source_target_pairs={{0,1},{1,0},{2,3},{3,2},{4,5},{5,4},{6,7},{7,6},{8,9},{9,8},{10,11... | collective-permute-start | bytes 786440 | tf_op jit(solution)/shard_map/ppermute | solution.py:532
  80.5 0.0 collective-permute-done.11
  80.5 1.2 %collective-permute-done.13 = f32[4,128,128]{2,1,0:T(8,128)S(1)} collective-permute-done((f32[4,128,128]{2,1,0:T(8,128)S(1)}, f32[4,128,128]{2,1,0:T(8,128)S(1)}, u32[]{:S(2)}, u32[]{:S(2)}) %collective-permute-start.13) | collective-permute-done | bytes 262176 | tf_op jit(solution)/shard_map/ppermute | solution.py:532
  81.6 0.1 broadcast_select_fusion.7
  81.7 1.0 %maximum_bitcast_fusion = f32[1,4,256,256]{3,2,1,0:T(8,128)} fusion(f32[4,128,128]{2,1,0:T(8,128)S(1)} %get-tuple-element.93, f32[4,128,128]{2,1,0:T(8,128)S(1)} %get-tuple-element.92, f32[4,128,128]{2,1,0:T(8,128)S(1)} %get-tuple-element.91, f32[4,128,128]{2,1,0:T(8,128)S(1)} %get-tuple-element.90), kind=kLoop, calls=%fused_computation | loop fusion | flops 786432 | bytes 2097152 | tf_op jit(solution)/shard_map/broadcast_in_dim | solution.py:661
  (16 shorter events, 0.1 us)
Async XLA Ops:
  0.0 4.5 %copy-start = (f32[1,4,256,256]{3,2,1,0:T(8,128)S(1)}, f32[1,4,256,256]{3,2,1,0:T(8,128)}, u32[]{:S(2)}) copy-start(f32[1,4,256,256]{3,2,1,0:T(8,128)} %param.4) | copy-start | bytes 3145732
  2.0 8.3 %collective-permute-start.1 = (f32[664,128]{1,0:T(8,128)S(1)}, f32[664,128]{1,0:T(8,128)S(1)}, u32[]{:S(2)}, u32[]{:S(2)}) collective-permute-start(f32[664,128]{1,0:T(8,128)S(1)} %get-tuple-element.50), channel_id=1, source_target_pairs={{0,1},{1,0},{2,3},{3,2},{4,5},{5,4},{6,7},{7,6},{8,9},{9,8},{10,11... | collective-permute-start | bytes 1019912 | tf_op jit(solution)/shard_map/ppermute | solution.py:532
  2.8 17.5 %collective-permute-start.3 = (f32[664,128]{1,0:T(8,128)S(1)}, f32[664,128]{1,0:T(8,128)S(1)}, u32[]{:S(2)}, u32[]{:S(2)}) collective-permute-start(f32[664,128]{1,0:T(8,128)S(1)} %get-tuple-element.60), channel_id=1, source_target_pairs={{0,2},{1,3},{2,0},{3,1},{4,6},{5,7},{6,4},{7,5},{8,10},{9,11},{10,... | collective-permute-start | bytes 1019912 | tf_op jit(solution)/shard_map/ppermute | solution.py:532
  4.4 15.9 %collective-permute-start.4 = (f32[664,128]{1,0:T(8,128)S(1)}, f32[664,128]{1,0:T(8,128)S(1)}, u32[]{:S(2)}, u32[]{:S(2)}) collective-permute-start(f32[664,128]{1,0:T(8,128)S(1)} %get-tuple-element.61), channel_id=1, source_target_pairs={{0,3},{1,2},{2,1},{3,0},{4,7},{5,6},{6,5},{7,4},{8,11},{9,10},{10,... | collective-permute-start | bytes 1019912 | tf_op jit(solution)/shard_map/ppermute | solution.py:532
  4.7 8.2 %collective-permute-start = (f32[160,128]{1,0:T(8,128)S(1)}, f32[160,128]{1,0:T(8,128)S(1)}, u32[]{:S(2)}, u32[]{:S(2)}) collective-permute-start(f32[160,128]{1,0:T(8,128)S(1)} %get-tuple-element.48), channel_id=1, source_target_pairs={{0,1},{1,0},{2,4},{4,2},{3,5},{5,3},{6,8},{8,6},{7,9},{9,7},{10,12... | collective-permute-start | bytes 245768 | tf_op jit(solution)/shard_map/ppermute | solution.py:529
  12.0 30.0 %copy-start.1 = (bf16[2,2,320,256]{3,2,1,0:T(8,128)(2,1)}, bf16[2,2,320,256]{3,2,1,0:T(8,128)(2,1)S(1)}, u32[]{:S(2)}) copy-start(bf16[2,2,320,256]{3,2,1,0:T(8,128)(2,1)S(1)} %get-tuple-element.71.refs_4_.refs_10_) | copy-start | bytes 1966084
  12.0 29.9 %copy-start.3 = (bf16[2,2,256,256]{3,2,1,0:T(8,128)(2,1)}, bf16[2,2,256,256]{3,2,1,0:T(8,128)(2,1)S(1)}, u32[]{:S(2)}) copy-start(bf16[2,2,256,256]{3,2,1,0:T(8,128)(2,1)S(1)} %get-tuple-element.67.refs_0_.refs_6_) | copy-start | bytes 1572868
  12.0 29.9 %copy-start.4 = (bf16[2,2,256,256]{3,2,1,0:T(8,128)(2,1)}, bf16[2,2,256,256]{3,2,1,0:T(8,128)(2,1)S(1)}, u32[]{:S(2)}) copy-start(bf16[2,2,256,256]{3,2,1,0:T(8,128)(2,1)S(1)} %get-tuple-element.68.refs_1_.refs_7_) | copy-start | bytes 1572868
  12.0 29.9 %copy-start.5 = (bf16[2,2,256,256]{3,2,1,0:T(8,128)(2,1)}, bf16[2,2,256,256]{3,2,1,0:T(8,128)(2,1)S(1)}, u32[]{:S(2)}) copy-start(bf16[2,2,256,256]{3,2,1,0:T(8,128)(2,1)S(1)} %get-tuple-element.72.refs_5_.refs_11_) | copy-start | bytes 1572868
  12.0 29.9 %copy-start.9 = (bf16[2,256,128]{2,1,0:T(8,128)(2,1)}, bf16[2,256,128]{2,1,0:T(8,128)(2,1)S(1)}, u32[]{:S(2)}) copy-start(bf16[2,256,128]{2,1,0:T(8,128)(2,1)S(1)} %get-tuple-element.69.refs_2_.refs_8_) | copy-start | bytes 393220
  12.0 29.9 %copy-start.10 = (bf16[2,256,128]{2,1,0:T(8,128)(2,1)}, bf16[2,256,128]{2,1,0:T(8,128)(2,1)S(1)}, u32[]{:S(2)}) copy-start(bf16[2,256,128]{2,1,0:T(8,128)(2,1)S(1)} %get-tuple-element.70.refs_3_.refs_9_) | copy-start | bytes 393220
  12.1 29.9 %copy-start.13 = (f32[2,2,16,128]{3,2,1,0:T(8,128)}, f32[2,2,16,128]{3,2,1,0:T(8,128)S(1)}, u32[]{:S(2)}) copy-start(f32[2,2,16,128]{3,2,1,0:T(8,128)S(1)} %get-tuple-element.74.refs_7_.refs_13_) | copy-start | bytes 98308
  12.1 29.9 %copy-start.15 = (f32[2,2,8,128]{3,2,1,0:T(8,128)}, f32[2,2,8,128]{3,2,1,0:T(8,128)S(1)}, u32[]{:S(2)}) copy-start(f32[2,2,8,128]{3,2,1,0:T(8,128)S(1)} %get-tuple-element.73.refs_6_.refs_12_) | copy-start | bytes 49156
  13.5 5.9 %collective-permute-start.2 = (f32[192,128]{1,0:T(8,128)S(1)}, f32[192,128]{1,0:T(8,128)S(1)}, u32[]{:S(2)}, u32[]{:S(2)}) collective-permute-start(f32[192,128]{1,0:T(8,128)S(1)} %shard_map.49), channel_id=1, source_target_pairs={{0,2},{1,32},{32,1},{2,0},{3,34},{34,3},{4,6},{5,36},{36,5},{6,4},... | collective-permute-start | bytes 294920 | tf_op jit(solution)/shard_map/ppermute | solution.py:529
  22.0 20.0 %copy-start.2 = (bf16[2,2,320,256]{3,2,1,0:T(8,128)(2,1)}, bf16[2,2,320,256]{3,2,1,0:T(8,128)(2,1)S(1)}, u32[]{:S(2)}) copy-start(bf16[2,2,320,256]{3,2,1,0:T(8,128)(2,1)S(1)} %get-tuple-element.79.refs_4_.refs_18_.refs_13_) | copy-start | bytes 1966084
  22.0 20.0 %copy-start.6 = (bf16[2,2,256,256]{3,2,1,0:T(8,128)(2,1)}, bf16[2,2,256,256]{3,2,1,0:T(8,128)(2,1)S(1)}, u32[]{:S(2)}) copy-start(bf16[2,2,256,256]{3,2,1,0:T(8,128)(2,1)S(1)} %get-tuple-element.75.refs_0_.refs_14_.refs_9_) | copy-start | bytes 1572868
  22.0 20.0 %copy-start.7 = (bf16[2,2,256,256]{3,2,1,0:T(8,128)(2,1)}, bf16[2,2,256,256]{3,2,1,0:T(8,128)(2,1)S(1)}, u32[]{:S(2)}) copy-start(bf16[2,2,256,256]{3,2,1,0:T(8,128)(2,1)S(1)} %get-tuple-element.76.refs_1_.refs_15_.refs_10_) | copy-start | bytes 1572868
  22.0 20.0 %copy-start.8 = (bf16[2,2,256,256]{3,2,1,0:T(8,128)(2,1)}, bf16[2,2,256,256]{3,2,1,0:T(8,128)(2,1)S(1)}, u32[]{:S(2)}) copy-start(bf16[2,2,256,256]{3,2,1,0:T(8,128)(2,1)S(1)} %get-tuple-element.80.refs_5_.refs_19_.refs_14_) | copy-start | bytes 1572868
  22.0 20.0 %copy-start.11 = (bf16[2,256,128]{2,1,0:T(8,128)(2,1)}, bf16[2,256,128]{2,1,0:T(8,128)(2,1)S(1)}, u32[]{:S(2)}) copy-start(bf16[2,256,128]{2,1,0:T(8,128)(2,1)S(1)} %get-tuple-element.77.refs_2_.refs_16_.refs_11_) | copy-start | bytes 393220
  22.0 20.0 %copy-start.12 = (bf16[2,256,128]{2,1,0:T(8,128)(2,1)}, bf16[2,256,128]{2,1,0:T(8,128)(2,1)S(1)}, u32[]{:S(2)}) copy-start(bf16[2,256,128]{2,1,0:T(8,128)(2,1)S(1)} %get-tuple-element.78.refs_3_.refs_17_.refs_12_) | copy-start | bytes 393220
  22.0 20.0 %copy-start.14 = (f32[2,2,16,128]{3,2,1,0:T(8,128)}, f32[2,2,16,128]{3,2,1,0:T(8,128)S(1)}, u32[]{:S(2)}) copy-start(f32[2,2,16,128]{3,2,1,0:T(8,128)S(1)} %get-tuple-element.82.refs_7_.refs_21_.refs_16_) | copy-start | bytes 98308
  22.0 20.0 %copy-start.16 = (f32[2,2,8,128]{3,2,1,0:T(8,128)}, f32[2,2,8,128]{3,2,1,0:T(8,128)S(1)}, u32[]{:S(2)}) copy-start(f32[2,2,8,128]{3,2,1,0:T(8,128)S(1)} %get-tuple-element.81.refs_6_.refs_20_.refs_15_) | copy-start | bytes 49156
  23.1 9.0 %collective-permute-start.5 = (f32[288,128]{1,0:T(8,128)S(1)}, f32[288,128]{1,0:T(8,128)S(1)}, u32[]{:S(2)}, u32[]{:S(2)}) collective-permute-start(f32[288,128]{1,0:T(8,128)S(1)} %shard_map.51), channel_id=1, source_target_pairs={{0,1},{1,0},{2,4},{4,2},{3,5},{5,3},{6,8},{8,6},{7,9},{9,7},{10,12... | collective-permute-start | bytes 442376 | tf_op jit(solution)/shard_map/ppermute | solution.py:529
  32.7 9.3 %collective-permute-start.6 = (f32[320,128]{1,0:T(8,128)S(1)}, f32[320,128]{1,0:T(8,128)S(1)}, u32[]{:S(2)}, u32[]{:S(2)}) collective-permute-start(f32[320,128]{1,0:T(8,128)S(1)} %shard_map.52), channel_id=1, source_target_pairs={{0,2},{1,32},{32,1},{2,0},{3,34},{34,3},{4,6},{5,36},{36,5},{6,4},... | collective-permute-start | bytes 491528 | tf_op jit(solution)/shard_map/ppermute | solution.py:529
  46.6 5.7 %collective-permute-start.8 = (f32[128,128]{1,0:T(8,128)S(1)}, f32[128,128]{1,0:T(8,128)S(1)}, u32[]{:S(2)}, u32[]{:S(2)}) collective-permute-start(f32[128,128]{1,0:T(8,128)S(1)} %get-tuple-element.85), channel_id=1, source_target_pairs={{0,1},{1,0},{2,4},{4,2},{3,5},{5,3},{6,8},{8,6},{7,9},{9,7},{10,12... | collective-permute-start | bytes 196616 | tf_op jit(solution)/shard_map/ppermute | solution.py:529
  49.7 3.8 %collective-permute-start.7 = (f32[128,128]{1,0:T(8,128)S(1)}, f32[128,128]{1,0:T(8,128)S(1)}, u32[]{:S(2)}, u32[]{:S(2)}) collective-permute-start(f32[128,128]{1,0:T(8,128)S(1)} %get-tuple-element.84), channel_id=1, source_target_pairs={{0,2},{1,3},{2,0},{3,1},{4,6},{5,7},{6,4},{7,5},{8,10},{9,11},{10,... | collective-permute-start | bytes 196616 | tf_op jit(solution)/shard_map/ppermute | solution.py:532
  53.6 3.6 %collective-permute-start.9 = (f32[6,32,128]{2,1,0:T(8,128)S(1)}, f32[6,32,128]{2,1,0:T(8,128)S(1)}, u32[]{:S(2)}, u32[]{:S(2)}) collective-permute-start(f32[6,32,128]{2,1,0:T(8,128)S(1)} %broadcast_select_fusion.9), channel_id=1, source_target_pairs={{0,1},{1,0},{2,3},{3,2},{4,5},{5,4},{6,7},{7,6},{8,9},{9,8},{10,11... | collective-permute-start | bytes 294920 | tf_op jit(solution)/shard_map/ppermute | solution.py:532
  54.4 6.6 %collective-permute-start.10 = (f32[6,32,128]{2,1,0:T(8,128)S(1)}, f32[6,32,128]{2,1,0:T(8,128)S(1)}, u32[]{:S(2)}, u32[]{:S(2)}) collective-permute-start(f32[6,32,128]{2,1,0:T(8,128)S(1)} %get-tuple-element.87), channel_id=1, source_target_pairs={{0,2},{1,32},{32,1},{2,0},{3,34},{34,3},{4,6},{5,36},{36,5},{6,4},... | collective-permute-start | bytes 294920 | tf_op jit(solution)/shard_map/ppermute | solution.py:529
  71.7 8.0 %collective-permute-start.12 = (f32[4,128,128]{2,1,0:T(8,128)S(1)}, f32[4,128,128]{2,1,0:T(8,128)S(1)}, u32[]{:S(2)}, u32[]{:S(2)}) collective-permute-start(f32[4,128,128]{2,1,0:T(8,128)S(1)} %shard_map.57), channel_id=1, source_target_pairs={{0,2},{1,3},{2,0},{3,1},{4,6},{5,7},{6,4},{7,5},{8,10},{9,11},{10,... | collective-permute-start | bytes 786440 | tf_op jit(solution)/shard_map/ppermute | solution.py:532
  71.8 8.7 %collective-permute-start.11 = (f32[4,128,128]{2,1,0:T(8,128)S(1)}, f32[4,128,128]{2,1,0:T(8,128)S(1)}, u32[]{:S(2)}, u32[]{:S(2)}) collective-permute-start(f32[4,128,128]{2,1,0:T(8,128)S(1)} %shard_map.57), channel_id=1, source_target_pairs={{0,1},{1,0},{2,3},{3,2},{4,5},{5,4},{6,7},{7,6},{8,9},{9,8},{10,11... | collective-permute-start | bytes 786440 | tf_op jit(solution)/shard_map/ppermute | solution.py:532
  79.6 2.0 %collective-permute-start.13 = (f32[4,128,128]{2,1,0:T(8,128)S(1)}, f32[4,128,128]{2,1,0:T(8,128)S(1)}, u32[]{:S(2)}, u32[]{:S(2)}) collective-permute-start(f32[4,128,128]{2,1,0:T(8,128)S(1)} %collective-permute-done.12), channel_id=1, source_target_pairs={{0,1},{1,0},{2,3},{3,2},{4,5},{5,4},{6,7},{7,6},{8,9},{9,8},{10,11... | collective-permute-start | bytes 786440 | tf_op jit(solution)/shard_map/ppermute | solution.py:532

commit v4 on v3

--- a/solution.py
+++ b/solution.py
@@ -17,34 +17,38 @@
 SMEM = pltpu.SMEM
 
 
-def call(body, outs, scratch, scalars, *args, flops=0, in_place=(), in_hbm=(), limit=24):
-    specs = [pl.BlockSpec(memory_space=SMEM)] * len(scalars)
-    specs += [
+def position():
+    tile, view = lax.axis_index("tile"), lax.axis_index("view")
+    qx, qy = lax.shift_right_logical(view, 1), jnp.bitwise_and(view, 1)
+    col, row = lax.rem(tile, GX), lax.div(tile, GX)
+    last = lax.axis_size("tile") // GX - 1
+    has_x = jnp.where(qx == 0, col, GX - 1 - col)
+    has_y = jnp.where(qy == 0, row, last - row)
+    return view, qx, qy, has_x, has_y
+
+
+def call(body, outs, scratch, *args, flops=0, in_place=(), kept_in=(), kept_out=(), limit=24):
+    specs = [
         pl.BlockSpec(memory_space=HBM if n in in_place else VMEM) for n in range(len(args))
     ]
-    args = [
-        pltpu.with_memory_space_constraint(a, HBM) if n in in_place else a
-        for n, a in enumerate(args)
-    ]
+    args = list(args)
+    for n in in_place:
+        args[n] = pltpu.with_memory_space_constraint(args[n], HBM)
+    for n in kept_in:
+        args[n] = pltpu.with_memory_space_constraint(args[n], VMEM)
     moved = sum(a.size * a.dtype.itemsize for a in args)
     leaves = [
-        HBM(a.shape, a.dtype) if n in in_hbm else a for n, a in enumerate(jax.tree.leaves(outs))
+        VMEM(a.shape, a.dtype) if n in kept_out else a for n, a in enumerate(jax.tree.leaves(outs))
     ]
     return pl.pallas_call(
-        body,
+        lambda *refs: body(position(), *refs),
         out_shape=jax.tree.unflatten(jax.tree.structure(outs), leaves),
         in_specs=specs,
-        out_specs=jax.tree.unflatten(
-            jax.tree.structure(outs),
-            [
-                pl.BlockSpec(memory_space=HBM if n in in_hbm else VMEM)
-                for n in range(len(jax.tree.leaves(outs)))
-            ],
-        ),
+        out_specs=jax.tree.map(lambda _: pl.BlockSpec(memory_space=VMEM), outs),
         scratch_shapes=scratch,
         compiler_params=pltpu.CompilerParams(vmem_limit_bytes=limit * 1024 * 1024),
         cost_estimate=pl.CostEstimate(flops=flops, bytes_accessed=moved, transcendentals=0),
-    )(*scalars, *args)
+    )(*args)
 
 
 def shape(*dims, dtype=F32):
@@ -99,7 +103,7 @@
     return both[:rows] + (both[rows:] + rest)
 
 
-def send_kernel(grid_rows, rec, table, variants, *refs):
+def send_kernel(grid_rows, info, rec, table, variants, *refs):
     sent, (raw, ids, whole, sems) = refs[:4], refs[4:]
     loads = [pltpu.make_async_copy(rec.at[z], whole.at[z], sems.at[z]) for z in range(4)]
     small = [
@@ -146,8 +150,8 @@
     return jnp.concatenate([jnp.where(mine, side, 0.0), low], 0)
 
 
-def start_kernel(first, main, inside, edge):
-    view = lax.axis_index("view")
+def start_kernel(info, first, main, inside, edge):
+    view = info[0]
     for q in range(4):
         qx, qy = q // 2, q % 2
 
@@ -362,18 +366,15 @@
 def forward_kernel(info, e, *refs):
     mats, refs = refs[:8], refs[8:]
     out, p = refs
-    clear(p, 192)
     far = far_mask(160, info[1])
-
-    def body(s, carry):
+    for s in range(2):
+        clear(p.at[s], 192)
+
         def put(where, value):
             out[s, :, where] = value
 
-        near, edge = forward(s, info[2], e, mats, p, put)
+        near, edge = forward(s, info[2], e, mats, p.at[s], put)
         out[s, :, 512:] = jnp.where(far, edge, near)
-        return carry
-
-    lax.fori_loop(0, 2, body, 0)
 
 
 def row_masks(info):
@@ -404,7 +405,7 @@
 def adjoint_kernel(info, main, cols, rows_in, *refs):
     got, blurs, refs = refs[:4], refs[4:6], refs[6:]
     groups, refs = (refs[:8], refs[8:16]), refs[16:]
-    out, near_edge, far_edge, kept, rec, r, total, sem = refs
+    out, near_edge, far_edge, rec, r, total = refs
     qx, qy = info[1], info[2]
     in_tile = pl.multiple_of(16 * (1 - qy), 16)
     out_tile = pl.multiple_of(144 * qy, 16)
@@ -417,37 +418,39 @@
         outer = cols[(s // 2) * 144 : (s // 2) * 144 + 144]
         rec[s, pl.ds(in_tile, 144), 512:] = both_sides(own_side(got[s], qx), outer, s % 2, qx)
         rec[s, pl.ds(out_tile, 16), 512:] = rows_in[256 + 16 * s : 272 + 16 * s]
-    keep = pltpu.make_async_copy(rec, kept, sem)
-    keep.start()
-    clear(r, 160)
+    for s in range(2):
+        clear(r.at[s], 160)
     total[...] = jnp.zeros_like(total)
     masks = row_masks(info)
     far = far_mask(128, qx)
     for pair in range(2):
         mats, blur = groups[pair], blurs[pair]
 
-        def body(s, carry):
+        for s in range(2):
             for a, b in ((0, 256), (256, 512), (512, 640)):
-                take_ratio(2 * pair + s, rec, r, masks, slice(a, b), blur[s, :, a:b])
-            planes, near, edge = adjoint(s, mats, r, total)
+                take_ratio(2 * pair + s, rec, r.at[s], masks, slice(a, b), blur[s, :, a:b])
+            planes, near, edge = adjoint(s, mats, r.at[s], total)
             finish(s, mats, planes, jnp.where(far, edge, near), total)
-            return carry
-
-        lax.fori_loop(0, 2, body, 0)
     at = pl.ds(pl.multiple_of(32 * qy, 32), 128)
     update(True, main, at, total, out, (near_edge, far_edge), qx)
-    keep.wait()
+
+
+def mid_rows_kernel(info, main, inside, beyond, near, far):
+    shown = (
+        *(main.at[z] for z in range(4)),
+        inside,
+        beyond,
+    )
+    for out, at in ((near, 96 - 96 * info[2]), (far, 96 * info[2])):
+        rows = pl.ds(pl.multiple_of(at, 32), 32)
+        for n in range(6):
+            piece = shown[n][rows]
+            out[n] = jnp.where(info[3] > 0, piece, 0.0) if n == 5 else piece
 
 
 def step_kernel(info, main, inside, beyond, rows_in, rows_out, *refs):
-    far_refs, (out, region, e, p, r, total), refs = refs[:17], refs[17:23], refs[23:]
-    near_refs, sems = refs[:17], refs[17]
-    loads = []
-    for n, (there, here) in enumerate(zip(far_refs, near_refs, strict=True)):
-        loads.append(pltpu.make_async_copy(there, here, sems.at[n]))
-    for n in (0, 1, 4, 6, 7, 8, 5, 2, 3, 9, 10, 13, 15, 16, 14, 11, 12):
-        loads[n].start()
-    groups, rec = (near_refs[:8], near_refs[9:]), near_refs[8]
+    rec, groups, refs = refs[0], (refs[1:9], refs[9:17]), refs[17:]
+    out, region, e, p, r, total = refs
     qx, qy = info[1], info[2]
     for z in range(4):
         region[z, 32:160] = main[z]
@@ -459,41 +462,28 @@
             info[4] > 0, rows_out[n], 0.0
         )
     spread(region, e, qx)
-    clear(p, 192)
-    clear(r, 160)
+    for s in range(2):
+        clear(p.at[s], 192)
+        clear(r.at[s], 160)
     total[...] = jnp.zeros_like(total)
     masks = row_masks(info)
     far160, far128 = far_mask(160, qx), far_mask(128, qx)
     for pair in range(2):
         mats = groups[pair]
-        early, late = ((0, 1, 4, 6, 7), (8, 5, 2, 3)) if pair == 0 else ((9, 10, 13, 15, 16), (14, 11, 12))
-        for n in early:
-            loads[n].wait()
-
-        def body(s, carry):
+        for s in range(2):
             slot = 2 * pair + s
 
             def put(where, value):
-                if where.start == 0:
-
-                    @pl.when(s == 0)
-                    def _():
-                        for n in late:
-                            loads[n].wait()
-
-                take_ratio(slot, rec, r, masks, where, value)
-
-            near, edge = forward(s, qy, e, mats, p, put)
+                take_ratio(slot, rec, r.at[s], masks, where, value)
+
+            near, edge = forward(s, qy, e, mats, p.at[s], put)
             put(slice(512, 640), jnp.where(far160, edge, near))
-            planes, near, edge = adjoint(s, mats, r, total)
+            planes, near, edge = adjoint(s, mats, r.at[s], total)
             finish(s, mats, planes, jnp.where(far128, edge, near), total)
-            return carry
-
-        lax.fori_loop(0, 2, body, 0)
     update(False, main, slice(0, 128), total, out, None, qx)
 
 
-def make_matrices(info, one, two):
+def make_matrices(one, two):
     return call(
         matrices_kernel,
         (
@@ -507,23 +497,16 @@
             shape(2, 2, 16, 128),
         ),
         [],
-        (info,),
         one,
         two,
         flops=1_000_000_000,
+        kept_out=range(8),
     )
 
 
 def per_device(initial, recorded, tap_table, variants):
-    tile = lax.axis_index("tile")
-    view = lax.axis_index("view")
     count_tiles = lax.axis_size("tile")
     grid_rows = count_tiles // GX
-    tile_row, tile_col = tile // GX, tile % GX
-    qx, qy = view // 2, view % 2
-    has_x = jnp.where(qx == 0, tile_col > 0, tile_col < GX - 1).astype(jnp.int32)
-    has_y = jnp.where(qy == 0, tile_row > 0, tile_row < grid_rows - 1).astype(jnp.int32)
-    info = jnp.stack([view, qx, qy, has_x, has_y])
 
     def route(x, pairs):
         return lax.ppermute(x, ("tile", "view"), pairs)
@@ -553,7 +536,6 @@
             VMEM((4, 256, 256), F32),
             pltpu.SemaphoreType.DMA((6,)),
         ],
-        (),
         recorded[0, 0],
         tap_table[0].transpose(1, 0, 2),
         variants,
@@ -564,53 +546,48 @@
         start_kernel,
         (shape(4, 160, 128), shape(160, 128), shape(160, 128)),
         [],
-        (),
         initial[0],
     )
     start_cols = route(edge, x_pairs)
-    mats = [make_matrices(info, *got[:2])]
+    mats = [make_matrices(*got[:2])]
     start_cols, mats[0] = lax.optimization_barrier((start_cols, mats[0]))
     start_rows = route(
-        call(start_rows_kernel, shape(192, 128), [], (info,), main, inside, start_cols), y_pairs
+        call(start_rows_kernel, shape(192, 128), [], main, inside, start_cols), y_pairs
     )
     e = call(
         region_kernel,
         shape(2, 4, 192, 256, dtype=BF16),
         [VMEM((6, 192, 128), F32)],
-        (info,),
         main,
         inside,
         start_cols,
         start_rows,
     )
     e, got = lax.optimization_barrier((e, got))
-    mats.append(make_matrices(info, *got[2:]))
+    mats.append(make_matrices(*got[2:]))
     blurs = [
         call(
             forward_kernel,
             shape(2, 160, 640),
-            [VMEM((2, 256, 640), BF16)],
-            (info,),
-            e,
+            [VMEM((2, 2, 256, 640), BF16)],
+                e,
             *group,
             flops=2_000_000_000,
+            kept_in=range(1, 9),
         )
         for group in mats
     ]
-    cols = route(call(pack_cols_kernel, shape(288, 128), [], (info,), *got), x_pairs)
-    rows = route(call(pack_rows_kernel, shape(320, 128), [], (info,), *got, cols), y_pairs)
+    cols = route(call(pack_cols_kernel, shape(288, 128), [], *got), x_pairs)
+    rows = route(call(pack_rows_kernel, shape(320, 128), [], *got, cols), y_pairs)
     quad = shape(4, 128, 128)
     flat = [*mats[0], *mats[1]]
     estimate, near_edge, far_edge, rec = call(
         adjoint_kernel,
         (quad, shape(128, 128), shape(128, 128), shape(4, 160, 640)),
         [
-            VMEM((4, 160, 640), F32),
-            VMEM((2, 256, 640), BF16),
+            VMEM((2, 2, 256, 640), BF16),
             VMEM((4, 128, 128), F32),
-            pltpu.SemaphoreType.DMA,
         ],
-        (info,),
         main,
         cols,
         rows,
@@ -618,39 +595,39 @@
         *blurs,
         *flat,
         flops=4_000_000_000,
-        in_hbm=(3,),
+        kept_in=range(9, 25),
+        kept_out=(3,),
     )
     for step in range(1, ITERS):
         inside = over_view(near_edge, 2)
         beyond = route(far_edge, x_pairs)
-        shown = jnp.where(has_x > 0, beyond, 0.0)
-        whole = jnp.concatenate([estimate, inside[None], shown[None]])
-        low, high = whole[:, :32], whole[:, 96:]
-        rows_in = over_view(jnp.where(qy == 0, high, low), 1)
-        rows_out = route(jnp.where(qy == 0, low, high), y_pairs)
-        far_args = [*mats[0], rec, *mats[1]]
+        near, far = call(
+            mid_rows_kernel, (shape(6, 32, 128),) * 2, [], estimate, inside, beyond
+        )
+        rows_in = over_view(near, 1)
+        rows_out = route(far, y_pairs)
         estimate = call(
             step_kernel,
             quad,
             [
                 VMEM((6, 192, 128), F32),
                 VMEM((2, 4, 192, 256), BF16),
-                VMEM((2, 256, 640), BF16),
-                VMEM((2, 256, 640), BF16),
+                VMEM((2, 2, 256, 640), BF16),
+                VMEM((2, 2, 256, 640), BF16),
                 VMEM((4, 128, 128), F32),
-                *(VMEM(a.shape, a.dtype) for a in far_args),
-                pltpu.SemaphoreType.DMA((17,)),
             ],
-            (info,),
-            estimate,
+                estimate,
             inside,
             beyond,
             rows_in,
             rows_out,
-            *far_args,
+            rec,
+            *flat,
             flops=8_000_000_000,
-            in_place=range(5, 22),
+            kept_in=range(5, 22),
         )
+    view = lax.axis_index("view")
+    qx, qy = view // 2, view % 2
     across, down = over_view(estimate, 2), over_view(estimate, 1)
     corner = over_view(across, 1)
     halves = []

time: 82.9 us -> 74.1 us (0.89)
  Pallas kernels: 29.5 us -> 19.3 us
  starting transfers between devices: 28.8 us -> 30.8 us
    pallas_call x12 -> x13, Pallas kernels: 29.5 us -> 19.3 us  [call(): pl.pallas_call(lambda *refs: body(position(), *refs), out_shape=jax.tree....]
    ppermute x8, waiting for transfers between devices: 9.97 us -> 5.26 us  [over_view(): return lax.ppermute(x, 'view', [(i, i ^ flip) for i in range(4)])]
    ppermute x6, waiting for transfers between devices: 12.8 us -> 17.1 us  [route(): return lax.ppermute(x, ('tile', 'view'), pairs)]
    ppermute x8, starting transfers between devices: 4.53 us -> 8.07 us  [over_view(): return lax.ppermute(x, 'view', [(i, i ^ flip) for i in range(4)])]
    ppermute x6, starting transfers between devices: 24.3 us -> 22.7 us  [route(): return lax.ppermute(x, ('tile', 'view'), pairs)]
  transfers between devices with their start and end apart: 14 -> 14, of which waited for: 9 -> 9; matrix products, arithmetic and copies ran while one was open for 0% -> 0% of each run, Pallas kernels for 11% -> 8%
where the time goes in v4:
time: 74.1 us; the launch traced here: 73.8 us
  starting transfers between devices  30.8 us (42%)
  waiting for transfers between devices  22.4 us (30%)
  Pallas kernels  19.3 us (26%)
  other arithmetic  1.14 us (2%)
    ppermute x6, starting transfers between devices, route(): return lax.ppermute(x, ('tile', 'view'), pairs)  22.7 us
    pallas_call x13, Pallas kernels, call(): pl.pallas_call(lambda *refs: body(position(), *refs), out_shape=jax.tree....  19.3 us
    ppermute x6, waiting for transfers between devices, route(): return lax.ppermute(x, ('tile', 'view'), pairs)  17.1 us
    ppermute x8, starting transfers between devices, over_view(): return lax.ppermute(x, 'view', [(i, i ^ flip) for i in range(4)])  8.07 us
    ppermute x8, waiting for transfers between devices, over_view(): return lax.ppermute(x, 'view', [(i, i ^ flip) for i in range(4)])  5.26 us
  transfers between devices with their start and end apart: 14, of which 9 were waited for; matrix products, arithmetic and copies ran while one was open for 0% of the time, Pallas kernels for 8%

profile of v4, /device:TPU:13, one launch (start us, length us, event | category | flops | bytes accessed | tf_op | source)
XLA Modules:
  0.0 73.8 jit_solution(8769171036433564585)
XLA Ops:
  0.0 0.0 copy-start
  0.0 2.0 %shard_map.47 = (f32[664,128]{1,0:T(8,128)S(1)}, f32[664,128]{1,0:T(8,128)S(1)}, f32[664,128]{1,0:T(8,128)S(1)}, f32[664,128]{1,0:T(8,128)S(1)}) custom-call(f32[4,256,256]{2,1,0:T(8,128)} %bitcast.8, f32[3,8,31]{2,1,0:T(8,128)} %bitcast.9, s32[1,64]{1,0:T(1,128)} %refs_2_.1), custom_call_target="tpu_custom_call" | custom-call | bytes 1051808 | tf_op jit(solution)/shard_map/pallas_call | solution.py:43
  2.0 0.8 %collective-permute-start.1 = (f32[664,128]{1,0:T(8,128)S(1)}, f32[664,128]{1,0:T(8,128)S(1)}, u32[]{:S(2)}, u32[]{:S(2)}) collective-permute-start(f32[664,128]{1,0:T(8,128)S(1)} %get-tuple-element.52), channel_id=1, source_target_pairs={{0,1},{1,0},{2,3},{3,2},{4,5},{5,4},{6,7},{7,6},{8,9},{9,8},{10,11... | collective-permute-start | bytes 1019912 | tf_op jit(solution)/shard_map/ppermute | solution.py:515
  2.8 1.7 %collective-permute-start.3 = (f32[664,128]{1,0:T(8,128)S(1)}, f32[664,128]{1,0:T(8,128)S(1)}, u32[]{:S(2)}, u32[]{:S(2)}) collective-permute-start(f32[664,128]{1,0:T(8,128)S(1)} %get-tuple-element.62), channel_id=1, source_target_pairs={{0,2},{1,3},{2,0},{3,1},{4,6},{5,7},{6,4},{7,5},{8,10},{9,11},{10,... | collective-permute-start | bytes 1019912 | tf_op jit(solution)/shard_map/ppermute | solution.py:515
  4.4 0.1 collective-permute-start.4
  4.5 0.0 copy-done
  4.5 0.2 shard_map.46
  4.7 5.5 %collective-permute-start = (f32[160,128]{1,0:T(8,128)S(1)}, f32[160,128]{1,0:T(8,128)S(1)}, u32[]{:S(2)}, u32[]{:S(2)}) collective-permute-start(f32[160,128]{1,0:T(8,128)S(1)} %get-tuple-element.50), channel_id=1, source_target_pairs={{0,1},{1,0},{2,4},{4,2},{3,5},{5,3},{6,8},{8,6},{7,9},{9,7},{10,12... | collective-permute-start | bytes 245768 | tf_op jit(solution)/shard_map/ppermute | solution.py:512
  10.2 0.0 collective-permute-done.1.refs_1_.refs_4_
  10.2 1.1 %shard_map.48 = (bf16[2,2,256,256]{3,2,1,0:T(8,128)(2,1)S(1)}, bf16[2,2,256,256]{3,2,1,0:T(8,128)(2,1)S(1)}, bf16[2,256,128]{2,1,0:T(8,128)(2,1)S(1)}, bf16[2,25...) custom-call(f32[664,128]{1,0:T(8,128)S(1)} %get-tuple-element.64.ref, ...), custom_call_target="tpu_custom_call" | custom-call | flops 1000000000 | bytes 679936 | tf_op jit(solution)/shard_map/pallas_call | solution.py:43
  11.4 2.0 %collective-permute-done.refs_2_ = f32[160,128]{1,0:T(8,128)S(1)} collective-permute-done((f32[160,128]{1,0:T(8,128)S(1)}, f32[160,128]{1,0:T(8,128)S(1)}, u32[]{:S(2)}, u32[]{:S(2)}) %collective-permute-start) | collective-permute-done | bytes 81952 | tf_op jit(solution)/shard_map/ppermute | solution.py:512
  13.4 2.5 %collective-permute-start.2 = (f32[192,128]{1,0:T(8,128)S(1)}, f32[192,128]{1,0:T(8,128)S(1)}, u32[]{:S(2)}, u32[]{:S(2)}) collective-permute-start(f32[192,128]{1,0:T(8,128)S(1)} %shard_map.49), channel_id=1, source_target_pairs={{0,2},{1,32},{32,1},{2,0},{3,34},{34,3},{4,6},{5,36},{36,5},{6,4},... | collective-permute-start | bytes 294920 | tf_op jit(solution)/shard_map/ppermute | solution.py:512
  15.9 3.1 %collective-permute-done.2.refs_3_ = f32[192,128]{1,0:T(8,128)S(1)} collective-permute-done((f32[192,128]{1,0:T(8,128)S(1)}, f32[192,128]{1,0:T(8,128)S(1)}, u32[]{:S(2)}, u32[]{:S(2)}) %collective-permute-start.2) | collective-permute-done | bytes 98336 | tf_op jit(solution)/shard_map/ppermute | solution.py:512
  19.1 0.4 shard_map.50.refs_0_
  19.4 0.0 collective-permute-done.3.refs_2_.refs_0_.refs_5_
  19.4 0.8 %collective-permute-done.4.refs_3_.refs_1_.refs_6_ = f32[664,128]{1,0:T(8,128)S(1)} collective-permute-done((f32[664,128]{1,0:T(8,128)S(1)}, f32[664,128]{1,0:T(8,128)S(1)}, u32[]{:S(2)}, u32[]{:S(2)}) %collective-permute-start.4) | collective-permute-done | bytes 340000 | tf_op jit(solution)/shard_map/ppermute | solution.py:515
  20.2 1.1 %shard_map.54 = (bf16[2,2,256,256]{3,2,1,0:T(8,128)(2,1)S(1)}, bf16[2,2,256,256]{3,2,1,0:T(8,128)(2,1)S(1)}, bf16[2,256,128]{2,1,0:T(8,128)(2,1)S(1)}, bf16[2,25...) custom-call(f32[664,128]{1,0:T(8,128)S(1)} %collective-permute-done., ...), custom_call_target="tpu_custom_call" | custom-call | flops 1000000000 | bytes 679936 | tf_op jit(solution)/shard_map/pallas_call | solution.py:43
  21.3 0.5 shard_map.51
  21.9 5.1 %collective-permute-start.5 = (f32[288,128]{1,0:T(8,128)S(1)}, f32[288,128]{1,0:T(8,128)S(1)}, u32[]{:S(2)}, u32[]{:S(2)}) collective-permute-start(f32[288,128]{1,0:T(8,128)S(1)} %shard_map.51), channel_id=1, source_target_pairs={{0,1},{1,0},{2,4},{4,2},{3,5},{5,3},{6,8},{8,6},{7,9},{9,7},{10,12... | collective-permute-start | bytes 442376 | tf_op jit(solution)/shard_map/ppermute | solution.py:512
  27.0 1.9 %shard_map.55.refs_8_ = f32[2,160,640]{2,1,0:T(8,128)S(1)} custom-call(bf16[2,4,192,256]{3,2,1,0:T(8,128)(2,1)S(1)} %shard_map.50.refs_0_, bf16[2,2,256,256]{3,2,1,0:T(8,128)(2,1)S(1)} %get-tuple-element.77.refs_1_.refs_17_.refs_14_, bf16[2,2,256,256]{3,2,1,0:T(8,128)(2,1)S(1)} %get-tuple-element.78.refs_2_.refs_18_.refs_15_, ...), custom_call_target="tpu_custom_call" | custom-call | flops 2000000000 | bytes 3325952 | tf_op jit(solution)/shard_map/pallas_call | solution.py:43
  28.9 2.8 %collective-permute-done.5.refs_4_.refs_1_ = f32[288,128]{1,0:T(8,128)S(1)} collective-permute-done((f32[288,128]{1,0:T(8,128)S(1)}, f32[288,128]{1,0:T(8,128)S(1)}, u32[]{:S(2)}, u32[]{:S(2)}) %collective-permute-start.5) | collective-permute-done | bytes 147488 | tf_op jit(solution)/shard_map/ppermute | solution.py:512
  31.6 0.1 shard_map.52
  31.7 3.0 %collective-permute-start.6 = (f32[320,128]{1,0:T(8,128)S(1)}, f32[320,128]{1,0:T(8,128)S(1)}, u32[]{:S(2)}, u32[]{:S(2)}) collective-permute-start(f32[320,128]{1,0:T(8,128)S(1)} %shard_map.52), channel_id=1, source_target_pairs={{0,2},{1,32},{32,1},{2,0},{3,34},{34,3},{4,6},{5,36},{36,5},{6,4},... | collective-permute-start | bytes 491528 | tf_op jit(solution)/shard_map/ppermute | solution.py:512
  34.7 1.9 %shard_map.53.refs_7_ = f32[2,160,640]{2,1,0:T(8,128)S(1)} custom-call(bf16[2,4,192,256]{3,2,1,0:T(8,128)(2,1)S(1)} %shard_map.50.refs_0_, bf16[2,2,256,256]{3,2,1,0:T(8,128)(2,1)S(1)} %get-tuple-element.69.refs_1_.refs_9_.refs_6_, bf16[2,2,256,256]{3,2,1,0:T(8,128)(2,1)S(1)} %get-tuple-element.70.refs_2_.refs_10_.refs_7_, ...), custom_call_target="tpu_custom_call" | custom-call | flops 2000000000 | bytes 3325952 | tf_op jit(solution)/shard_map/pallas_call | solution.py:43
  36.6 3.5 %collective-permute-done.6.refs_2_ = f32[320,128]{1,0:T(8,128)S(1)} collective-permute-done((f32[320,128]{1,0:T(8,128)S(1)}, f32[320,128]{1,0:T(8,128)S(1)}, u32[]{:S(2)}, u32[]{:S(2)}) %collective-permute-start.6) | collective-permute-done | bytes 163872 | tf_op jit(solution)/shard_map/ppermute | solution.py:512
  40.1 3.2 %shard_map.56 = (f32[4,128,128]{2,1,0:T(8,128)S(1)}, f32[128,128]{1,0:T(8,128)S(1)}, f32[128,128]{1,0:T(8,128)S(1)}, f32[4,160,640]{2,1,0:T(8,128)S(1)}) custom-call(f32[4,160,128]{2,1,0:T(8,128)S(1)} %get-tuple-element.48.refs_0_, f32[288,128]{1,0:T(8,128)S(1)} %collective-permute-done.5.refs_4_.refs_1_, f32[320,128]{1,0:T(8,128)S(1)} %collective-permute-done.6.refs_2_, ...), custom_call_target="tpu_custom_call" | custom-call | flops 4000000000 | bytes 8716288 | tf_op jit(solution)/shard_map/pallas_call | solution.py:43
  43.3 0.1 collective-permute-start.7
  43.4 4.0 %collective-permute-start.8 = (f32[128,128]{1,0:T(8,128)S(1)}, f32[128,128]{1,0:T(8,128)S(1)}, u32[]{:S(2)}, u32[]{:S(2)}) collective-permute-start(f32[128,128]{1,0:T(8,128)S(1)} %get-tuple-element.87), channel_id=1, source_target_pairs={{0,1},{1,0},{2,4},{4,2},{3,5},{5,3},{6,8},{8,6},{7,9},{9,7},{10,12... | collective-permute-start | bytes 196616 | tf_op jit(solution)/shard_map/ppermute | solution.py:512
  47.4 0.0 collective-permute-done.7.refs_1_
  47.4 2.8 %collective-permute-done.8.refs_2_ = f32[128,128]{1,0:T(8,128)S(1)} collective-permute-done((f32[128,128]{1,0:T(8,128)S(1)}, f32[128,128]{1,0:T(8,128)S(1)}, u32[]{:S(2)}, u32[]{:S(2)}) %collective-permute-start.8) | collective-permute-done | bytes 65568 | tf_op jit(solution)/shard_map/ppermute | solution.py:512
  50.2 2.7 %collective-permute-start.10 = (f32[6,32,128]{2,1,0:T(8,128)S(1)}, f32[6,32,128]{2,1,0:T(8,128)S(1)}, u32[]{:S(2)}, u32[]{:S(2)}) collective-permute-start(f32[6,32,128]{2,1,0:T(8,128)S(1)} %get-tuple-element.89), channel_id=1, source_target_pairs={{0,2},{1,32},{32,1},{2,0},{3,34},{34,3},{4,6},{5,36},{36,5},{6,4},... | collective-permute-start | bytes 294920 | tf_op jit(solution)/shard_map/ppermute | solution.py:512
  52.9 0.0 collective-permute-start.9
  52.9 3.0 %collective-permute-done.10.refs_4_ = f32[6,32,128]{2,1,0:T(8,128)S(1)} collective-permute-done((f32[6,32,128]{2,1,0:T(8,128)S(1)}, f32[6,32,128]{2,1,0:T(8,128)S(1)}, u32[]{:S(2)}, u32[]{:S(2)}) %collective-permute-start.10) | collective-permute-done | bytes 98336 | tf_op jit(solution)/shard_map/ppermute | solution.py:512
  55.8 0.0 collective-permute-done.9.refs_3_
  55.8 6.8 %shard_map.58 = f32[4,128,128]{2,1,0:T(8,128)S(1)} custom-call(f32[4,128,128]{2,1,0:T(8,128)S(1)} %get-tuple-element.85.refs_0_, f32[128,128]{1,0:T(8,128)S(1)} %collective-permute-done.7.refs_1_, f32[128,128]{1,0:T(8,128)S(1)} %collective-permute-done.8.refs_2_, f32[6,32,128]{2,1,0:T(8,128)S(1)} %collective-permute-done.9.refs_3_, ...), custom_call_target="tpu_custom_call" | custom-call | flops 8000000000 | bytes 7307264 | tf_op jit(solution)/shard_map/pallas_call | solution.py:43
  62.7 0.1 collective-permute-start.12
  62.8 2.3 %collective-permute-start.11 = (f32[4,128,128]{2,1,0:T(8,128)S(1)}, f32[4,128,128]{2,1,0:T(8,128)S(1)}, u32[]{:S(2)}, u32[]{:S(2)}) collective-permute-start(f32[4,128,128]{2,1,0:T(8,128)S(1)} %shard_map.58), channel_id=1, source_target_pairs={{0,1},{1,0},{2,3},{3,2},{4,5},{5,4},{6,7},{7,6},{8,9},{9,8},{10,11... | collective-permute-start | bytes 786440 | tf_op jit(solution)/shard_map/ppermute | solution.py:515
  65.1 3.3 %collective-permute-done.12 = f32[4,128,128]{2,1,0:T(8,128)S(1)} collective-permute-done((f32[4,128,128]{2,1,0:T(8,128)S(1)}, f32[4,128,128]{2,1,0:T(8,128)S(1)}, u32[]{:S(2)}, u32[]{:S(2)}) %collective-permute-start.12) | collective-permute-done | bytes 262176 | tf_op jit(solution)/shard_map/ppermute | solution.py:515
  68.4 3.1 %collective-permute-start.13 = (f32[4,128,128]{2,1,0:T(8,128)S(1)}, f32[4,128,128]{2,1,0:T(8,128)S(1)}, u32[]{:S(2)}, u32[]{:S(2)}) collective-permute-start(f32[4,128,128]{2,1,0:T(8,128)S(1)} %collective-permute-done.12), channel_id=1, source_target_pairs={{0,1},{1,0},{2,3},{3,2},{4,5},{5,4},{6,7},{7,6},{8,9},{9,8},{10,11... | collective-permute-start | bytes 786440 | tf_op jit(solution)/shard_map/ppermute | solution.py:515
  71.5 0.0 collective-permute-done.11
  71.5 1.2 %collective-permute-done.13 = f32[4,128,128]{2,1,0:T(8,128)S(1)} collective-permute-done((f32[4,128,128]{2,1,0:T(8,128)S(1)}, f32[4,128,128]{2,1,0:T(8,128)S(1)}, u32[]{:S(2)}, u32[]{:S(2)}) %collective-permute-start.13) | collective-permute-done | bytes 262176 | tf_op jit(solution)/shard_map/ppermute | solution.py:515
  72.7 0.1 broadcast_select_fusion.7
  72.8 1.0 %maximum_bitcast_fusion = f32[1,4,256,256]{3,2,1,0:T(8,128)} fusion(f32[4,128,128]{2,1,0:T(8,128)S(1)} %get-tuple-element.94, f32[4,128,128]{2,1,0:T(8,128)S(1)} %get-tuple-element.93, f32[4,128,128]{2,1,0:T(8,128)S(1)} %get-tuple-element.92, f32[4,128,128]{2,1,0:T(8,128)S(1)} %get-tuple-element.91), kind=kLoop, calls=%fused_computation | loop fusion | flops 786432 | bytes 2097152 | tf_op jit(solution)/shard_map/broadcast_in_dim | solution.py:638
  (2 shorter events, 0.0 us)
Async XLA Ops:
  0.0 4.5 %copy-start = (f32[1,4,256,256]{3,2,1,0:T(8,128)S(1)}, f32[1,4,256,256]{3,2,1,0:T(8,128)}, u32[]{:S(2)}) copy-start(f32[1,4,256,256]{3,2,1,0:T(8,128)} %param.4) | copy-start | bytes 3145732
  2.0 8.2 %collective-permute-start.1 = (f32[664,128]{1,0:T(8,128)S(1)}, f32[664,128]{1,0:T(8,128)S(1)}, u32[]{:S(2)}, u32[]{:S(2)}) collective-permute-start(f32[664,128]{1,0:T(8,128)S(1)} %get-tuple-element.52), channel_id=1, source_target_pairs={{0,1},{1,0},{2,3},{3,2},{4,5},{5,4},{6,7},{7,6},{8,9},{9,8},{10,11... | collective-permute-start | bytes 1019912 | tf_op jit(solution)/shard_map/ppermute | solution.py:515
  2.8 16.7 %collective-permute-start.3 = (f32[664,128]{1,0:T(8,128)S(1)}, f32[664,128]{1,0:T(8,128)S(1)}, u32[]{:S(2)}, u32[]{:S(2)}) collective-permute-start(f32[664,128]{1,0:T(8,128)S(1)} %get-tuple-element.62), channel_id=1, source_target_pairs={{0,2},{1,3},{2,0},{3,1},{4,6},{5,7},{6,4},{7,5},{8,10},{9,11},{10,... | collective-permute-start | bytes 1019912 | tf_op jit(solution)/shard_map/ppermute | solution.py:515
  4.4 15.8 %collective-permute-start.4 = (f32[664,128]{1,0:T(8,128)S(1)}, f32[664,128]{1,0:T(8,128)S(1)}, u32[]{:S(2)}, u32[]{:S(2)}) collective-permute-start(f32[664,128]{1,0:T(8,128)S(1)} %get-tuple-element.63), channel_id=1, source_target_pairs={{0,3},{1,2},{2,1},{3,0},{4,7},{5,6},{6,5},{7,4},{8,11},{9,10},{10,... | collective-permute-start | bytes 1019912 | tf_op jit(solution)/shard_map/ppermute | solution.py:515
  4.7 8.7 %collective-permute-start = (f32[160,128]{1,0:T(8,128)S(1)}, f32[160,128]{1,0:T(8,128)S(1)}, u32[]{:S(2)}, u32[]{:S(2)}) collective-permute-start(f32[160,128]{1,0:T(8,128)S(1)} %get-tuple-element.50), channel_id=1, source_target_pairs={{0,1},{1,0},{2,4},{4,2},{3,5},{5,3},{6,8},{8,6},{7,9},{9,7},{10,12... | collective-permute-start | bytes 245768 | tf_op jit(solution)/shard_map/ppermute | solution.py:512
  13.4 5.6 %collective-permute-start.2 = (f32[192,128]{1,0:T(8,128)S(1)}, f32[192,128]{1,0:T(8,128)S(1)}, u32[]{:S(2)}, u32[]{:S(2)}) collective-permute-start(f32[192,128]{1,0:T(8,128)S(1)} %shard_map.49), channel_id=1, source_target_pairs={{0,2},{1,32},{32,1},{2,0},{3,34},{34,3},{4,6},{5,36},{36,5},{6,4},... | collective-permute-start | bytes 294920 | tf_op jit(solution)/shard_map/ppermute | solution.py:512
  21.9 9.8 %collective-permute-start.5 = (f32[288,128]{1,0:T(8,128)S(1)}, f32[288,128]{1,0:T(8,128)S(1)}, u32[]{:S(2)}, u32[]{:S(2)}) collective-permute-start(f32[288,128]{1,0:T(8,128)S(1)} %shard_map.51), channel_id=1, source_target_pairs={{0,1},{1,0},{2,4},{4,2},{3,5},{5,3},{6,8},{8,6},{7,9},{9,7},{10,12... | collective-permute-start | bytes 442376 | tf_op jit(solution)/shard_map/ppermute | solution.py:512
  31.7 8.4 %collective-permute-start.6 = (f32[320,128]{1,0:T(8,128)S(1)}, f32[320,128]{1,0:T(8,128)S(1)}, u32[]{:S(2)}, u32[]{:S(2)}) collective-permute-start(f32[320,128]{1,0:T(8,128)S(1)} %shard_map.52), channel_id=1, source_target_pairs={{0,2},{1,32},{32,1},{2,0},{3,34},{34,3},{4,6},{5,36},{36,5},{6,4},... | collective-permute-start | bytes 491528 | tf_op jit(solution)/shard_map/ppermute | solution.py:512
  43.3 4.1 %collective-permute-start.7 = (f32[128,128]{1,0:T(8,128)S(1)}, f32[128,128]{1,0:T(8,128)S(1)}, u32[]{:S(2)}, u32[]{:S(2)}) collective-permute-start(f32[128,128]{1,0:T(8,128)S(1)} %get-tuple-element.86), channel_id=1, source_target_pairs={{0,2},{1,3},{2,0},{3,1},{4,6},{5,7},{6,4},{7,5},{8,10},{9,11},{10,... | collective-permute-start | bytes 196616 | tf_op jit(solution)/shard_map/ppermute | solution.py:515
  43.4 6.7 %collective-permute-start.8 = (f32[128,128]{1,0:T(8,128)S(1)}, f32[128,128]{1,0:T(8,128)S(1)}, u32[]{:S(2)}, u32[]{:S(2)}) collective-permute-start(f32[128,128]{1,0:T(8,128)S(1)} %get-tuple-element.87), channel_id=1, source_target_pairs={{0,1},{1,0},{2,4},{4,2},{3,5},{5,3},{6,8},{8,6},{7,9},{9,7},{10,12... | collective-permute-start | bytes 196616 | tf_op jit(solution)/shard_map/ppermute | solution.py:512
  50.2 5.6 %collective-permute-start.10 = (f32[6,32,128]{2,1,0:T(8,128)S(1)}, f32[6,32,128]{2,1,0:T(8,128)S(1)}, u32[]{:S(2)}, u32[]{:S(2)}) collective-permute-start(f32[6,32,128]{2,1,0:T(8,128)S(1)} %get-tuple-element.89), channel_id=1, source_target_pairs={{0,2},{1,32},{32,1},{2,0},{3,34},{34,3},{4,6},{5,36},{36,5},{6,4},... | collective-permute-start | bytes 294920 | tf_op jit(solution)/shard_map/ppermute | solution.py:512
  52.9 3.0 %collective-permute-start.9 = (f32[6,32,128]{2,1,0:T(8,128)S(1)}, f32[6,32,128]{2,1,0:T(8,128)S(1)}, u32[]{:S(2)}, u32[]{:S(2)}) collective-permute-start(f32[6,32,128]{2,1,0:T(8,128)S(1)} %get-tuple-element.88), channel_id=1, source_target_pairs={{0,1},{1,0},{2,3},{3,2},{4,5},{5,4},{6,7},{7,6},{8,9},{9,8},{10,11... | collective-permute-start | bytes 294920 | tf_op jit(solution)/shard_map/ppermute | solution.py:515
  62.7 5.7 %collective-permute-start.12 = (f32[4,128,128]{2,1,0:T(8,128)S(1)}, f32[4,128,128]{2,1,0:T(8,128)S(1)}, u32[]{:S(2)}, u32[]{:S(2)}) collective-permute-start(f32[4,128,128]{2,1,0:T(8,128)S(1)} %shard_map.58), channel_id=1, source_target_pairs={{0,2},{1,3},{2,0},{3,1},{4,6},{5,7},{6,4},{7,5},{8,10},{9,11},{10,... | collective-permute-start | bytes 786440 | tf_op jit(solution)/shard_map/ppermute | solution.py:515
  62.8 8.7 %collective-permute-start.11 = (f32[4,128,128]{2,1,0:T(8,128)S(1)}, f32[4,128,128]{2,1,0:T(8,128)S(1)}, u32[]{:S(2)}, u32[]{:S(2)}) collective-permute-start(f32[4,128,128]{2,1,0:T(8,128)S(1)} %shard_map.58), channel_id=1, source_target_pairs={{0,1},{1,0},{2,3},{3,2},{4,5},{5,4},{6,7},{7,6},{8,9},{9,8},{10,11... | collective-permute-start | bytes 786440 | tf_op jit(solution)/shard_map/ppermute | solution.py:515
  68.4 4.3 %collective-permute-start.13 = (f32[4,128,128]{2,1,0:T(8,128)S(1)}, f32[4,128,128]{2,1,0:T(8,128)S(1)}, u32[]{:S(2)}, u32[]{:S(2)}) collective-permute-start(f32[4,128,128]{2,1,0:T(8,128)S(1)} %collective-permute-done.12), channel_id=1, source_target_pairs={{0,1},{1,0},{2,3},{3,2},{4,5},{5,4},{6,7},{7,6},{8,9},{9,8},{10,11... | collective-permute-start | bytes 786440 | tf_op jit(solution)/shard_map/ppermute | solution.py:515

commit v5 on v4

--- a/solution.py
+++ b/solution.py
@@ -27,7 +27,7 @@
     return view, qx, qy, has_x, has_y
 
 
-def call(body, outs, scratch, *args, flops=0, in_place=(), kept_in=(), kept_out=(), limit=24):
+def call(body, outs, scratch, *args, flops=0, in_place=(), kept_in=(), kept_out=(), after=None, limit=24):
     specs = [
         pl.BlockSpec(memory_space=HBM if n in in_place else VMEM) for n in range(len(args))
     ]
@@ -36,6 +36,14 @@
         args[n] = pltpu.with_memory_space_constraint(args[n], HBM)
     for n in kept_in:
         args[n] = pltpu.with_memory_space_constraint(args[n], VMEM)
+    plain = body
+    if after is not None:
+        specs.append(pl.BlockSpec(memory_space=pl.ANY))
+        args.append(after)
+
+        def body(info, *refs):
+            plain(info, *refs[: len(args) - 1], *refs[len(args) :])
+
     moved = sum(a.size * a.dtype.itemsize for a in args)
     leaves = [
         VMEM(a.shape, a.dtype) if n in kept_out else a for n, a in enumerate(jax.tree.leaves(outs))
@@ -363,18 +371,17 @@
     ref[:, first:] = jnp.zeros((2, 256 - first, 640), BF16)
 
 
-def forward_kernel(info, e, *refs):
-    mats, refs = refs[:8], refs[8:]
-    out, p = refs
+def forward_kernel(parts, info, e, *refs):
+    groups, (out, p) = (refs[:8], refs[8:-2]), refs[-2:]
     far = far_mask(160, info[1])
-    for s in range(2):
-        clear(p.at[s], 192)
+    for n, (group, s) in enumerate(parts):
+        clear(p.at[n], 192)
 
         def put(where, value):
-            out[s, :, where] = value
-
-        near, edge = forward(s, info[2], e, mats, p.at[s], put)
-        out[s, :, 512:] = jnp.where(far, edge, near)
+            out[n, :, where] = value
+
+        near, edge = forward(s, info[2], e, groups[group], p.at[n], put)
+        out[n, :, 512:] = jnp.where(far, edge, near)
 
 
 def row_masks(info):
@@ -424,11 +431,13 @@
     masks = row_masks(info)
     far = far_mask(128, qx)
     for pair in range(2):
-        mats, blur = groups[pair], blurs[pair]
+        mats = groups[pair]
 
         for s in range(2):
             for a, b in ((0, 256), (256, 512), (512, 640)):
-                take_ratio(2 * pair + s, rec, r.at[s], masks, slice(a, b), blur[s, :, a:b])
+                slot = 2 * pair + s
+                blurred = blurs[1][slot - 1, :, a:b] if slot else blurs[0][0, :, a:b]
+                take_ratio(slot, rec, r.at[s], masks, slice(a, b), blurred)
             planes, near, edge = adjoint(s, mats, r.at[s], total)
             finish(s, mats, planes, jnp.where(far, edge, near), total)
     at = pl.ds(pl.multiple_of(32 * qy, 32), 128)
@@ -483,7 +492,7 @@
     update(False, main, slice(0, 128), total, out, None, qx)
 
 
-def make_matrices(one, two):
+def make_matrices(one, two, after=None):
     return call(
         matrices_kernel,
         (
@@ -501,6 +510,7 @@
         two,
         flops=1_000_000_000,
         kept_out=range(8),
+        after=after,
     )
 
 
@@ -563,22 +573,26 @@
         start_cols,
         start_rows,
     )
-    e, got = lax.optimization_barrier((e, got))
-    mats.append(make_matrices(*got[2:]))
-    blurs = [
-        call(
-            forward_kernel,
-            shape(2, 160, 640),
-            [VMEM((2, 2, 256, 640), BF16)],
-                e,
-            *group,
-            flops=2_000_000_000,
-            kept_in=range(1, 9),
+
+    def blur(parts, after, *groups):
+        return call(
+            functools.partial(forward_kernel, parts),
+            shape(len(parts), 160, 640),
+            [VMEM((len(parts), 2, 256, 640), BF16)],
+            e,
+            *groups,
+            flops=1_000_000_000 * len(parts),
+            kept_in=range(1, 1 + len(groups)),
+            after=after,
         )
-        for group in mats
-    ]
-    cols = route(call(pack_cols_kernel, shape(288, 128), [], *got), x_pairs)
-    rows = route(call(pack_rows_kernel, shape(320, 128), [], *got, cols), y_pairs)
+
+    packed_cols = call(pack_cols_kernel, shape(288, 128), [], *got, after=e)
+    cols = route(packed_cols, x_pairs)
+    mats.append(make_matrices(*got[2:], after=packed_cols))
+    blurs = [blur(((0, 0),), packed_cols, *mats[0])]
+    packed_rows = call(pack_rows_kernel, shape(320, 128), [], *got, cols, after=blurs[0])
+    rows = route(packed_rows, y_pairs)
+    blurs.append(blur(((0, 1), (1, 0), (1, 1)), packed_rows, *mats[0], *mats[1]))
     quad = shape(4, 128, 128)
     flat = [*mats[0], *mats[1]]
     estimate, near_edge, far_edge, rec = call(
@@ -630,12 +644,12 @@
     qx, qy = view // 2, view % 2
     across, down = over_view(estimate, 2), over_view(estimate, 1)
     corner = over_view(across, 1)
-    halves = []
-    for y in range(2):
-        near, far = jnp.where(qy == y, estimate, down), jnp.where(qy == y, across, corner)
-        left, right = jnp.where(qx == 0, near, far), jnp.where(qx == 0, far, near)
-        halves.append(jnp.concatenate([left, right], 2))
-    return jnp.concatenate(halves, 1)[None]
+    top = jnp.where(qx == 0, *(jnp.concatenate(p, 2) for p in ((estimate, across), (across, estimate))))
+    low = jnp.concatenate([down, down], 2)
+    result = jnp.where(qy == 0, *(jnp.concatenate(p, 1) for p in ((top, low), (low, top))))
+    zero = jnp.zeros((), jnp.int32)
+    place = (zero, 128 * (1 - qy), 128 * (1 - qx))
+    return lax.dynamic_update_slice(result, corner, place)[None]
 
 
 def solution(mesh):

time: 74.1 us -> 72.5 us (0.978)
  waiting for transfers between devices: 22.4 us -> 19.1 us
  starting transfers between devices: 30.8 us -> 31.9 us
    ppermute x6, waiting for transfers between devices: 17.1 us -> 14.7 us  [route(): return lax.ppermute(x, ('tile', 'view'), pairs)]
    ppermute x6, starting transfers between devices: 22.7 us -> 24.2 us  [route(): return lax.ppermute(x, ('tile', 'view'), pairs)]
    broadcast_in_dim x1 -> x0, other arithmetic: 1.04 us -> none  [per_device(): return jnp.concatenate(halves, 1)[None]]
    select_n x1, other arithmetic: 0.1 us -> 1.05 us  [per_device(): jnp.where(qy == 0, *(jnp.concatenate(p, 1) for p in ((top, low), (low, to...]
    ppermute x8, waiting for transfers between devices: 5.26 us -> 4.47 us  [over_view(): return lax.ppermute(x, 'view', [(i, i ^ flip) for i in range(4)])]
  transfers between devices with their start and end apart: 14 -> 14, of which waited for: 9 -> 8; matrix products, arithmetic and copies ran while one was open for 0% -> 2% of each run, Pallas kernels for 8% -> 9%
where the time goes in v5:
time: 72.5 us; the launch traced here: 72.4 us
  starting transfers between devices  31.9 us (44%)
  Pallas kernels  19.4 us (27%)
  waiting for transfers between devices  19.1 us (26%)
  other arithmetic  1.12 us (2%)
    ppermute x6, starting transfers between devices, route(): return lax.ppermute(x, ('tile', 'view'), pairs)  24.2 us
    pallas_call x13, Pallas kernels, call(): pl.pallas_call(lambda *refs: body(position(), *refs), out_shape=jax.tree....  19.4 us
    ppermute x6, waiting for transfers between devices, route(): return lax.ppermute(x, ('tile', 'view'), pairs)  14.7 us
    ppermute x8, starting transfers between devices, over_view(): return lax.ppermute(x, 'view', [(i, i ^ flip) for i in range(4)])  7.72 us
    ppermute x8, waiting for transfers between devices, over_view(): return lax.ppermute(x, 'view', [(i, i ^ flip) for i in range(4)])  4.47 us
  transfers between devices with their start and end apart: 14, of which 8 were waited for; matrix products, arithmetic and copies ran while one was open for 2% of the time, Pallas kernels for 9%

profile of v5, /device:TPU:13, one launch (start us, length us, event | category | flops | bytes accessed | tf_op | source)
XLA Modules:
  0.0 72.4 jit_solution(17669983059022927156)
XLA Ops:
  0.0 0.0 copy-start
  0.0 2.0 %shard_map.47 = (f32[664,128]{1,0:T(8,128)S(1)}, f32[664,128]{1,0:T(8,128)S(1)}, f32[664,128]{1,0:T(8,128)S(1)}, f32[664,128]{1,0:T(8,128)S(1)}) custom-call(f32[4,256,256]{2,1,0:T(8,128)} %bitcast.12, f32[3,8,31]{2,1,0:T(8,128)} %bitcast.13, s32[1,64]{1,0:T(1,128)} %refs_2_.1), custom_call_target="tpu_custom_call" | custom-call | bytes 1051808 | tf_op jit(solution)/shard_map/pallas_call | solution.py:51
  2.0 0.8 %collective-permute-start = (f32[664,128]{1,0:T(8,128)S(1)}, f32[664,128]{1,0:T(8,128)S(1)}, u32[]{:S(2)}, u32[]{:S(2)}) collective-permute-start(f32[664,128]{1,0:T(8,128)S(1)} %get-tuple-element.45), channel_id=1, source_target_pairs={{0,1},{1,0},{2,3},{3,2},{4,5},{5,4},{6,7},{7,6},{8,9},{9,8},{10,11... | collective-permute-start | bytes 1019912 | tf_op jit(solution)/shard_map/ppermute | solution.py:525
  2.8 1.7 %collective-permute-start.1 = (f32[664,128]{1,0:T(8,128)S(1)}, f32[664,128]{1,0:T(8,128)S(1)}, u32[]{:S(2)}, u32[]{:S(2)}) collective-permute-start(f32[664,128]{1,0:T(8,128)S(1)} %get-tuple-element.46), channel_id=1, source_target_pairs={{0,2},{1,3},{2,0},{3,1},{4,6},{5,7},{6,4},{7,5},{8,10},{9,11},{10,... | collective-permute-start | bytes 1019912 | tf_op jit(solution)/shard_map/ppermute | solution.py:525
  4.4 0.1 collective-permute-start.2
  4.5 0.0 copy-done
  4.5 0.2 shard_map.46
  4.7 5.5 %collective-permute-start.3 = (f32[160,128]{1,0:T(8,128)S(1)}, f32[160,128]{1,0:T(8,128)S(1)}, u32[]{:S(2)}, u32[]{:S(2)}) collective-permute-start(f32[160,128]{1,0:T(8,128)S(1)} %get-tuple-element.49), channel_id=1, source_target_pairs={{0,1},{1,0},{2,4},{4,2},{3,5},{5,3},{6,8},{8,6},{7,9},{9,7},{10,12... | collective-permute-start | bytes 245768 | tf_op jit(solution)/shard_map/ppermute | solution.py:522
  10.2 0.0 collective-permute-done.refs_1_.refs_4_
  10.2 1.1 %shard_map.48 = (bf16[2,2,256,256]{3,2,1,0:T(8,128)(2,1)S(1)}, bf16[2,2,256,256]{3,2,1,0:T(8,128)(2,1)S(1)}, bf16[2,256,128]{2,1,0:T(8,128)(2,1)S(1)}, bf16[2,25...) custom-call(f32[664,128]{1,0:T(8,128)S(1)} %get-tuple-element.44.ref, ...), custom_call_target="tpu_custom_call" | custom-call | flops 1000000000 | bytes 679936 | tf_op jit(solution)/shard_map/pallas_call | solution.py:51
  11.4 2.0 %collective-permute-done.3.refs_2_ = f32[160,128]{1,0:T(8,128)S(1)} collective-permute-done((f32[160,128]{1,0:T(8,128)S(1)}, f32[160,128]{1,0:T(8,128)S(1)}, u32[]{:S(2)}, u32[]{:S(2)}) %collective-permute-start.3) | collective-permute-done | bytes 81952 | tf_op jit(solution)/shard_map/ppermute | solution.py:522
  13.4 2.5 %collective-permute-start.4 = (f32[192,128]{1,0:T(8,128)S(1)}, f32[192,128]{1,0:T(8,128)S(1)}, u32[]{:S(2)}, u32[]{:S(2)}) collective-permute-start(f32[192,128]{1,0:T(8,128)S(1)} %shard_map.49), channel_id=1, source_target_pairs={{0,2},{1,32},{32,1},{2,0},{3,34},{34,3},{4,6},{5,36},{36,5},{6,4},... | collective-permute-start | bytes 294920 | tf_op jit(solution)/shard_map/ppermute | solution.py:522
  15.9 3.1 %collective-permute-done.4.refs_3_ = f32[192,128]{1,0:T(8,128)S(1)} collective-permute-done((f32[192,128]{1,0:T(8,128)S(1)}, f32[192,128]{1,0:T(8,128)S(1)}, u32[]{:S(2)}, u32[]{:S(2)}) %collective-permute-start.4) | collective-permute-done | bytes 98336 | tf_op jit(solution)/shard_map/ppermute | solution.py:522
  19.1 0.4 shard_map.50.refs_4_.refs_0_
  19.4 0.0 collective-permute-done.1.refs_2_.refs_0_.refs_5_
  19.4 0.8 %collective-permute-done.2.refs_3_.refs_1_.refs_6_ = f32[664,128]{1,0:T(8,128)S(1)} collective-permute-done((f32[664,128]{1,0:T(8,128)S(1)}, f32[664,128]{1,0:T(8,128)S(1)}, u32[]{:S(2)}, u32[]{:S(2)}) %collective-permute-start.2) | collective-permute-done | bytes 340000 | tf_op jit(solution)/shard_map/ppermute | solution.py:525
  20.2 0.5 shard_map.51.refs_9_.refs_2_
  20.7 5.1 %collective-permute-start.5 = (f32[288,128]{1,0:T(8,128)S(1)}, f32[288,128]{1,0:T(8,128)S(1)}, u32[]{:S(2)}, u32[]{:S(2)}) collective-permute-start(f32[288,128]{1,0:T(8,128)S(1)} %shard_map.51.refs_9_.refs_2_), channel_id=1, source_target_pairs={{0,1},{1,0},{2,4},{4,2},{3,5},{5,3},{6,8},{8,6},{7,9},{9,7},{10,12... | collective-permute-start | bytes 442376 | tf_op jit(solution)/shard_map/ppermute | solution.py:522
  25.8 1.0 %shard_map.52.refs_5_.refs_7_ = f32[1,160,640]{2,1,0:T(8,128)S(1)} custom-call(bf16[2,4,192,256]{3,2,1,0:T(8,128)(2,1)S(1)} %shard_map.50.refs_4_.refs_0_, bf16[2,2,256,256]{3,2,1,0:T(8,128)(2,1)S(1)} %get-tuple-element.59.refs_1_.refs_9_.refs_6_, bf16[2,2,256,256]{3,2,1,0:T(8,128)(2,1)S(1)} %get-tuple-element.60.refs_2_.refs_10_.refs_7_, ...), custom_call_target="tpu_custom_call" | custom-call | flops 1000000000 | bytes 3473408 | tf_op jit(solution)/shard_map/pallas_call | solution.py:51
  26.9 1.1 %shard_map.54 = (bf16[2,2,256,256]{3,2,1,0:T(8,128)(2,1)S(1)}, bf16[2,2,256,256]{3,2,1,0:T(8,128)(2,1)S(1)}, bf16[2,256,128]{2,1,0:T(8,128)(2,1)S(1)}, bf16[2,25...) custom-call(f32[664,128]{1,0:T(8,128)S(1)} %collective-permute-done., ...), custom_call_target="tpu_custom_call" | custom-call | flops 1000000000 | bytes 827392 | tf_op jit(solution)/shard_map/pallas_call | solution.py:51
  28.0 2.2 %collective-permute-done.5.refs_4_.refs_1_ = f32[288,128]{1,0:T(8,128)S(1)} collective-permute-done((f32[288,128]{1,0:T(8,128)S(1)}, f32[288,128]{1,0:T(8,128)S(1)}, u32[]{:S(2)}, u32[]{:S(2)}) %collective-permute-start.5) | collective-permute-done | bytes 147488 | tf_op jit(solution)/shard_map/ppermute | solution.py:522
  30.2 0.1 shard_map.53.refs_17_
  30.3 3.5 %collective-permute-start.6 = (f32[320,128]{1,0:T(8,128)S(1)}, f32[320,128]{1,0:T(8,128)S(1)}, u32[]{:S(2)}, u32[]{:S(2)}) collective-permute-start(f32[320,128]{1,0:T(8,128)S(1)} %shard_map.53.refs_17_), channel_id=1, source_target_pairs={{0,2},{1,32},{32,1},{2,0},{3,34},{34,3},{4,6},{5,36},{36,5},{6,4},... | collective-permute-start | bytes 491528 | tf_op jit(solution)/shard_map/ppermute | solution.py:522
  33.8 2.8 %shard_map.55.refs_8_ = f32[3,160,640]{2,1,0:T(8,128)S(1)} custom-call(bf16[2,4,192,256]{3,2,1,0:T(8,128)(2,1)S(1)} %shard_map.50.refs_4_.refs_0_, bf16[2,2,256,256]{3,2,1,0:T(8,128)(2,1)S(1)} %get-tuple-element.59.refs_1_.refs_9_.refs_6_, bf16[2,2,256,256]{3,2,1,0:T(8,128)(2,1)S(1)} %get-tuple-element.60.refs_2_.refs_10_.refs_7_, ...), custom_call_target="tpu_custom_call" | custom-call | flops 3000000000 | bytes 6029312 | tf_op jit(solution)/shard_map/pallas_call | solution.py:51
  36.6 1.2 %collective-permute-done.6.refs_2_ = f32[320,128]{1,0:T(8,128)S(1)} collective-permute-done((f32[320,128]{1,0:T(8,128)S(1)}, f32[320,128]{1,0:T(8,128)S(1)}, u32[]{:S(2)}, u32[]{:S(2)}) %collective-permute-start.6) | collective-permute-done | bytes 163872 | tf_op jit(solution)/shard_map/ppermute | solution.py:522
  37.8 3.2 %shard_map.56 = (f32[4,128,128]{2,1,0:T(8,128)S(1)}, f32[128,128]{1,0:T(8,128)S(1)}, f32[128,128]{1,0:T(8,128)S(1)}, f32[4,160,640]{2,1,0:T(8,128)S(1)}) custom-call(f32[4,160,128]{2,1,0:T(8,128)S(1)} %get-tuple-element.43.refs_0_, f32[288,128]{1,0:T(8,128)S(1)} %collective-permute-done.5.refs_4_.refs_1_, f32[320,128]{1,0:T(8,128)S(1)} %collective-permute-done.6.refs_2_, ...), custom_call_target="tpu_custom_call" | custom-call | flops 4000000000 | bytes 8716288 | tf_op jit(solution)/shard_map/pallas_call | solution.py:51
  41.1 0.1 collective-permute-start.7
  41.2 5.0 %collective-permute-start.8 = (f32[128,128]{1,0:T(8,128)S(1)}, f32[128,128]{1,0:T(8,128)S(1)}, u32[]{:S(2)}, u32[]{:S(2)}) collective-permute-start(f32[128,128]{1,0:T(8,128)S(1)} %get-tuple-element.77), channel_id=1, source_target_pairs={{0,1},{1,0},{2,4},{4,2},{3,5},{5,3},{6,8},{8,6},{7,9},{9,7},{10,12... | collective-permute-start | bytes 196616 | tf_op jit(solution)/shard_map/ppermute | solution.py:522
  46.2 0.0 collective-permute-done.7.refs_1_
  46.2 3.0 %collective-permute-done.8.refs_2_ = f32[128,128]{1,0:T(8,128)S(1)} collective-permute-done((f32[128,128]{1,0:T(8,128)S(1)}, f32[128,128]{1,0:T(8,128)S(1)}, u32[]{:S(2)}, u32[]{:S(2)}) %collective-permute-start.8) | collective-permute-done | bytes 65568 | tf_op jit(solution)/shard_map/ppermute | solution.py:522
  49.2 2.5 %collective-permute-start.10 = (f32[6,32,128]{2,1,0:T(8,128)S(1)}, f32[6,32,128]{2,1,0:T(8,128)S(1)}, u32[]{:S(2)}, u32[]{:S(2)}) collective-permute-start(f32[6,32,128]{2,1,0:T(8,128)S(1)} %get-tuple-element.79), channel_id=1, source_target_pairs={{0,2},{1,32},{32,1},{2,0},{3,34},{34,3},{4,6},{5,36},{36,5},{6,4},... | collective-permute-start | bytes 294920 | tf_op jit(solution)/shard_map/ppermute | solution.py:522
  51.7 0.0 collective-permute-start.9
  51.7 3.1 %collective-permute-done.10.refs_4_ = f32[6,32,128]{2,1,0:T(8,128)S(1)} collective-permute-done((f32[6,32,128]{2,1,0:T(8,128)S(1)}, f32[6,32,128]{2,1,0:T(8,128)S(1)}, u32[]{:S(2)}, u32[]{:S(2)}) %collective-permute-start.10) | collective-permute-done | bytes 98336 | tf_op jit(solution)/shard_map/ppermute | solution.py:522
  54.9 0.0 collective-permute-done.9.refs_3_
  54.9 6.9 %shard_map.58 = f32[4,128,128]{2,1,0:T(8,128)S(1)} custom-call(f32[4,128,128]{2,1,0:T(8,128)S(1)} %get-tuple-element.75.refs_0_, f32[128,128]{1,0:T(8,128)S(1)} %collective-permute-done.7.refs_1_, f32[128,128]{1,0:T(8,128)S(1)} %collective-permute-done.8.refs_2_, f32[6,32,128]{2,1,0:T(8,128)S(1)} %collective-permute-done.9.refs_3_, ...), custom_call_target="tpu_custom_call" | custom-call | flops 8000000000 | bytes 7307264 | tf_op jit(solution)/shard_map/pallas_call | solution.py:51
  61.7 0.1 collective-permute-start.11
  61.8 2.1 %collective-permute-start.12 = (f32[4,128,128]{2,1,0:T(8,128)S(1)}, f32[4,128,128]{2,1,0:T(8,128)S(1)}, u32[]{:S(2)}, u32[]{:S(2)}) collective-permute-start(f32[4,128,128]{2,1,0:T(8,128)S(1)} %shard_map.58), channel_id=1, source_target_pairs={{0,1},{1,0},{2,3},{3,2},{4,5},{5,4},{6,7},{7,6},{8,9},{9,8},{10,11... | collective-permute-start | bytes 786440 | tf_op jit(solution)/shard_map/ppermute | solution.py:525
  63.9 3.7 %collective-permute-done.11 = f32[4,128,128]{2,1,0:T(8,128)S(1)} collective-permute-done((f32[4,128,128]{2,1,0:T(8,128)S(1)}, f32[4,128,128]{2,1,0:T(8,128)S(1)}, u32[]{:S(2)}, u32[]{:S(2)}) %collective-permute-start.11) | collective-permute-done | bytes 262176 | tf_op jit(solution)/shard_map/ppermute | solution.py:525
  67.6 2.9 %collective-permute-start.13 = (f32[4,128,128]{2,1,0:T(8,128)S(1)}, f32[4,128,128]{2,1,0:T(8,128)S(1)}, u32[]{:S(2)}, u32[]{:S(2)}) collective-permute-start(f32[4,128,128]{2,1,0:T(8,128)S(1)} %collective-permute-done.11), channel_id=1, source_target_pairs={{0,1},{1,0},{2,3},{3,2},{4,5},{5,4},{6,7},{7,6},{8,9},{9,8},{10,11... | collective-permute-start | bytes 786440 | tf_op jit(solution)/shard_map/ppermute | solution.py:525
  70.6 0.0 collective-permute-done.12
  70.6 1.1 %maximum_select_fusion = f32[1,4,256,256]{3,2,1,0:T(8,128)} fusion(f32[1,4,128,256]{3,2,1,0:T(8,128)S(1)} %maximum_bitcast_fusion, f32[1,4,128,256]{3,2,1,0:T(8,128)S(1)} %fusion, pred[]{:T(512)S(6)} %eq.8), kind=kLoop, calls=%fused_computation | loop fusion | flops 786432 | bytes 2097153 | tf_op jit(solution)/shard_map/jit(_where)/select_n | solution.py:649
  71.7 0.0 collective-permute-done.13
  71.7 0.7 bitcast_dynamic-update-slice_fusion
  (4 shorter events, 0.1 us)
Async XLA Ops:
  0.0 4.5 %copy-start = (f32[1,4,256,256]{3,2,1,0:T(8,128)S(1)}, f32[1,4,256,256]{3,2,1,0:T(8,128)}, u32[]{:S(2)}) copy-start(f32[1,4,256,256]{3,2,1,0:T(8,128)} %param.4) | copy-start | bytes 3145732
  2.0 8.2 %collective-permute-start = (f32[664,128]{1,0:T(8,128)S(1)}, f32[664,128]{1,0:T(8,128)S(1)}, u32[]{:S(2)}, u32[]{:S(2)}) collective-permute-start(f32[664,128]{1,0:T(8,128)S(1)} %get-tuple-element.45), channel_id=1, source_target_pairs={{0,1},{1,0},{2,3},{3,2},{4,5},{5,4},{6,7},{7,6},{8,9},{9,8},{10,11... | collective-permute-start | bytes 1019912 | tf_op jit(solution)/shard_map/ppermute | solution.py:525
  2.8 16.7 %collective-permute-start.1 = (f32[664,128]{1,0:T(8,128)S(1)}, f32[664,128]{1,0:T(8,128)S(1)}, u32[]{:S(2)}, u32[]{:S(2)}) collective-permute-start(f32[664,128]{1,0:T(8,128)S(1)} %get-tuple-element.46), channel_id=1, source_target_pairs={{0,2},{1,3},{2,0},{3,1},{4,6},{5,7},{6,4},{7,5},{8,10},{9,11},{10,... | collective-permute-start | bytes 1019912 | tf_op jit(solution)/shard_map/ppermute | solution.py:525
  4.4 15.8 %collective-permute-start.2 = (f32[664,128]{1,0:T(8,128)S(1)}, f32[664,128]{1,0:T(8,128)S(1)}, u32[]{:S(2)}, u32[]{:S(2)}) collective-permute-start(f32[664,128]{1,0:T(8,128)S(1)} %get-tuple-element.47), channel_id=1, source_target_pairs={{0,3},{1,2},{2,1},{3,0},{4,7},{5,6},{6,5},{7,4},{8,11},{9,10},{10,... | collective-permute-start | bytes 1019912 | tf_op jit(solution)/shard_map/ppermute | solution.py:525
  4.7 8.7 %collective-permute-start.3 = (f32[160,128]{1,0:T(8,128)S(1)}, f32[160,128]{1,0:T(8,128)S(1)}, u32[]{:S(2)}, u32[]{:S(2)}) collective-permute-start(f32[160,128]{1,0:T(8,128)S(1)} %get-tuple-element.49), channel_id=1, source_target_pairs={{0,1},{1,0},{2,4},{4,2},{3,5},{5,3},{6,8},{8,6},{7,9},{9,7},{10,12... | collective-permute-start | bytes 245768 | tf_op jit(solution)/shard_map/ppermute | solution.py:522
  13.4 5.6 %collective-permute-start.4 = (f32[192,128]{1,0:T(8,128)S(1)}, f32[192,128]{1,0:T(8,128)S(1)}, u32[]{:S(2)}, u32[]{:S(2)}) collective-permute-start(f32[192,128]{1,0:T(8,128)S(1)} %shard_map.49), channel_id=1, source_target_pairs={{0,2},{1,32},{32,1},{2,0},{3,34},{34,3},{4,6},{5,36},{36,5},{6,4},... | collective-permute-start | bytes 294920 | tf_op jit(solution)/shard_map/ppermute | solution.py:522
  20.7 9.5 %collective-permute-start.5 = (f32[288,128]{1,0:T(8,128)S(1)}, f32[288,128]{1,0:T(8,128)S(1)}, u32[]{:S(2)}, u32[]{:S(2)}) collective-permute-start(f32[288,128]{1,0:T(8,128)S(1)} %shard_map.51.refs_9_.refs_2_), channel_id=1, source_target_pairs={{0,1},{1,0},{2,4},{4,2},{3,5},{5,3},{6,8},{8,6},{7,9},{9,7},{10,12... | collective-permute-start | bytes 442376 | tf_op jit(solution)/shard_map/ppermute | solution.py:522
  30.3 7.5 %collective-permute-start.6 = (f32[320,128]{1,0:T(8,128)S(1)}, f32[320,128]{1,0:T(8,128)S(1)}, u32[]{:S(2)}, u32[]{:S(2)}) collective-permute-start(f32[320,128]{1,0:T(8,128)S(1)} %shard_map.53.refs_17_), channel_id=1, source_target_pairs={{0,2},{1,32},{32,1},{2,0},{3,34},{34,3},{4,6},{5,36},{36,5},{6,4},... | collective-permute-start | bytes 491528 | tf_op jit(solution)/shard_map/ppermute | solution.py:522
  41.1 5.2 %collective-permute-start.7 = (f32[128,128]{1,0:T(8,128)S(1)}, f32[128,128]{1,0:T(8,128)S(1)}, u32[]{:S(2)}, u32[]{:S(2)}) collective-permute-start(f32[128,128]{1,0:T(8,128)S(1)} %get-tuple-element.76), channel_id=1, source_target_pairs={{0,2},{1,3},{2,0},{3,1},{4,6},{5,7},{6,4},{7,5},{8,10},{9,11},{10,... | collective-permute-start | bytes 196616 | tf_op jit(solution)/shard_map/ppermute | solution.py:525
  41.2 8.0 %collective-permute-start.8 = (f32[128,128]{1,0:T(8,128)S(1)}, f32[128,128]{1,0:T(8,128)S(1)}, u32[]{:S(2)}, u32[]{:S(2)}) collective-permute-start(f32[128,128]{1,0:T(8,128)S(1)} %get-tuple-element.77), channel_id=1, source_target_pairs={{0,1},{1,0},{2,4},{4,2},{3,5},{5,3},{6,8},{8,6},{7,9},{9,7},{10,12... | collective-permute-start | bytes 196616 | tf_op jit(solution)/shard_map/ppermute | solution.py:522
  49.2 5.6 %collective-permute-start.10 = (f32[6,32,128]{2,1,0:T(8,128)S(1)}, f32[6,32,128]{2,1,0:T(8,128)S(1)}, u32[]{:S(2)}, u32[]{:S(2)}) collective-permute-start(f32[6,32,128]{2,1,0:T(8,128)S(1)} %get-tuple-element.79), channel_id=1, source_target_pairs={{0,2},{1,32},{32,1},{2,0},{3,34},{34,3},{4,6},{5,36},{36,5},{6,4},... | collective-permute-start | bytes 294920 | tf_op jit(solution)/shard_map/ppermute | solution.py:522
  51.7 3.1 %collective-permute-start.9 = (f32[6,32,128]{2,1,0:T(8,128)S(1)}, f32[6,32,128]{2,1,0:T(8,128)S(1)}, u32[]{:S(2)}, u32[]{:S(2)}) collective-permute-start(f32[6,32,128]{2,1,0:T(8,128)S(1)} %get-tuple-element.78), channel_id=1, source_target_pairs={{0,1},{1,0},{2,3},{3,2},{4,5},{5,4},{6,7},{7,6},{8,9},{9,8},{10,11... | collective-permute-start | bytes 294920 | tf_op jit(solution)/shard_map/ppermute | solution.py:525
  61.7 5.9 %collective-permute-start.11 = (f32[4,128,128]{2,1,0:T(8,128)S(1)}, f32[4,128,128]{2,1,0:T(8,128)S(1)}, u32[]{:S(2)}, u32[]{:S(2)}) collective-permute-start(f32[4,128,128]{2,1,0:T(8,128)S(1)} %shard_map.58), channel_id=1, source_target_pairs={{0,2},{1,3},{2,0},{3,1},{4,6},{5,7},{6,4},{7,5},{8,10},{9,11},{10,... | collective-permute-start | bytes 786440 | tf_op jit(solution)/shard_map/ppermute | solution.py:525
  61.8 8.8 %collective-permute-start.12 = (f32[4,128,128]{2,1,0:T(8,128)S(1)}, f32[4,128,128]{2,1,0:T(8,128)S(1)}, u32[]{:S(2)}, u32[]{:S(2)}) collective-permute-start(f32[4,128,128]{2,1,0:T(8,128)S(1)} %shard_map.58), channel_id=1, source_target_pairs={{0,1},{1,0},{2,3},{3,2},{4,5},{5,4},{6,7},{7,6},{8,9},{9,8},{10,11... | collective-permute-start | bytes 786440 | tf_op jit(solution)/shard_map/ppermute | solution.py:525
  67.6 4.1 %collective-permute-start.13 = (f32[4,128,128]{2,1,0:T(8,128)S(1)}, f32[4,128,128]{2,1,0:T(8,128)S(1)}, u32[]{:S(2)}, u32[]{:S(2)}) collective-permute-start(f32[4,128,128]{2,1,0:T(8,128)S(1)} %collective-permute-done.11), channel_id=1, source_target_pairs={{0,1},{1,0},{2,3},{3,2},{4,5},{5,4},{6,7},{7,6},{8,9},{9,8},{10,11... | collective-permute-start | bytes 786440 | tf_op jit(solution)/shard_map/ppermute | solution.py:525

commit v6 on v5

--- a/solution.py
+++ b/solution.py
@@ -126,7 +126,7 @@
     for s in range(4):
         q = jnp.bitwise_xor(view, s)
         qx, qy = lax.shift_right_logical(q, 1), jnp.bitwise_and(q, 1)
-        rows = pl.ds(pl.multiple_of(112 * qy, 16), 144)
+        rows = pl.ds(pl.multiple_of(128 * qy, 128), 128)
         here = pl.ds(pl.multiple_of(128 * qx, 128), 128)
         there = pl.ds(pl.multiple_of(128 - 128 * qx, 128), 128)
         places.append((qx, qy, rows, here, there))
@@ -134,26 +134,26 @@
         load.wait()
     raw[...] = raw[...] / jnp.sum(raw[...], axis=-1, keepdims=True)
     for s, (qx, qy, _, _, _) in enumerate(places):
-        sent[s][648:664] = jnp.zeros((16, 128), F32)
+        sent[s][576:592] = jnp.zeros((16, 128), F32)
         for n in range(4):
             x = jnp.clip(col + (2 * qx - 1) * (n % 2), 0, GX - 1)
             y = jnp.clip(row + (2 * qy - 1) * (n // 2), 0, grid_rows - 1)
             which = ids[0, y * GX + x]
             for axis in range(3):
-                at = 648 + 3 * n + axis
+                at = 576 + 3 * n + axis
                 sent[s][at : at + 1, 0:31] = raw[axis, pl.ds(which, 1)]
     for z in range(4):
         loads[z].wait()
         for s, (_, _, rows, here, _) in enumerate(places):
-            sent[s][144 * z : 144 * z + 144] = whole[z, rows, here]
+            sent[s][128 * z : 128 * z + 128] = whole[z, rows, here]
     for s, (qx, _, rows, _, there) in enumerate(places):
         side = shared([whole[z, rows, there] for z in range(4)], qx)
-        sent[s][576:648] = side[:72] + turn(side[72:], 16 + 96 * qx)
+        sent[s][512:576] = side[:64] + turn(side[64:], 16 + 96 * qx)
 
 
 def own_side(block, qx):
-    side = block[576:648]
-    mine = right_half(72) == (qx == 0)
+    side = block[512:576]
+    mine = right_half(64) == (qx == 0)
     low = jnp.where(mine, turn(side, 112 - 96 * qx), 0.0)
     return jnp.concatenate([jnp.where(mine, side, 0.0), low], 0)
 
@@ -181,9 +181,9 @@
         cols = []
         for s in (2 * h, 2 * h + 1):
             block = got[s ^ 2]
-            cols.append(shared([block[144 * z : 144 * z + 144] for z in range(4)], qx))
+            cols.append(shared([block[128 * z : 128 * z + 128] for z in range(4)], qx))
         other = turn(cols[1], 16 + 96 * qx)
-        out[h * 144 : h * 144 + 144] = cols[0] + other
+        out[h * 128 : h * 128 + 128] = cols[0] + other
 
 
 def both_sides(inner, cols, odd, qx):
@@ -193,18 +193,20 @@
     return jnp.where(right_half(rows) == (qx == 0), inner, cols)
 
 
-def pack_rows_kernel(info, *refs):
+def pack_rows_kernel(far, info, *refs):
     got, cols, out = refs[:4], refs[4], refs[5]
-    at = pl.multiple_of(128 * info[2], 16)
-    sides = [own_side(got[s], info[1]) for s in range(4)]
+    qx, qy = info[1], info[2]
+    sides = [own_side(got[s], qx) for s in range(4)]
+    start = 112 * qy if far else 112 - 112 * qy
+    at = pl.multiple_of(start, 16)
     for s in range(4):
         o = s ^ 1
         for z in range(4):
             n = 4 * s + z
-            out[n * 16 : n * 16 + 16] = got[o][pl.ds(144 * z + at, 16)]
-        inner = jnp.where(info[2] == 0, sides[o][:16], sides[o][128:])
-        outer = cols[pl.ds((o // 2) * 144 + at, 16)]
-        out[256 + 16 * s : 272 + 16 * s] = both_sides(inner, outer, o % 2, info[1])
+            out[n * 16 : n * 16 + 16] = got[o][pl.ds(128 * z + at, 16)]
+        inner = jnp.where(start == 0, sides[o][:16], sides[o][112:])
+        outer = cols[pl.ds((o // 2) * 128 + at, 16)]
+        out[256 + 16 * s : 272 + 16 * s] = both_sides(inner, outer, o % 2, qx)
 
 
 def start_rows_kernel(info, main, inside, cols, out):
@@ -222,7 +224,7 @@
 def matrices_kernel(info, one, two, xh, xl, ah, al, y, t, zm, zs):
     qx, qy = info[1], info[2]
     for s, table in enumerate((one, two)):
-        fwd = table[648:664]
+        fwd = table[576:592]
         flip = lax.broadcasted_iota(jnp.int32, (128, 128), 0) + lanes(128) == 30
         rev = jnp.dot(fwd, flip.astype(F32), precision=lax.Precision.HIGHEST)
         zero = jnp.zeros((16, 128), F32)
@@ -409,23 +411,23 @@
         edges[1][...] = jnp.where(qx == 0, low, high)
 
 
-def adjoint_kernel(info, main, cols, rows_in, *refs):
+def adjoint_kernel(info, main, cols, rows_near, rows_far, *refs):
     got, blurs, refs = refs[:4], refs[4:6], refs[6:]
     groups, refs = (refs[:8], refs[8:16]), refs[16:]
     out, near_edge, far_edge, rec, r, total = refs
     qx, qy = info[1], info[2]
-    in_tile = pl.multiple_of(16 * (1 - qy), 16)
-    out_tile = pl.multiple_of(144 * qy, 16)
     for s in range(4):
         for z in range(4):
-            here = slice(128 * z, 128 * z + 128)
-            rec[s, pl.ds(in_tile, 144), here] = got[s][144 * z : 144 * z + 144]
-            n = 4 * s + z
-            rec[s, pl.ds(out_tile, 16), here] = rows_in[n * 16 : n * 16 + 16]
-        outer = cols[(s // 2) * 144 : (s // 2) * 144 + 144]
-        rec[s, pl.ds(in_tile, 144), 512:] = both_sides(own_side(got[s], qx), outer, s % 2, qx)
-        rec[s, pl.ds(out_tile, 16), 512:] = rows_in[256 + 16 * s : 272 + 16 * s]
-    for s in range(2):
+            rec[s, 16:144, 128 * z : 128 * z + 128] = got[s][128 * z : 128 * z + 128]
+        outer = cols[(s // 2) * 128 : (s // 2) * 128 + 128]
+        rec[s, 16:144, 512:] = both_sides(own_side(got[s], qx), outer, s % 2, qx)
+        for rows, start in ((rows_near, 144 * (1 - qy)), (rows_far, 144 * qy)):
+            at = pl.ds(pl.multiple_of(start, 16), 16)
+            for z in range(4):
+                n = 4 * s + z
+                rec[s, at, 128 * z : 128 * z + 128] = rows[n * 16 : n * 16 + 16]
+            rec[s, at, 512:] = rows[256 + 16 * s : 272 + 16 * s]
+    for s in range(4):
         clear(r.at[s], 160)
     total[...] = jnp.zeros_like(total)
     masks = row_masks(info)
@@ -437,24 +439,21 @@
             for a, b in ((0, 256), (256, 512), (512, 640)):
                 slot = 2 * pair + s
                 blurred = blurs[1][slot - 1, :, a:b] if slot else blurs[0][0, :, a:b]
-                take_ratio(slot, rec, r.at[s], masks, slice(a, b), blurred)
-            planes, near, edge = adjoint(s, mats, r.at[s], total)
+                take_ratio(slot, rec, r.at[slot], masks, slice(a, b), blurred)
+            planes, near, edge = adjoint(s, mats, r.at[slot], total)
             finish(s, mats, planes, jnp.where(far, edge, near), total)
     at = pl.ds(pl.multiple_of(32 * qy, 32), 128)
     update(True, main, at, total, out, (near_edge, far_edge), qx)
 
 
-def mid_rows_kernel(info, main, inside, beyond, near, far):
-    shown = (
-        *(main.at[z] for z in range(4)),
-        inside,
-        beyond,
-    )
-    for out, at in ((near, 96 - 96 * info[2]), (far, 96 * info[2])):
-        rows = pl.ds(pl.multiple_of(at, 32), 32)
-        for n in range(6):
-            piece = shown[n][rows]
-            out[n] = jnp.where(info[3] > 0, piece, 0.0) if n == 5 else piece
+def mid_rows_kernel(far, info, main, inside, beyond, out):
+    rows = pl.ds(pl.multiple_of(96 * info[2] if far else 96 - 96 * info[2], 32), 32)
+    for z in range(4):
+        out[z] = main[z, rows]
+    out[4] = inside[rows]
+    out[5] = jnp.where(info[3] > 0, beyond[rows], 0.0)
+    if far:
+        out[6:] = jnp.zeros((1, 32, 128), F32)
 
 
 def step_kernel(info, main, inside, beyond, rows_in, rows_out, *refs):
@@ -471,7 +470,7 @@
             info[4] > 0, rows_out[n], 0.0
         )
     spread(region, e, qx)
-    for s in range(2):
+    for s in range(4):
         clear(p.at[s], 192)
         clear(r.at[s], 160)
     total[...] = jnp.zeros_like(total)
@@ -483,11 +482,11 @@
             slot = 2 * pair + s
 
             def put(where, value):
-                take_ratio(slot, rec, r.at[s], masks, where, value)
-
-            near, edge = forward(s, qy, e, mats, p.at[s], put)
+                take_ratio(slot, rec, r.at[slot], masks, where, value)
+
+            near, edge = forward(s, qy, e, mats, p.at[slot], put)
             put(slice(512, 640), jnp.where(far160, edge, near))
-            planes, near, edge = adjoint(s, mats, r.at[s], total)
+            planes, near, edge = adjoint(s, mats, r.at[slot], total)
             finish(s, mats, planes, jnp.where(far128, edge, near), total)
     update(False, main, slice(0, 128), total, out, None, qx)
 
@@ -539,7 +538,7 @@
 
     sent = call(
         functools.partial(send_kernel, grid_rows),
-        (shape(664, 128),) * 4,
+        (shape(592, 128),) * 4,
         [
             VMEM((3, 8, 31), F32),
             SMEM((1, count_tiles), jnp.int32),
@@ -586,48 +585,61 @@
             after=after,
         )
 
-    packed_cols = call(pack_cols_kernel, shape(288, 128), [], *got, after=e)
+    packed_cols = call(pack_cols_kernel, shape(256, 128), [], *got, after=e)
     cols = route(packed_cols, x_pairs)
     mats.append(make_matrices(*got[2:], after=packed_cols))
     blurs = [blur(((0, 0),), packed_cols, *mats[0])]
-    packed_rows = call(pack_rows_kernel, shape(320, 128), [], *got, cols, after=blurs[0])
+    pack_rows = [functools.partial(pack_rows_kernel, far) for far in (True, False)]
+    packed_rows = call(pack_rows[0], shape(320, 128), [], *got, cols, after=blurs[0])
     rows = route(packed_rows, y_pairs)
-    blurs.append(blur(((0, 1), (1, 0), (1, 1)), packed_rows, *mats[0], *mats[1]))
+    inner_rows = call(pack_rows[1], shape(320, 128), [], *got, cols, after=packed_rows)
+    rows_near = over_view(inner_rows, 1)
+    blurs.append(blur(((0, 1), (1, 0), (1, 1)), inner_rows, *mats[0], *mats[1]))
     quad = shape(4, 128, 128)
     flat = [*mats[0], *mats[1]]
     estimate, near_edge, far_edge, rec = call(
         adjoint_kernel,
         (quad, shape(128, 128), shape(128, 128), shape(4, 160, 640)),
         [
-            VMEM((2, 2, 256, 640), BF16),
+            VMEM((4, 2, 256, 640), BF16),
             VMEM((4, 128, 128), F32),
         ],
         main,
         cols,
+        rows_near,
         rows,
         *got,
         *blurs,
         *flat,
         flops=4_000_000_000,
-        kept_in=range(9, 25),
+        kept_in=range(10, 26),
         kept_out=(3,),
     )
     for step in range(1, ITERS):
         inside = over_view(near_edge, 2)
         beyond = route(far_edge, x_pairs)
-        near, far = call(
-            mid_rows_kernel, (shape(6, 32, 128),) * 2, [], estimate, inside, beyond
+        mid_rows = [functools.partial(mid_rows_kernel, far) for far in (True, False)]
+        far_rows = call(mid_rows[0], shape(7, 32, 128), [], estimate, inside, beyond)
+        rows_out = route(far_rows, y_pairs)
+        near_rows = call(
+            mid_rows[1],
+            shape(6, 32, 128),
+            [],
+            estimate,
+            inside,
+            beyond,
+            after=far_rows,
+            flops=2_000_000_000,
         )
-        rows_in = over_view(near, 1)
-        rows_out = route(far, y_pairs)
+        rows_in = over_view(near_rows, 1)
         estimate = call(
             step_kernel,
             quad,
             [
                 VMEM((6, 192, 128), F32),
                 VMEM((2, 4, 192, 256), BF16),
-                VMEM((2, 2, 256, 640), BF16),
-                VMEM((2, 2, 256, 640), BF16),
+                VMEM((4, 2, 256, 640), BF16),
+                VMEM((4, 2, 256, 640), BF16),
                 VMEM((4, 128, 128), F32),
             ],
                 estimate,

time: 72.5 us -> 71.5 us (0.986); the launches traced: 72.4 us -> 70.2 us
  waiting for transfers between devices: 19.1 us -> 15.1 us
  starting transfers between devices: 31.9 us -> 33.8 us
    ppermute x6, waiting for transfers between devices: 14.7 us -> 10.9 us  [route(): return lax.ppermute(x, ('tile', 'view'), pairs)]
    ppermute x8 -> x9, starting transfers between devices: 7.72 us -> 9.15 us  [over_view(): return lax.ppermute(x, 'view', [(i, i ^ flip) for i in range(4)])]
    ppermute x8 -> x9, waiting for transfers between devices: 4.47 us -> 4.14 us  [over_view(): return lax.ppermute(x, 'view', [(i, i ^ flip) for i in range(4)])]
    pallas_call x13 -> x15, Pallas kernels: 19.4 us -> 19.3 us  [call(): pl.pallas_call(lambda *refs: body(position(), *refs), out_shape=jax.tree....]
  transfers between devices with their start and end apart: 14 -> 15, of which waited for: 8 -> 8; matrix products, arithmetic and copies ran while one was open for 2% -> 2% of each run, Pallas kernels for 9% -> 10%
where the time goes in v6:
time: 71.5 us; the launch traced here: 70.2 us
  starting transfers between devices  33.8 us (47%)
  Pallas kernels  19.3 us (27%)
  waiting for transfers between devices  15.1 us (21%)
  other arithmetic  1.12 us (2%)
  local copies, waits for them, and re-layouts  0.72 us (1%)
    ppermute x6, starting transfers between devices, route(): return lax.ppermute(x, ('tile', 'view'), pairs)  24.7 us
    pallas_call x15, Pallas kernels, call(): pl.pallas_call(lambda *refs: body(position(), *refs), out_shape=jax.tree....  19.3 us
    ppermute x6, waiting for transfers between devices, route(): return lax.ppermute(x, ('tile', 'view'), pairs)  10.9 us
    ppermute x9, starting transfers between devices, over_view(): return lax.ppermute(x, 'view', [(i, i ^ flip) for i in range(4)])  9.15 us
    ppermute x9, waiting for transfers between devices, over_view(): return lax.ppermute(x, 'view', [(i, i ^ flip) for i in range(4)])  4.14 us
  transfers between devices with their start and end apart: 15, of which 8 were waited for; matrix products, arithmetic and copies ran while one was open for 2% of the time, Pallas kernels for 10%

profile of v6, /device:TPU:13, one launch (start us, length us, event | category | flops | bytes accessed | tf_op | source)
XLA Modules:
  0.0 70.2 jit_solution(729827641034391631)
XLA Ops:
  0.0 0.0 copy-start
  0.0 1.9 %shard_map.47 = (f32[592,128]{1,0:T(8,128)S(1)}, f32[592,128]{1,0:T(8,128)S(1)}, f32[592,128]{1,0:T(8,128)S(1)}, f32[592,128]{1,0:T(8,128)S(1)}) custom-call(f32[4,256,256]{2,1,0:T(8,128)} %bitcast.12, f32[3,8,31]{2,1,0:T(8,128)} %bitcast.13, s32[1,64]{1,0:T(1,128)} %refs_2_.1), custom_call_target="tpu_custom_call" | custom-call | bytes 1051808 | tf_op jit(solution)/shard_map/pallas_call | solution.py:51
  2.0 0.8 %collective-permute-start = (f32[592,128]{1,0:T(8,128)S(1)}, f32[592,128]{1,0:T(8,128)S(1)}, u32[]{:S(2)}, u32[]{:S(2)}) collective-permute-start(f32[592,128]{1,0:T(8,128)S(1)} %get-tuple-element.43), channel_id=1, source_target_pairs={{0,1},{1,0},{2,3},{3,2},{4,5},{5,4},{6,7},{7,6},{8,9},{9,8},{10,11... | collective-permute-start | bytes 909320 | tf_op jit(solution)/shard_map/ppermute | solution.py:524
  2.7 1.7 %collective-permute-start.1 = (f32[592,128]{1,0:T(8,128)S(1)}, f32[592,128]{1,0:T(8,128)S(1)}, u32[]{:S(2)}, u32[]{:S(2)}) collective-permute-start(f32[592,128]{1,0:T(8,128)S(1)} %get-tuple-element.44), channel_id=1, source_target_pairs={{0,2},{1,3},{2,0},{3,1},{4,6},{5,7},{6,4},{7,5},{8,10},{9,11},{10,... | collective-permute-start | bytes 909320 | tf_op jit(solution)/shard_map/ppermute | solution.py:524
  4.4 0.1 collective-permute-start.2
  4.4 0.0 copy-done
  4.4 0.2 shard_map.46
  4.7 5.5 %collective-permute-start.3 = (f32[160,128]{1,0:T(8,128)S(1)}, f32[160,128]{1,0:T(8,128)S(1)}, u32[]{:S(2)}, u32[]{:S(2)}) collective-permute-start(f32[160,128]{1,0:T(8,128)S(1)} %get-tuple-element.47), channel_id=1, source_target_pairs={{0,1},{1,0},{2,4},{4,2},{3,5},{5,3},{6,8},{8,6},{7,9},{9,7},{10,12... | collective-permute-start | bytes 245768 | tf_op jit(solution)/shard_map/ppermute | solution.py:521
  10.2 0.0 collective-permute-done.refs_1_.refs_5_
  10.2 1.1 %shard_map.48 = (bf16[2,2,256,256]{3,2,1,0:T(8,128)(2,1)S(1)}, bf16[2,2,256,256]{3,2,1,0:T(8,128)(2,1)S(1)}, bf16[2,256,128]{2,1,0:T(8,128)(2,1)S(1)}, bf16[2,25...) custom-call(f32[592,128]{1,0:T(8,128)S(1)} %get-tuple-element.42.ref, ...), custom_call_target="tpu_custom_call" | custom-call | flops 1000000000 | bytes 606208 | tf_op jit(solution)/shard_map/pallas_call | solution.py:51
  11.3 2.0 %collective-permute-done.3.refs_2_ = f32[160,128]{1,0:T(8,128)S(1)} collective-permute-done((f32[160,128]{1,0:T(8,128)S(1)}, f32[160,128]{1,0:T(8,128)S(1)}, u32[]{:S(2)}, u32[]{:S(2)}) %collective-permute-start.3) | collective-permute-done | bytes 81952 | tf_op jit(solution)/shard_map/ppermute | solution.py:521
  13.4 2.5 %collective-permute-start.4 = (f32[192,128]{1,0:T(8,128)S(1)}, f32[192,128]{1,0:T(8,128)S(1)}, u32[]{:S(2)}, u32[]{:S(2)}) collective-permute-start(f32[192,128]{1,0:T(8,128)S(1)} %shard_map.49), channel_id=1, source_target_pairs={{0,2},{1,32},{32,1},{2,0},{3,34},{34,3},{4,6},{5,36},{36,5},{6,4},... | collective-permute-start | bytes 294920 | tf_op jit(solution)/shard_map/ppermute | solution.py:521
  15.9 3.1 %collective-permute-done.4.refs_3_ = f32[192,128]{1,0:T(8,128)S(1)} collective-permute-done((f32[192,128]{1,0:T(8,128)S(1)}, f32[192,128]{1,0:T(8,128)S(1)}, u32[]{:S(2)}, u32[]{:S(2)}) %collective-permute-start.4) | collective-permute-done | bytes 98336 | tf_op jit(solution)/shard_map/ppermute | solution.py:521
  19.0 0.4 shard_map.50.refs_4_.refs_0_
  19.4 0.0 collective-permute-done.1.refs_2_.refs_0_.refs_6_
  19.4 0.0 collective-permute-done.2.refs_3_.refs_1_.refs_7_
  19.4 0.5 shard_map.51.refs_9_.refs_2_
  19.9 5.2 %collective-permute-start.5 = (f32[256,128]{1,0:T(8,128)S(1)}, f32[256,128]{1,0:T(8,128)S(1)}, u32[]{:S(2)}, u32[]{:S(2)}) collective-permute-start(f32[256,128]{1,0:T(8,128)S(1)} %shard_map.51.refs_9_.refs_2_), channel_id=1, source_target_pairs={{0,1},{1,0},{2,4},{4,2},{3,5},{5,3},{6,8},{8,6},{7,9},{9,7},{10,12... | collective-permute-start | bytes 393224 | tf_op jit(solution)/shard_map/ppermute | solution.py:521
  25.1 1.0 %shard_map.52.refs_5_.refs_8_ = f32[1,160,640]{2,1,0:T(8,128)S(1)} custom-call(bf16[2,4,192,256]{3,2,1,0:T(8,128)(2,1)S(1)} %shard_map.50.refs_4_.refs_0_, bf16[2,2,256,256]{3,2,1,0:T(8,128)(2,1)S(1)} %get-tuple-element.57.refs_1_.refs_10_.refs_6_, bf16[2,2,256,256]{3,2,1,0:T(8,128)(2,1)S(1)} %get-tuple-element.58.refs_2_.refs_11_.refs_7_, ...), custom_call_target="tpu_custom_call" | custom-call | flops 1000000000 | bytes 3457024 | tf_op jit(solution)/shard_map/pallas_call | solution.py:51
  26.1 1.1 %shard_map.55 = (bf16[2,2,256,256]{3,2,1,0:T(8,128)(2,1)S(1)}, bf16[2,2,256,256]{3,2,1,0:T(8,128)(2,1)S(1)}, bf16[2,256,128]{2,1,0:T(8,128)(2,1)S(1)}, bf16[2,25...) custom-call(f32[592,128]{1,0:T(8,128)S(1)} %collective-permute-done., ...), custom_call_target="tpu_custom_call" | custom-call | flops 1000000000 | bytes 737280 | tf_op jit(solution)/shard_map/pallas_call | solution.py:51
  27.3 1.0 %collective-permute-done.5.refs_4_.refs_1_ = f32[256,128]{1,0:T(8,128)S(1)} collective-permute-done((f32[256,128]{1,0:T(8,128)S(1)}, f32[256,128]{1,0:T(8,128)S(1)}, u32[]{:S(2)}, u32[]{:S(2)}) %collective-permute-start.5) | collective-permute-done | bytes 131104 | tf_op jit(solution)/shard_map/ppermute | solution.py:521
  28.3 0.1 shard_map.53.refs_5_
  28.4 3.1 %collective-permute-start.7 = (f32[320,128]{1,0:T(8,128)S(1)}, f32[320,128]{1,0:T(8,128)S(1)}, u32[]{:S(2)}, u32[]{:S(2)}) collective-permute-start(f32[320,128]{1,0:T(8,128)S(1)} %shard_map.53.refs_5_), channel_id=1, source_target_pairs={{0,2},{1,32},{32,1},{2,0},{3,34},{34,3},{4,6},{5,36},{36,5},{6,4},... | collective-permute-start | bytes 491528 | tf_op jit(solution)/shard_map/ppermute | solution.py:521
  31.4 0.1 shard_map.54.refs_17_
  31.5 0.3 collective-permute-start.6
  31.8 2.8 %shard_map.56.refs_9_ = f32[3,160,640]{2,1,0:T(8,128)S(1)} custom-call(bf16[2,4,192,256]{3,2,1,0:T(8,128)(2,1)S(1)} %shard_map.50.refs_4_.refs_0_, bf16[2,2,256,256]{3,2,1,0:T(8,128)(2,1)S(1)} %get-tuple-element.57.refs_1_.refs_10_.refs_6_, bf16[2,2,256,256]{3,2,1,0:T(8,128)(2,1)S(1)} %get-tuple-element.58.refs_2_.refs_11_.refs_7_, ...), custom_call_target="tpu_custom_call" | custom-call | flops 3000000000 | bytes 6029312 | tf_op jit(solution)/shard_map/pallas_call | solution.py:51
  34.6 0.0 collective-permute-done.6.refs_2_
  34.6 0.6 collective-permute-done.7.refs_3_
  35.3 3.1 %shard_map.57 = (f32[4,128,128]{2,1,0:T(8,128)S(1)}, f32[128,128]{1,0:T(8,128)S(1)}, f32[128,128]{1,0:T(8,128)S(1)}, f32[4,160,640]{2,1,0:T(8,128)S(1)}) custom-call(f32[4,160,128]{2,1,0:T(8,128)S(1)} %get-tuple-element.41.refs_0_, f32[256,128]{1,0:T(8,128)S(1)} %collective-permute-done.5.refs_4_.refs_1_, f32[320,128]{1,0:T(8,128)S(1)} %collective-permute-done.6.refs_2_, ...), custom_call_target="tpu_custom_call" | custom-call | flops 4000000000 | bytes 8716288 | tf_op jit(solution)/shard_map/pallas_call | solution.py:51
  38.4 0.1 collective-permute-start.8
  38.5 6.2 %collective-permute-start.9 = (f32[128,128]{1,0:T(8,128)S(1)}, f32[128,128]{1,0:T(8,128)S(1)}, u32[]{:S(2)}, u32[]{:S(2)}) collective-permute-start(f32[128,128]{1,0:T(8,128)S(1)} %get-tuple-element.75), channel_id=1, source_target_pairs={{0,1},{1,0},{2,4},{4,2},{3,5},{5,3},{6,8},{8,6},{7,9},{9,7},{10,12... | collective-permute-start | bytes 196616 | tf_op jit(solution)/shard_map/ppermute | solution.py:521
  44.7 0.0 collective-permute-done.8.refs_1_
  44.7 2.1 %collective-permute-done.9.refs_2_ = f32[128,128]{1,0:T(8,128)S(1)} collective-permute-done((f32[128,128]{1,0:T(8,128)S(1)}, f32[128,128]{1,0:T(8,128)S(1)}, u32[]{:S(2)}, u32[]{:S(2)}) %collective-permute-start.9) | collective-permute-done | bytes 65568 | tf_op jit(solution)/shard_map/ppermute | solution.py:521
  46.9 2.2 %collective-permute-start.11 = (f32[7,32,128]{2,1,0:T(8,128)S(1)}, f32[7,32,128]{2,1,0:T(8,128)S(1)}, u32[]{:S(2)}, u32[]{:S(2)}) collective-permute-start(f32[7,32,128]{2,1,0:T(8,128)S(1)} %shard_map.58.refs_3_), channel_id=1, source_target_pairs={{0,2},{1,32},{32,1},{2,0},{3,34},{34,3},{4,6},{5,36},{36,5},{6,4},... | collective-permute-start | bytes 344072 | tf_op jit(solution)/shard_map/ppermute | solution.py:521
  49.1 0.3 collective-permute-start.10
  49.4 1.3 %collective-permute-done.10.refs_3_ = f32[6,32,128]{2,1,0:T(8,128)S(1)} collective-permute-done((f32[6,32,128]{2,1,0:T(8,128)S(1)}, f32[6,32,128]{2,1,0:T(8,128)S(1)}, u32[]{:S(2)}, u32[]{:S(2)}) %collective-permute-start.10) | collective-permute-done | bytes 98336 | tf_op jit(solution)/shard_map/ppermute | solution.py:524
  50.7 1.9 %collective-permute-done.11.refs_4_ = f32[7,32,128]{2,1,0:T(8,128)S(1)} collective-permute-done((f32[7,32,128]{2,1,0:T(8,128)S(1)}, f32[7,32,128]{2,1,0:T(8,128)S(1)}, u32[]{:S(2)}, u32[]{:S(2)}) %collective-permute-start.11) | collective-permute-done | bytes 114720 | tf_op jit(solution)/shard_map/ppermute | solution.py:521
  52.7 6.8 %shard_map.60 = f32[4,128,128]{2,1,0:T(8,128)S(1)} custom-call(f32[4,128,128]{2,1,0:T(8,128)S(1)} %get-tuple-element.73.refs_0_, f32[128,128]{1,0:T(8,128)S(1)} %collective-permute-done.8.refs_1_, f32[128,128]{1,0:T(8,128)S(1)} %collective-permute-done.9.refs_2_, f32[6,32,128]{2,1,0:T(8,128)S(1)} %collective-permute-done.10.refs_3_, ...), custom_call_target="tpu_custom_call" | custom-call | flops 8000000000 | bytes 7323648 | tf_op jit(solution)/shard_map/pallas_call | solution.py:51
  59.5 0.1 collective-permute-start.12
  59.6 2.4 %collective-permute-start.13 = (f32[4,128,128]{2,1,0:T(8,128)S(1)}, f32[4,128,128]{2,1,0:T(8,128)S(1)}, u32[]{:S(2)}, u32[]{:S(2)}) collective-permute-start(f32[4,128,128]{2,1,0:T(8,128)S(1)} %shard_map.60), channel_id=1, source_target_pairs={{0,1},{1,0},{2,3},{3,2},{4,5},{5,4},{6,7},{7,6},{8,9},{9,8},{10,11... | collective-permute-start | bytes 786440 | tf_op jit(solution)/shard_map/ppermute | solution.py:524
  62.0 2.8 %collective-permute-done.12 = f32[4,128,128]{2,1,0:T(8,128)S(1)} collective-permute-done((f32[4,128,128]{2,1,0:T(8,128)S(1)}, f32[4,128,128]{2,1,0:T(8,128)S(1)}, u32[]{:S(2)}, u32[]{:S(2)}) %collective-permute-start.12) | collective-permute-done | bytes 262176 | tf_op jit(solution)/shard_map/ppermute | solution.py:524
  64.8 3.5 %collective-permute-start.14 = (f32[4,128,128]{2,1,0:T(8,128)S(1)}, f32[4,128,128]{2,1,0:T(8,128)S(1)}, u32[]{:S(2)}, u32[]{:S(2)}) collective-permute-start(f32[4,128,128]{2,1,0:T(8,128)S(1)} %collective-permute-done.12), channel_id=1, source_target_pairs={{0,1},{1,0},{2,3},{3,2},{4,5},{5,4},{6,7},{7,6},{8,9},{9,8},{10,11... | collective-permute-start | bytes 786440 | tf_op jit(solution)/shard_map/ppermute | solution.py:524
  68.4 0.0 collective-permute-done.13
  68.4 1.1 %maximum_select_fusion = f32[1,4,256,256]{3,2,1,0:T(8,128)} fusion(f32[1,4,128,256]{3,2,1,0:T(8,128)S(1)} %maximum_bitcast_fusion, f32[1,4,128,256]{3,2,1,0:T(8,128)S(1)} %fusion, pred[]{:T(512)S(6)} %eq.8), kind=kLoop, calls=%fused_computation | loop fusion | flops 786432 | bytes 2097153 | tf_op jit(solution)/shard_map/jit(_where)/select_n | solution.py:661
  69.5 0.0 collective-permute-done.14
  69.5 0.7 %bitcast_dynamic-update-slice_fusion = f32[1,4,256,256]{3,2,1,0:T(8,128)} fusion(f32[1,4,256,256]{3,2,1,0:T(8,128)} %maximum_select_fusion, s32[]{:T(128)S(6)} %select_n.55, s32[]{:T(128)S(6)} %select_n.56, f32[4,128,128]{2,1,0:T(8,128)S(1)} %collective-permute-done.14), kind=kLoop, calls=%fused_computation.4 | loop fusion | bytes 524296 | tf_op jit(solution)/shard_map/dynamic_update_slice | solution.py:664
  (5 shorter events, 0.1 us)
Async XLA Ops:
  0.0 4.4 %copy-start = (f32[1,4,256,256]{3,2,1,0:T(8,128)S(1)}, f32[1,4,256,256]{3,2,1,0:T(8,128)}, u32[]{:S(2)}) copy-start(f32[1,4,256,256]{3,2,1,0:T(8,128)} %param.4) | copy-start | bytes 3145732
  2.0 8.2 %collective-permute-start = (f32[592,128]{1,0:T(8,128)S(1)}, f32[592,128]{1,0:T(8,128)S(1)}, u32[]{:S(2)}, u32[]{:S(2)}) collective-permute-start(f32[592,128]{1,0:T(8,128)S(1)} %get-tuple-element.43), channel_id=1, source_target_pairs={{0,1},{1,0},{2,3},{3,2},{4,5},{5,4},{6,7},{7,6},{8,9},{9,8},{10,11... | collective-permute-start | bytes 909320 | tf_op jit(solution)/shard_map/ppermute | solution.py:524
  2.7 16.7 %collective-permute-start.1 = (f32[592,128]{1,0:T(8,128)S(1)}, f32[592,128]{1,0:T(8,128)S(1)}, u32[]{:S(2)}, u32[]{:S(2)}) collective-permute-start(f32[592,128]{1,0:T(8,128)S(1)} %get-tuple-element.44), channel_id=1, source_target_pairs={{0,2},{1,3},{2,0},{3,1},{4,6},{5,7},{6,4},{7,5},{8,10},{9,11},{10,... | collective-permute-start | bytes 909320 | tf_op jit(solution)/shard_map/ppermute | solution.py:524
  4.4 15.0 %collective-permute-start.2 = (f32[592,128]{1,0:T(8,128)S(1)}, f32[592,128]{1,0:T(8,128)S(1)}, u32[]{:S(2)}, u32[]{:S(2)}) collective-permute-start(f32[592,128]{1,0:T(8,128)S(1)} %get-tuple-element.45), channel_id=1, source_target_pairs={{0,3},{1,2},{2,1},{3,0},{4,7},{5,6},{6,5},{7,4},{8,11},{9,10},{10,... | collective-permute-start | bytes 909320 | tf_op jit(solution)/shard_map/ppermute | solution.py:524
  4.7 8.7 %collective-permute-start.3 = (f32[160,128]{1,0:T(8,128)S(1)}, f32[160,128]{1,0:T(8,128)S(1)}, u32[]{:S(2)}, u32[]{:S(2)}) collective-permute-start(f32[160,128]{1,0:T(8,128)S(1)} %get-tuple-element.47), channel_id=1, source_target_pairs={{0,1},{1,0},{2,4},{4,2},{3,5},{5,3},{6,8},{8,6},{7,9},{9,7},{10,12... | collective-permute-start | bytes 245768 | tf_op jit(solution)/shard_map/ppermute | solution.py:521
  13.4 5.6 %collective-permute-start.4 = (f32[192,128]{1,0:T(8,128)S(1)}, f32[192,128]{1,0:T(8,128)S(1)}, u32[]{:S(2)}, u32[]{:S(2)}) collective-permute-start(f32[192,128]{1,0:T(8,128)S(1)} %shard_map.49), channel_id=1, source_target_pairs={{0,2},{1,32},{32,1},{2,0},{3,34},{34,3},{4,6},{5,36},{36,5},{6,4},... | collective-permute-start | bytes 294920 | tf_op jit(solution)/shard_map/ppermute | solution.py:521
  19.9 8.4 %collective-permute-start.5 = (f32[256,128]{1,0:T(8,128)S(1)}, f32[256,128]{1,0:T(8,128)S(1)}, u32[]{:S(2)}, u32[]{:S(2)}) collective-permute-start(f32[256,128]{1,0:T(8,128)S(1)} %shard_map.51.refs_9_.refs_2_), channel_id=1, source_target_pairs={{0,1},{1,0},{2,4},{4,2},{3,5},{5,3},{6,8},{8,6},{7,9},{9,7},{10,12... | collective-permute-start | bytes 393224 | tf_op jit(solution)/shard_map/ppermute | solution.py:521
  28.4 6.9 %collective-permute-start.7 = (f32[320,128]{1,0:T(8,128)S(1)}, f32[320,128]{1,0:T(8,128)S(1)}, u32[]{:S(2)}, u32[]{:S(2)}) collective-permute-start(f32[320,128]{1,0:T(8,128)S(1)} %shard_map.53.refs_5_), channel_id=1, source_target_pairs={{0,2},{1,32},{32,1},{2,0},{3,34},{34,3},{4,6},{5,36},{36,5},{6,4},... | collective-permute-start | bytes 491528 | tf_op jit(solution)/shard_map/ppermute | solution.py:521
  31.5 3.1 %collective-permute-start.6 = (f32[320,128]{1,0:T(8,128)S(1)}, f32[320,128]{1,0:T(8,128)S(1)}, u32[]{:S(2)}, u32[]{:S(2)}) collective-permute-start(f32[320,128]{1,0:T(8,128)S(1)} %shard_map.54.refs_17_), channel_id=1, source_target_pairs={{0,1},{1,0},{2,3},{3,2},{4,5},{5,4},{6,7},{7,6},{8,9},{9,8},{10,11... | collective-permute-start | bytes 491528 | tf_op jit(solution)/shard_map/ppermute | solution.py:524
  38.4 6.3 %collective-permute-start.8 = (f32[128,128]{1,0:T(8,128)S(1)}, f32[128,128]{1,0:T(8,128)S(1)}, u32[]{:S(2)}, u32[]{:S(2)}) collective-permute-start(f32[128,128]{1,0:T(8,128)S(1)} %get-tuple-element.74), channel_id=1, source_target_pairs={{0,2},{1,3},{2,0},{3,1},{4,6},{5,7},{6,4},{7,5},{8,10},{9,11},{10,... | collective-permute-start | bytes 196616 | tf_op jit(solution)/shard_map/ppermute | solution.py:524
  38.5 8.3 %collective-permute-start.9 = (f32[128,128]{1,0:T(8,128)S(1)}, f32[128,128]{1,0:T(8,128)S(1)}, u32[]{:S(2)}, u32[]{:S(2)}) collective-permute-start(f32[128,128]{1,0:T(8,128)S(1)} %get-tuple-element.75), channel_id=1, source_target_pairs={{0,1},{1,0},{2,4},{4,2},{3,5},{5,3},{6,8},{8,6},{7,9},{9,7},{10,12... | collective-permute-start | bytes 196616 | tf_op jit(solution)/shard_map/ppermute | solution.py:521
  46.9 5.8 %collective-permute-start.11 = (f32[7,32,128]{2,1,0:T(8,128)S(1)}, f32[7,32,128]{2,1,0:T(8,128)S(1)}, u32[]{:S(2)}, u32[]{:S(2)}) collective-permute-start(f32[7,32,128]{2,1,0:T(8,128)S(1)} %shard_map.58.refs_3_), channel_id=1, source_target_pairs={{0,2},{1,32},{32,1},{2,0},{3,34},{34,3},{4,6},{5,36},{36,5},{6,4},... | collective-permute-start | bytes 344072 | tf_op jit(solution)/shard_map/ppermute | solution.py:521
  49.1 1.6 %collective-permute-start.10 = (f32[6,32,128]{2,1,0:T(8,128)S(1)}, f32[6,32,128]{2,1,0:T(8,128)S(1)}, u32[]{:S(2)}, u32[]{:S(2)}) collective-permute-start(f32[6,32,128]{2,1,0:T(8,128)S(1)} %shard_map.59), channel_id=1, source_target_pairs={{0,1},{1,0},{2,3},{3,2},{4,5},{5,4},{6,7},{7,6},{8,9},{9,8},{10,11... | collective-permute-start | bytes 294920 | tf_op jit(solution)/shard_map/ppermute | solution.py:524
  59.5 5.3 %collective-permute-start.12 = (f32[4,128,128]{2,1,0:T(8,128)S(1)}, f32[4,128,128]{2,1,0:T(8,128)S(1)}, u32[]{:S(2)}, u32[]{:S(2)}) collective-permute-start(f32[4,128,128]{2,1,0:T(8,128)S(1)} %shard_map.60), channel_id=1, source_target_pairs={{0,2},{1,3},{2,0},{3,1},{4,6},{5,7},{6,4},{7,5},{8,10},{9,11},{10,... | collective-permute-start | bytes 786440 | tf_op jit(solution)/shard_map/ppermute | solution.py:524
  59.6 8.8 %collective-permute-start.13 = (f32[4,128,128]{2,1,0:T(8,128)S(1)}, f32[4,128,128]{2,1,0:T(8,128)S(1)}, u32[]{:S(2)}, u32[]{:S(2)}) collective-permute-start(f32[4,128,128]{2,1,0:T(8,128)S(1)} %shard_map.60), channel_id=1, source_target_pairs={{0,1},{1,0},{2,3},{3,2},{4,5},{5,4},{6,7},{7,6},{8,9},{9,8},{10,11... | collective-permute-start | bytes 786440 | tf_op jit(solution)/shard_map/ppermute | solution.py:524
  64.8 4.7 %collective-permute-start.14 = (f32[4,128,128]{2,1,0:T(8,128)S(1)}, f32[4,128,128]{2,1,0:T(8,128)S(1)}, u32[]{:S(2)}, u32[]{:S(2)}) collective-permute-start(f32[4,128,128]{2,1,0:T(8,128)S(1)} %collective-permute-done.12), channel_id=1, source_target_pairs={{0,1},{1,0},{2,3},{3,2},{4,5},{5,4},{6,7},{7,6},{8,9},{9,8},{10,11... | collective-permute-start | bytes 786440 | tf_op jit(solution)/shard_map/ppermute | solution.py:524
